TPU v7x, 32 devices: a whole 2x2x4 slice. The times are simulated.
32 devices in a mesh: row: 16 (over z, y, core), col: 2 (over x).
Axes of the slice: x: 2, y: 2, z: 4, core: 2. Of those that a mesh axis runs over, the one named last changes fastest.
Arguments:
- features: bfloat16 [12, 64, 64, 128], P(None, 'row', 'col'), may hold values from -6 to 6
- cotangent: bfloat16 [12, 32, 32, 128], P(None, 'row', 'col'), may hold values from -0.25 to 0.25
- conv_weight: bfloat16 [1152, 512], P('row', 'col'), may hold values from -0.1875 to 0.1875
- projection_weight: bfloat16 [512, 128], P('row', 'col'), may hold values from -0.25 to 0.25
- down_weight: bfloat16 [512, 128], P('row', 'col'), may hold values from -0.25 to 0.25
- edge_links: int32 [12, 4, 3], replicated, may hold values from 0 to 11, as said below
- corner_links: int32 [12, 4, 3], replicated, may hold values from -1 to 11, as said below
Outputs:
- block_out: bfloat16 [12, 32, 32, 128], P(None, 'row', 'col')
- grad_conv: float32 [1152, 512], P('row', 'col')
- projection_gradient: float32 [512, 128], P('row', 'col')
- grad_down: float32 [512, 128], P('row', 'col')
Inputs may be any that keep to these rules, and one draw needn't show every extreme that they name: edge_links[f, s] = (g, t, r): the halo beyond side s of face f is read from side t of face g, positions reversed when r = 1; pairs are mutual and g differs from f; the links are those of the HEALPix sphere with the faces relabelled and each face turned by a multiple of 90 degrees. corner_links[f, e] = (g, e', w): the diagonal face across corner e of face f, its corner, and a swap flag; g = -1 (and e' = w = 0) at the corners where only three faces meet, which are two corners of every face.
All inputs are finite; a program needn't handle non-finite values.
Results may differ from a plain program's by a relative error of at most 0.0052.
Values may be sent and summed in bfloat16 or wider, within the bound.
No kernel may reach another device: no remote copies, remote signals or barrier semaphores. Data moves between devices by JAX's collectives and lax.ppermute only.
A program may use at most 64 MiB of HBM per device.

v0:
```python
import jax
import jax.numpy as jnp
from jax import lax
from jax.sharding import PartitionSpec as P

DILATION_STEP = 2


def from_root(value, axis, source):
    kept = jnp.where(lax.axis_index(axis) == source, value, 0).astype(value.dtype)
    return lax.psum(kept, axis)


def padded_2(block, sides, width):
    for axis, dim in sides:
        count = lax.axis_size(axis)
        forward = [(i, i + 1) for i in range(count - 1)]
        backward = [(target, source) for source, target in forward]
        low = lax.ppermute(
            lax.slice_in_dim(block, block.shape[dim] - width, None, axis=dim), axis, forward
        )
        high = lax.ppermute(lax.slice_in_dim(block, 0, width, axis=dim), axis, backward)
        block = jnp.concatenate([low, block, high], axis=dim)
    return block


def gelu_value(values):
    return 0.5 * values * (1.0 + jax.scipy.special.erf(values * 0.7071067811865476))


def gelu_slope(values):
    erf_part = 0.5 * (1.0 + jax.scipy.special.erf(values * 0.7071067811865476))
    return erf_part + values * jnp.exp(-0.5 * values * values) * 0.3989422804014327


def side_strips(top_side, right_side, bottom_side, left_side):
    return jnp.stack(
        [
            top_side,
            jnp.swapaxes(right_side, 1, 2)[:, ::-1],
            bottom_side[:, ::-1],
            jnp.swapaxes(left_side, 1, 2),
        ]
    )


def corner_blocks(top_side, bottom_side, channel_depth):
    extent = top_side.shape[2]
    upper_left = top_side[:, :, :channel_depth]
    upper_right = top_side[:, :, extent - channel_depth :][:, :, ::-1]
    lower_right = bottom_side[:, ::-1, extent - channel_depth :][:, :, ::-1]
    bottom_left_corner = bottom_side[:, ::-1, :channel_depth]
    return jnp.stack([upper_left, upper_right, lower_right, bottom_left_corner])


def border_bands(top_side, right_side, bottom_side, left_side, edge_links, corner_links):
    channel_depth = top_side.shape[1]
    strips = side_strips(top_side, right_side, bottom_side, left_side)
    blocks = corner_blocks(top_side, bottom_side, channel_depth)
    picked = strips[edge_links[:, :, 1], edge_links[:, :, 0]]
    flipped = edge_links[:, :, 2][:, :, None, None, None] == 1
    picked = jnp.where(flipped, picked[:, :, :, ::-1], picked)
    present = corner_links[:, :, 0]
    patches = blocks[corner_links[:, :, 1], jnp.maximum(present, 0)]
    swapped = corner_links[:, :, 2][:, :, None, None, None] == 1
    patches = jnp.where(swapped, jnp.swapaxes(patches, 2, 3), patches)
    patches = jnp.where(present[:, :, None, None, None] >= 0, patches, jnp.zeros_like(patches))
    top_band = jnp.concatenate(
        [patches[:, 0, ::-1, ::-1], picked[:, 0, ::-1], patches[:, 1, ::-1, :]], axis=2
    )
    bottom_band = jnp.concatenate([patches[:, 3, :, ::-1], picked[:, 2], patches[:, 2]], axis=2)
    left_band = jnp.swapaxes(picked[:, 3, ::-1], 1, 2)
    right_band = jnp.swapaxes(picked[:, 1], 1, 2)
    return (top_band, bottom_band, left_band, right_band)


def face_pass(totals, items, conv_full, proj_full, down_full):
    padded_face, face_values, face_cotangent = items
    height, breadth, channels = face_values.shape
    channel_depth = (padded_face.shape[0] - height) // 2
    hidden_width = conv_full.shape[1]
    pixels = height * breadth
    windows = []
    pre_act = jnp.zeros((pixels, hidden_width), jnp.float32)
    for row_tap in range(3):
        for col_tap in range(3):
            window = padded_face[
                row_tap * channel_depth : row_tap * channel_depth + height,
                col_tap * channel_depth : col_tap * channel_depth + breadth,
            ]
            window = window.reshape(pixels, channels)
            windows.append(window)
            offset = (3 * row_tap + col_tap) * channels
            pre_act = pre_act + jnp.dot(
                window, conv_full[offset : offset + channels], preferred_element_type=jnp.float32
            )
    hidden = gelu_value(pre_act).astype(jnp.bfloat16)
    resid = (
        face_values.reshape(pixels, channels).astype(jnp.float32)
        + jnp.dot(hidden, proj_full, preferred_element_type=jnp.float32)
    ).astype(jnp.bfloat16)
    grouped = (
        resid.reshape(height // 2, 2, breadth // 2, 2, channels)
        .transpose(0, 2, 1, 3, 4)
        .reshape(pixels // 4, 4 * channels)
    )
    block_out = jnp.dot(grouped, down_full, preferred_element_type=jnp.float32).astype(jnp.bfloat16)
    block_out = block_out.reshape(height // 2, breadth // 2, channels)
    upstream = face_cotangent.reshape(pixels // 4, channels)
    grad_down = jnp.dot(grouped.T, upstream, preferred_element_type=jnp.float32)
    gresid = jnp.dot(upstream, down_full.T, preferred_element_type=jnp.float32).astype(jnp.bfloat16)
    gresid = (
        gresid.reshape(height // 2, breadth // 2, 2, 2, channels)
        .transpose(0, 2, 1, 3, 4)
        .reshape(pixels, channels)
    )
    projection_gradient = jnp.dot(hidden.T, gresid, preferred_element_type=jnp.float32)
    gpre = (
        jnp.dot(gresid, proj_full.T, preferred_element_type=jnp.float32) * gelu_slope(pre_act)
    ).astype(jnp.bfloat16)
    grad_conv = jnp.concatenate(
        [jnp.dot(window.T, gpre, preferred_element_type=jnp.float32) for window in windows], axis=0
    )
    totals = (totals[0] + grad_conv, totals[1] + projection_gradient, totals[2] + grad_down)
    return (totals, block_out)


def on_device(
    features, cotangent, conv_weight, projection_weight, down_weight, edge_links, corner_links
):
    height = features.shape[1]
    breadth = features.shape[2]
    channel_depth = DILATION_STEP
    row_count = lax.axis_size("row")
    col_count = lax.axis_size("col")
    row_location = lax.axis_index("row")
    col_place = lax.axis_index("col")
    conv_full, proj_full, down_full = (
        lax.all_gather(conv_weight, "row", axis=0, tiled=True),
        lax.all_gather(projection_weight, "row", axis=0, tiled=True),
        lax.all_gather(down_weight, "row", axis=0, tiled=True),
    )
    conv_full, proj_full, down_full = (
        lax.all_gather(conv_full, "col", axis=1, tiled=True),
        lax.all_gather(proj_full, "col", axis=1, tiled=True),
        lax.all_gather(down_full, "col", axis=1, tiled=True),
    )
    top_rim = features[:, :channel_depth]
    bottom_rim = features[:, height - channel_depth :]
    left_rim = features[:, :, :channel_depth]
    right_rim = features[:, :, breadth - channel_depth :]
    left_column, rightmost_column = (
        lax.all_gather(left_rim, "row", axis=1, tiled=True),
        lax.all_gather(right_rim, "row", axis=1, tiled=True),
    )
    top_line, bottom_line = (
        lax.all_gather(top_rim, "col", axis=2, tiled=True),
        lax.all_gather(bottom_rim, "col", axis=2, tiled=True),
    )
    left_side = from_root(left_column, "col", 0)
    right_side = from_root(rightmost_column, "col", col_count - 1)
    top_side = from_root(top_line, "row", 0)
    bottom_side = from_root(bottom_line, "row", row_count - 1)
    top_band, bottom_band, left_band, right_band = border_bands(
        top_side, right_side, bottom_side, left_side, edge_links, corner_links
    )
    padded = padded_2(features, (("row", 1), ("col", 2)), channel_depth)
    edge_zeros = jnp.zeros(
        (features.shape[0], channel_depth, channel_depth, features.shape[3]), jnp.bfloat16
    )
    left_long = jnp.concatenate([edge_zeros, left_band, edge_zeros], axis=1)
    right_long = jnp.concatenate([edge_zeros, right_band, edge_zeros], axis=1)
    left_piece = lax.dynamic_slice_in_dim(
        left_long, row_location * height, height + 2 * channel_depth, 1
    )
    right_piece = lax.dynamic_slice_in_dim(
        right_long, row_location * height, height + 2 * channel_depth, 1
    )
    top_piece = lax.dynamic_slice_in_dim(
        top_band, col_place * breadth, breadth + 2 * channel_depth, 2
    )
    bottom_piece = lax.dynamic_slice_in_dim(
        bottom_band, col_place * breadth, breadth + 2 * channel_depth, 2
    )
    padded = padded.at[:, :, :channel_depth].set(
        jnp.where(col_place == 0, left_piece, padded[:, :, :channel_depth])
    )
    padded = padded.at[:, :, breadth + channel_depth :].set(
        jnp.where(col_place == col_count - 1, right_piece, padded[:, :, breadth + channel_depth :])
    )
    padded = padded.at[:, :channel_depth].set(
        jnp.where(row_location == 0, top_piece, padded[:, :channel_depth])
    )
    padded = padded.at[:, height + channel_depth :].set(
        jnp.where(row_location == row_count - 1, bottom_piece, padded[:, height + channel_depth :])
    )
    start = (
        jnp.zeros(conv_full.shape, jnp.float32),
        jnp.zeros(proj_full.shape, jnp.float32),
        jnp.zeros(down_full.shape, jnp.float32),
    )

    def one_face(totals, items):
        return face_pass(totals, items, conv_full, proj_full, down_full)

    totals, block_out = lax.scan(one_face, start, (padded, features, cotangent))
    partial_value = (
        lax.psum_scatter(totals[0], "row", scatter_dimension=0, tiled=True),
        lax.psum_scatter(totals[1], "row", scatter_dimension=0, tiled=True),
        lax.psum_scatter(totals[2], "row", scatter_dimension=0, tiled=True),
    )
    grad_conv, projection_gradient, grad_down = (
        lax.psum_scatter(partial_value[0], "col", scatter_dimension=1, tiled=True),
        lax.psum_scatter(partial_value[1], "col", scatter_dimension=1, tiled=True),
        lax.psum_scatter(partial_value[2], "col", scatter_dimension=1, tiled=True),
    )
    return (block_out, grad_conv, projection_gradient, grad_down)


def solution(mesh):
    return jax.shard_map(
        on_device,
        mesh=mesh,
        in_specs=(
            P(None, "row", "col", None),
            P(None, "row", "col", None),
            P("row", "col"),
            P("row", "col"),
            P("row", "col"),
            P(),
            P(),
        ),
        out_specs=(P(None, "row", "col", None), P("row", "col"), P("row", "col"), P("row", "col")),
        check_vma=False,
    )
```

profile of v0, /device:TPU:0, one launch (start us, length us, event | category | flops | bytes accessed | tf_op | source)
XLA Modules:
  0.0 632.7 jit_solution(11221950437851858596)
XLA Ops:
  8.6 8.5 %all_gather.32 = bf16[12,2,64,128]{3,1,0,2:T(2,128)(2,1)S(1)} all-gather(bf16[12,2,32,128]{3,1,0,2:T(2,128)(2,1)S(1)} %copy.77), channel_id=1, replica_groups=mesh['row'=16,'col'=2] {'col'}, dimensions={2}, use_global_device_ids=true | all-gather | bytes 589824 | tf_op jit(solution)/shard_map/all_gather | solution.py:158
  17.1 6.7 %all_gather.30 = bf16[12,2,64,128]{3,1,0,2:T(2,128)(2,1)S(1)} all-gather(bf16[12,2,32,128]{3,1,0,2:T(2,128)(2,1)S(1)} %copy.78), channel_id=1, replica_groups=mesh['row'=16,'col'=2] {'col'}, dimensions={2}, use_global_device_ids=true | all-gather | bytes 589824 | tf_op jit(solution)/shard_map/all_gather | solution.py:157
  27.2 23.1 %all_gather.31 = bf16[12,64,2,128]{3,2,0,1:T(2,128)(2,1)S(1)} all-gather(bf16[12,4,2,128]{3,2,0,1:T(2,128)(2,1)S(1)} %copy.79), channel_id=1, replica_groups=mesh['row'=16,'col'=2] {'row'}, dimensions={1}, use_global_device_ids=true | all-gather | bytes 417792 | tf_op jit(solution)/shard_map/all_gather | solution.py:154
  50.6 3.1 rev.34
  53.7 18.6 %all_gather.33 = bf16[12,64,2,128]{3,2,0,1:T(2,128)(2,1)S(1)} all-gather(bf16[12,4,2,128]{3,2,0,1:T(2,128)(2,1)S(1)} %copy.80), channel_id=1, replica_groups=mesh['row'=16,'col'=2] {'row'}, dimensions={1}, use_global_device_ids=true | all-gather | bytes 417792 | tf_op jit(solution)/shard_map/all_gather | solution.py:153
  73.4 2.9 collective-permute-start
  77.6 23.4 %all_gather.38 = bf16[1152,256]{1,0:T(8,128)(2,1)} all-gather(bf16[72,256]{1,0:T(8,128)(2,1)S(1)} %copy-done.24), channel_id=1, replica_groups=mesh['row'=16,'col'=2] {'row'}, dimensions={0}, use_global_device_ids=true | all-gather | bytes 626688 | tf_op jit(solution)/shard_map/all_gather | solution.py:139
  102.0 17.9 %all_gather.36 = bf16[512,64]{1,0:T(8,128)(2,1)S(1)} all-gather(bf16[32,64]{1,0:T(8,128)(2,1)S(1)} %copy-done.26), channel_id=1, replica_groups=mesh['row'=16,'col'=2] {'row'}, dimensions={0}, use_global_device_ids=true | all-gather | bytes 69632 | tf_op jit(solution)/shard_map/all_gather | solution.py:140
  120.0 5.0 all_gather.37
  128.6 3.2 collective-permute-start.2
  133.2 19.3 %all_gather.34 = bf16[512,64]{1,0:T(8,128)(2,1)S(1)} all-gather(bf16[32,64]{1,0:T(8,128)(2,1)S(1)} %copy-done.27), channel_id=1, replica_groups=mesh['row'=16,'col'=2] {'row'}, dimensions={0}, use_global_device_ids=true | all-gather | bytes 69632 | tf_op jit(solution)/shard_map/all_gather | solution.py:141
  152.5 6.5 %all_gather.35 = bf16[512,128]{0,1:T(8,128)(2,1)S(1)} all-gather(bf16[512,64]{0,1:T(8,128)(2,1)S(1)} %copy.69), channel_id=1, replica_groups=mesh['row'=16,'col'=2] {'col'}, dimensions={1}, use_global_device_ids=true | all-gather | bytes 196608 | tf_op jit(solution)/shard_map/all_gather | solution.py:146
  159.8 1.5 pad_maximum_fusion.1
  161.3 3.6 rev.35
  169.7 5.0 pad_maximum_fusion
  174.7 9.5 %gather_fusion = bf16[48,2,64,128]{3,1,2,0:T(2,128)(2,1)} fusion(bf16[4,12,2,64,128]{4,2,1,3,0:T(2,128)(2,1)} %pad_maximum_fusion, s32[48]{0:T(128)S(1)} %reshape.222), kind=kCustom, calls=%fused_computation | custom fusion | bytes 3146112 | tf_op jit(solution)/shard_map/gather | solution.py:60
  184.3 2.7 copy.62
  187.0 2.9 broadcast_select_fusion
  189.9 2.3 slice_bitcast_fusion
  192.2 4.3 rev.42
  196.5 5.0 rev.37
  202.8 1.4 fusion.23
  204.2 1.6 fusion.26
  205.8 1.7 fusion.27
  207.5 1.7 fusion.19
  209.2 1.7 fusion.18
  211.0 200.4 %while.21 = (s32[]{:T(128)}, f32[1152,512]{1,0:T(8,128)S(1)}, f32[512,128]{1,0:T(8,128)}, f32[512,128]{1,0:T(8,128)}, bf16[12,2,16,128]{3,2,1,0:T(8,128)(2,1)}, ...) while((s32[]{:T(128)}, f32[1152,512]{1,0:T(8,128)S(1)}, ...), condition=%wide.region_5.6_spmd.clone, body=%wide.region_4.5_spmd.clone.sunk | while | flops 367923200 | bytes 30253824 | solution.py:206
  238.6 1.9 convolution_add_fusion.27
  255.4 1.9 convolution_add_fusion.27
  272.2 1.9 convolution_add_fusion.27
  288.9 1.9 convolution_add_fusion.27
  305.7 1.9 convolution_add_fusion.27
  322.5 1.9 convolution_add_fusion.27
  339.3 1.9 convolution_add_fusion.27
  356.1 1.9 convolution_add_fusion.27
  372.9 1.9 convolution_add_fusion.27
  389.6 1.9 convolution_add_fusion.27
  406.4 1.9 convolution_add_fusion.27
  412.9 52.4 %reduce-scatter.17.cloned.1.call-done = f32[32,128]{1,0:T(8,128)} async-done(((f32[512,128]{1,0:T(8,128)}), f32[32,128]{1,0:T(8,128)}) %reduce-scatter.17.cloned.1.call-update) | async-done | bytes 16400 | tf_op jit(solution)/shard_map/reduce_scatter | solution.py:210
  465.3 1.4 copy.75
  466.8 56.7 %reduce-scatter.15.cloned.1.call-done = f32[32,128]{1,0:T(8,128)} async-done(((f32[512,128]{1,0:T(8,128)}), f32[32,128]{1,0:T(8,128)}) %reduce-scatter.15.cloned.1.call-update) | async-done | bytes 16400 | tf_op jit(solution)/shard_map/reduce_scatter | solution.py:209
  523.4 1.5 copy.73
  525.0 64.4 %reduce-scatter.11.cloned.1.call-done = f32[72,512]{1,0:T(8,128)} async-done(((f32[1152,512]{1,0:T(8,128)}), f32[72,512]{1,0:T(8,128)}) %reduce-scatter.11.cloned.1.call-update) | async-done | bytes 147472 | tf_op jit(solution)/shard_map/reduce_scatter | solution.py:208
  589.4 11.2 %reduce-scatter.21.cloned.1.call-done = f32[64,32]{1,0:T(8,128)} async-done(((f32[128,32]{1,0:T(8,128)}), f32[64,32]{1,0:T(8,128)}) %reduce-scatter.21.cloned.1.call-update) | async-done | bytes 8208
  600.6 1.4 copy.76
  602.0 10.8 %reduce-scatter.19.cloned.1.call-done = f32[64,32]{1,0:T(8,128)} async-done(((f32[128,32]{1,0:T(8,128)}), f32[64,32]{1,0:T(8,128)}) %reduce-scatter.19.cloned.1.call-update) | async-done | bytes 8208
  612.8 1.4 copy.74
  614.3 11.9 %reduce-scatter.13.cloned.1.call-done = f32[72,256]{1,0:T(8,128)} async-done(((f32[72,512]{1,0:T(8,128)}), f32[72,256]{1,0:T(8,128)}) %reduce-scatter.13.cloned.1.call-update) | async-done | bytes 73744 | tf_op jit(solution)/shard_map/reduce_scatter | solution.py:213
  (998 shorter events, 195.0 us)
Async XLA Ops:
  7.2 154.1 %all-reduce.5.cloned.1.call-start = ((), (), s32[]{:S(2)}) async-start(), calls=%async_computation.13 | async-start | bytes 1572864 | tf_op jit(solution)/shard_map/psum | solution.py:11
  26.0 143.6 %all-reduce.7.cloned.1.call-start = ((), (), s32[]{:S(2)}) async-start(), calls=%async_computation.14 | async-start | bytes 1572864 | tf_op jit(solution)/shard_map/psum | solution.py:11
  27.1 50.5 %copy-start.24 = (bf16[72,256]{1,0:T(8,128)(2,1)S(1)}, bf16[72,256]{1,0:T(8,128)(2,1)}, u32[]{:S(2)}) copy-start(bf16[72,256]{1,0:T(8,128)(2,1)} %param.19) | copy-start | bytes 110596
  50.5 50.6 %copy-start.25 = (s32[12,4,3]{0,1,2:T(4,128)S(1)}, s32[12,4,3]{0,1,2:T(4,128)}, u32[]{:S(2)}) copy-start(s32[12,4,3]{0,1,2:T(4,128)} %param.23) | copy-start | bytes 1732
  50.6 51.1 %copy-start.28 = (s32[12,4,3]{0,1,2:T(4,128)S(1)}, s32[12,4,3]{0,1,2:T(4,128)}, u32[]{:S(2)}) copy-start(s32[12,4,3]{0,1,2:T(4,128)} %param.22) | copy-start | bytes 1732
  50.6 51.5 %copy-start.26 = (bf16[32,64]{1,0:T(8,128)(2,1)S(1)}, bf16[32,64]{1,0:T(8,128)(2,1)}, u32[]{:S(2)}) copy-start(bf16[32,64]{1,0:T(8,128)(2,1)} %param.20) | copy-start | bytes 12292
  73.4 59.8 %copy-start.27 = (bf16[32,64]{1,0:T(8,128)(2,1)S(1)}, bf16[32,64]{1,0:T(8,128)(2,1)}, u32[]{:S(2)}) copy-start(bf16[32,64]{1,0:T(8,128)(2,1)} %param.21) | copy-start | bytes 12292
  73.4 137.6 %all-gather.2.cloned.1.call-start = ((), (), s32[]{:S(2)}) async-start(), calls=%async_computation.6 | async-start | bytes 1769472 | tf_op jit(solution)/shard_map/all_gather | solution.py:144
  73.4 53.0 %collective-permute-start = (bf16[12,2,32,128]{3,1,0,2:T(2,128)(2,1)S(1)}, bf16[12,2,32,128]{3,1,0,2:T(2,128)(2,1)}, u32[]{:S(2)}, u32[]{:S(2)}) collective-permute-start(bf16[12,2,32,128]{3,1,0,2:T(2,128)(2,1)S(1)} %copy.77), channel_id=1, source_target_pairs={{0,2},{2,4},{4,6},{6,8},{8,10},{10,12},{12,14},{14,16},{16,18},{18... | collective-permute-start | bytes 589832 | tf_op jit(solution)/shard_map/ppermute | solution.py:19
  76.3 52.1 %collective-permute-start.1 = (bf16[12,2,32,128]{3,1,0,2:T(2,128)(2,1)S(1)}, bf16[12,2,32,128]{3,1,0,2:T(2,128)(2,1)S(1)}, u32[]{:S(2)}, u32[]{:S(2)}) collective-permute-start(bf16[12,2,32,128]{3,1,0,2:T(2,128)(2,1)S(1)} %copy.78), channel_id=1, source_target_pairs={{2,0},{4,2},{6,4},{8,6},{10,8},{12,10},{14,12},{16,14},{18,16},{20... | collective-permute-start | bytes 589832 | tf_op jit(solution)/shard_map/ppermute | solution.py:22
  101.0 364.2 %reduce-scatter.17.cloned.1.call-start = ((), (), s32[]{:S(2)}) async-start(), calls=%async_computation.10 | async-start | bytes 278528 | tf_op jit(solution)/shard_map/reduce_scatter | solution.py:210
  128.6 31.2 %collective-permute-start.2 = (bf16[12,8,2,128]{3,2,1,0:T(2,128)(2,1)S(1)}, bf16[12,8,2,128]{3,2,1,0:T(2,128)(2,1)S(1)}, u32[]{:S(2)}, u32[]{:S(2)}) collective-permute-start(bf16[12,8,2,128]{3,2,1,0:T(2,128)(2,1)S(1)} %get-tuple-element.217), channel_id=1, source_target_pairs={{0,1},{2,3},{4,5},{6,7},{8,9},{10,11},{12,13},{14,15},{16,17},{18,... | collective-permute-start | bytes 147464 | tf_op jit(solution)/shard_map/ppermute | solution.py:19
  131.9 28.0 %collective-permute-start.3 = (bf16[12,8,2,128]{3,2,1,0:T(2,128)(2,1)S(1)}, bf16[12,8,2,128]{3,2,1,0:T(2,128)(2,1)S(1)}, u32[]{:S(2)}, u32[]{:S(2)}) collective-permute-start(bf16[12,8,2,128]{3,2,1,0:T(2,128)(2,1)S(1)} %get-tuple-element.218), channel_id=1, source_target_pairs={{1,0},{3,2},{5,4},{7,6},{9,8},{11,10},{13,12},{15,14},{17,16},{19,... | collective-permute-start | bytes 147464 | tf_op jit(solution)/shard_map/ppermute | solution.py:22
  159.8 14.9 %copy-start.23 = (bf16[12,8,2,128]{3,2,1,0:T(2,128)(2,1)}, bf16[12,8,2,128]{3,2,1,0:T(2,128)(2,1)S(1)}, u32[]{:S(2)}) copy-start(bf16[12,8,2,128]{3,2,1,0:T(2,128)(2,1)S(1)} %collective-permute-done.2) | copy-start | bytes 147460
  232.5 7.9 %copy-start.2 = (f32[512,128]{1,0:T(8,128)S(1)}, f32[512,128]{1,0:T(8,128)}, u32[]{:S(2)}) copy-start(f32[512,128]{1,0:T(8,128)} %get-tuple-element.346) | copy-start | bytes 786436 | tf_op jit(solution)/shard_map/while
  232.5 8.2 %copy-start.7 = (bf16[4,32,128]{2,1,0:T(8,128)(2,1)S(1)}, bf16[4,32,128]{2,1,0:T(8,128)(2,1)}, u32[]{:S(2)}) copy-start(bf16[4,32,128]{2,1,0:T(8,128)(2,1)} %copy-done.6) | copy-start | bytes 98308 | tf_op jit(solution)/shard_map/while
  233.7 7.5 %copy-start.19 = (bf16[4,32,128]{2,1,0:T(8,128)(2,1)S(1)}, bf16[4,32,128]{2,1,0:T(8,128)(2,1)}, u32[]{:S(2)}) copy-start(bf16[4,32,128]{2,1,0:T(8,128)(2,1)} %copy-done.18) | copy-start | bytes 98308 | tf_op jit(solution)/shard_map/while
  249.3 7.9 %copy-start.2 = (f32[512,128]{1,0:T(8,128)S(1)}, f32[512,128]{1,0:T(8,128)}, u32[]{:S(2)}) copy-start(f32[512,128]{1,0:T(8,128)} %get-tuple-element.346) | copy-start | bytes 786436 | tf_op jit(solution)/shard_map/while
  249.3 8.2 %copy-start.7 = (bf16[4,32,128]{2,1,0:T(8,128)(2,1)S(1)}, bf16[4,32,128]{2,1,0:T(8,128)(2,1)}, u32[]{:S(2)}) copy-start(bf16[4,32,128]{2,1,0:T(8,128)(2,1)} %copy-done.6) | copy-start | bytes 98308 | tf_op jit(solution)/shard_map/while
  250.5 7.5 %copy-start.19 = (bf16[4,32,128]{2,1,0:T(8,128)(2,1)S(1)}, bf16[4,32,128]{2,1,0:T(8,128)(2,1)}, u32[]{:S(2)}) copy-start(bf16[4,32,128]{2,1,0:T(8,128)(2,1)} %copy-done.18) | copy-start | bytes 98308 | tf_op jit(solution)/shard_map/while
  266.1 7.9 %copy-start.2 = (f32[512,128]{1,0:T(8,128)S(1)}, f32[512,128]{1,0:T(8,128)}, u32[]{:S(2)}) copy-start(f32[512,128]{1,0:T(8,128)} %get-tuple-element.346) | copy-start | bytes 786436 | tf_op jit(solution)/shard_map/while
  266.1 8.2 %copy-start.7 = (bf16[4,32,128]{2,1,0:T(8,128)(2,1)S(1)}, bf16[4,32,128]{2,1,0:T(8,128)(2,1)}, u32[]{:S(2)}) copy-start(bf16[4,32,128]{2,1,0:T(8,128)(2,1)} %copy-done.6) | copy-start | bytes 98308 | tf_op jit(solution)/shard_map/while
  282.9 7.9 %copy-start.2 = (f32[512,128]{1,0:T(8,128)S(1)}, f32[512,128]{1,0:T(8,128)}, u32[]{:S(2)}) copy-start(f32[512,128]{1,0:T(8,128)} %get-tuple-element.346) | copy-start | bytes 786436 | tf_op jit(solution)/shard_map/while
  282.9 8.2 %copy-start.7 = (bf16[4,32,128]{2,1,0:T(8,128)(2,1)S(1)}, bf16[4,32,128]{2,1,0:T(8,128)(2,1)}, u32[]{:S(2)}) copy-start(bf16[4,32,128]{2,1,0:T(8,128)(2,1)} %copy-done.6) | copy-start | bytes 98308 | tf_op jit(solution)/shard_map/while
  299.7 7.9 %copy-start.2 = (f32[512,128]{1,0:T(8,128)S(1)}, f32[512,128]{1,0:T(8,128)}, u32[]{:S(2)}) copy-start(f32[512,128]{1,0:T(8,128)} %get-tuple-element.346) | copy-start | bytes 786436 | tf_op jit(solution)/shard_map/while
  299.7 8.2 %copy-start.7 = (bf16[4,32,128]{2,1,0:T(8,128)(2,1)S(1)}, bf16[4,32,128]{2,1,0:T(8,128)(2,1)}, u32[]{:S(2)}) copy-start(bf16[4,32,128]{2,1,0:T(8,128)(2,1)} %copy-done.6) | copy-start | bytes 98308 | tf_op jit(solution)/shard_map/while
  300.9 7.5 %copy-start.19 = (bf16[4,32,128]{2,1,0:T(8,128)(2,1)S(1)}, bf16[4,32,128]{2,1,0:T(8,128)(2,1)}, u32[]{:S(2)}) copy-start(bf16[4,32,128]{2,1,0:T(8,128)(2,1)} %copy-done.18) | copy-start | bytes 98308 | tf_op jit(solution)/shard_map/while
  316.4 7.9 %copy-start.2 = (f32[512,128]{1,0:T(8,128)S(1)}, f32[512,128]{1,0:T(8,128)}, u32[]{:S(2)}) copy-start(f32[512,128]{1,0:T(8,128)} %get-tuple-element.346) | copy-start | bytes 786436 | tf_op jit(solution)/shard_map/while
  316.5 8.2 %copy-start.7 = (bf16[4,32,128]{2,1,0:T(8,128)(2,1)S(1)}, bf16[4,32,128]{2,1,0:T(8,128)(2,1)}, u32[]{:S(2)}) copy-start(bf16[4,32,128]{2,1,0:T(8,128)(2,1)} %copy-done.6) | copy-start | bytes 98308 | tf_op jit(solution)/shard_map/while
  317.6 7.5 %copy-start.19 = (bf16[4,32,128]{2,1,0:T(8,128)(2,1)S(1)}, bf16[4,32,128]{2,1,0:T(8,128)(2,1)}, u32[]{:S(2)}) copy-start(bf16[4,32,128]{2,1,0:T(8,128)(2,1)} %copy-done.18) | copy-start | bytes 98308 | tf_op jit(solution)/shard_map/while
  333.2 7.9 %copy-start.2 = (f32[512,128]{1,0:T(8,128)S(1)}, f32[512,128]{1,0:T(8,128)}, u32[]{:S(2)}) copy-start(f32[512,128]{1,0:T(8,128)} %get-tuple-element.346) | copy-start | bytes 786436 | tf_op jit(solution)/shard_map/while
  333.2 8.2 %copy-start.7 = (bf16[4,32,128]{2,1,0:T(8,128)(2,1)S(1)}, bf16[4,32,128]{2,1,0:T(8,128)(2,1)}, u32[]{:S(2)}) copy-start(bf16[4,32,128]{2,1,0:T(8,128)(2,1)} %copy-done.6) | copy-start | bytes 98308 | tf_op jit(solution)/shard_map/while
  334.4 7.5 %copy-start.19 = (bf16[4,32,128]{2,1,0:T(8,128)(2,1)S(1)}, bf16[4,32,128]{2,1,0:T(8,128)(2,1)}, u32[]{:S(2)}) copy-start(bf16[4,32,128]{2,1,0:T(8,128)(2,1)} %copy-done.18) | copy-start | bytes 98308 | tf_op jit(solution)/shard_map/while
  350.0 7.9 %copy-start.2 = (f32[512,128]{1,0:T(8,128)S(1)}, f32[512,128]{1,0:T(8,128)}, u32[]{:S(2)}) copy-start(f32[512,128]{1,0:T(8,128)} %get-tuple-element.346) | copy-start | bytes 786436 | tf_op jit(solution)/shard_map/while
  350.0 8.2 %copy-start.7 = (bf16[4,32,128]{2,1,0:T(8,128)(2,1)S(1)}, bf16[4,32,128]{2,1,0:T(8,128)(2,1)}, u32[]{:S(2)}) copy-start(bf16[4,32,128]{2,1,0:T(8,128)(2,1)} %copy-done.6) | copy-start | bytes 98308 | tf_op jit(solution)/shard_map/while
  351.2 7.5 %copy-start.19 = (bf16[4,32,128]{2,1,0:T(8,128)(2,1)S(1)}, bf16[4,32,128]{2,1,0:T(8,128)(2,1)}, u32[]{:S(2)}) copy-start(bf16[4,32,128]{2,1,0:T(8,128)(2,1)} %copy-done.18) | copy-start | bytes 98308 | tf_op jit(solution)/shard_map/while
  366.8 7.9 %copy-start.2 = (f32[512,128]{1,0:T(8,128)S(1)}, f32[512,128]{1,0:T(8,128)}, u32[]{:S(2)}) copy-start(f32[512,128]{1,0:T(8,128)} %get-tuple-element.346) | copy-start | bytes 786436 | tf_op jit(solution)/shard_map/while
  366.8 8.2 %copy-start.7 = (bf16[4,32,128]{2,1,0:T(8,128)(2,1)S(1)}, bf16[4,32,128]{2,1,0:T(8,128)(2,1)}, u32[]{:S(2)}) copy-start(bf16[4,32,128]{2,1,0:T(8,128)(2,1)} %copy-done.6) | copy-start | bytes 98308 | tf_op jit(solution)/shard_map/while
  368.0 7.5 %copy-start.19 = (bf16[4,32,128]{2,1,0:T(8,128)(2,1)S(1)}, bf16[4,32,128]{2,1,0:T(8,128)(2,1)}, u32[]{:S(2)}) copy-start(bf16[4,32,128]{2,1,0:T(8,128)(2,1)} %copy-done.18) | copy-start | bytes 98308 | tf_op jit(solution)/shard_map/while
  383.6 7.9 %copy-start.2 = (f32[512,128]{1,0:T(8,128)S(1)}, f32[512,128]{1,0:T(8,128)}, u32[]{:S(2)}) copy-start(f32[512,128]{1,0:T(8,128)} %get-tuple-element.346) | copy-start | bytes 786436 | tf_op jit(solution)/shard_map/while
  383.6 8.2 %copy-start.7 = (bf16[4,32,128]{2,1,0:T(8,128)(2,1)S(1)}, bf16[4,32,128]{2,1,0:T(8,128)(2,1)}, u32[]{:S(2)}) copy-start(bf16[4,32,128]{2,1,0:T(8,128)(2,1)} %copy-done.6) | copy-start | bytes 98308 | tf_op jit(solution)/shard_map/while
  400.4 7.9 %copy-start.2 = (f32[512,128]{1,0:T(8,128)S(1)}, f32[512,128]{1,0:T(8,128)}, u32[]{:S(2)}) copy-start(f32[512,128]{1,0:T(8,128)} %get-tuple-element.346) | copy-start | bytes 786436 | tf_op jit(solution)/shard_map/while
  400.4 8.2 %copy-start.7 = (bf16[4,32,128]{2,1,0:T(8,128)(2,1)S(1)}, bf16[4,32,128]{2,1,0:T(8,128)(2,1)}, u32[]{:S(2)}) copy-start(bf16[4,32,128]{2,1,0:T(8,128)(2,1)} %copy-done.6) | copy-start | bytes 98308 | tf_op jit(solution)/shard_map/while
  411.4 112.0 %reduce-scatter.15.cloned.1.call-start = ((), (), s32[]{:S(2)}) async-start(), calls=%async_computation.9 | async-start | bytes 278528 | tf_op jit(solution)/shard_map/reduce_scatter | solution.py:209
  412.0 177.3 %reduce-scatter.11.cloned.1.call-start = ((), (), s32[]{:S(2)}) async-start(), calls=%async_computation.7 | async-start | bytes 2506752 | tf_op jit(solution)/shard_map/reduce_scatter | solution.py:208
  412.8 187.7 %reduce-scatter.21.cloned.1.call-start = ((), (), s32[]{:S(2)}) async-start(), calls=%async_computation.12 | async-start | bytes 98304
  466.7 146.1 %reduce-scatter.19.cloned.1.call-start = ((), (), s32[]{:S(2)}) async-start(), calls=%async_computation.11 | async-start | bytes 98304
  524.9 101.2 %reduce-scatter.13.cloned.1.call-start = ((), (), s32[]{:S(2)}) async-start(), calls=%async_computation.8 | async-start | bytes 221184 | tf_op jit(solution)/shard_map/reduce_scatter | solution.py:213
  (237 other events, 916.3 us)
Sparse Core Ops, SparseCore 0:
  26.2 94.8 all-reduce.4
  123.4 35.0 all-reduce.6
  160.0 23.5 all-gather.1
  411.5 53.6 reduce-scatter.16
  468.6 54.7 reduce-scatter.14
  527.1 62.2 reduce-scatter.10
  591.5 8.9 reduce-scatter.20
  602.7 10.0 reduce-scatter.18
  615.6 10.4 reduce-scatter.12
where the time goes:
time: 637 us; the launch traced here: 633 us
  waiting for transfers between devices  208 us (33%)
  matrix products  138 us (22%)
  blocking collectives  129 us (20%)
  local copies, waits for them, and re-layouts  93.2 us (15%)
  other arithmetic  34.3 us (5%)
  between operations  14.2 us (2%)
  starting transfers between devices  9.09 us (1%)
  loops' own time  6.47 us (1%)
    reduce_scatter x1, waiting for transfers between devices, on_device(): lax.psum_scatter(totals[0], 'row', scatter_dimension=0, tiled=True)  64.4 us
    reduce_scatter x1, waiting for transfers between devices, on_device(): lax.psum_scatter(totals[1], 'row', scatter_dimension=0, tiled=True)  56.7 us
    reduce_scatter x1, waiting for transfers between devices, on_device(): lax.psum_scatter(totals[2], 'row', scatter_dimension=0, tiled=True)  52.4 us
    dot_general x108, matrix products, face_pass(): jnp.dot(window, conv_full[offset:offset + channels], preferred_element_ty...  51.6 us
    all_gather x1, blocking collectives, on_device(): lax.all_gather(conv_weight, 'row', axis=0, tiled=True)  23.4 us
    all_gather x1, blocking collectives, on_device(): lax.all_gather(right_rim, 'row', axis=1, tiled=True)  23.1 us
    unnamed x11, waiting for transfers between devices  22.7 us
    dot_general x108, matrix products, face_pass(): jnp.dot(window.T, gpre, preferred_element_type=jnp.float32)  22 us
  transfers between devices with their start and end apart: 13, of which 6 were waited for; matrix products, arithmetic and copies ran while one was open for 11% of the time, Pallas kernels for 0%

commit v1 on v0

v1 whole, which is shorter than its diff:
```python
import functools

import jax
import jax.numpy as jnp
from jax import lax
from jax.experimental import pallas as pl
from jax.experimental.pallas import tpu as pltpu
from jax.sharding import PartitionSpec as P

DEPTH = 2
BF = jnp.bfloat16
F32 = jnp.float32


def swap(value, axis, bit):
    count = lax.axis_size(axis)
    return lax.ppermute(value, axis, [(i, i ^ bit) for i in range(count)])


def gather_pair(value, axis, dim):
    if lax.axis_size(axis) != 2:
        return lax.all_gather(value, axis, axis=dim, tiled=True)
    other = swap(value, axis, 1)
    first = lax.axis_index(axis) == 0
    low = jnp.where(first, value, other)
    high = jnp.where(first, other, value)
    return jnp.concatenate([low, high], axis=dim)


def scatter_sum_pair(value, axis, dim):
    count = lax.axis_size(axis)
    if count != 2:
        return lax.psum_scatter(value, axis, scatter_dimension=dim, tiled=True)
    low, high = jnp.split(value, 2, axis=dim)
    first = lax.axis_index(axis) == 0
    return jnp.where(first, low, high) + swap(jnp.where(first, high, low), axis, 1)


def pack_cols(value):
    width = value.shape[-1]
    if width % 128 == 0:
        return jnp.concatenate(
            [value[..., j : j + 128] for j in range(0, width, 128)], axis=-2
        )
    return value.reshape(value.shape[:-2] + (-1, 128))


def unpack_cols(value, width):
    if width % 128 == 0:
        parts = width // 128
        rows = value.shape[-2] // parts
        return jnp.concatenate(
            [value[..., j * rows : (j + 1) * rows, :] for j in range(parts)], axis=-1
        )
    return value.reshape(value.shape[:-2] + (-1, width))


def dot(a, b, dims=((1,), (0,))):
    return lax.dot_general(a, b, (dims, ((), ())), preferred_element_type=F32)


def block_kernel(
    group, last_row, edge, corner, where_ref,
    feat, up, down_rows, near, own, far, sides, cot, wc, pj, dw,
    out_ref, gc_ref, pg_ref, gd_ref,
    pad, shifted, resid_scr,
):
    step = pl.program_id(0)
    row = where_ref[0]
    col = where_ref[1]
    height, width = feat.shape[1], feat.shape[2]
    tall = height + 2 * DEPTH
    base = 8

    @pl.when(step == 0)
    def _():
        gc_ref[...] = jnp.zeros_like(gc_ref)
        pg_ref[...] = jnp.zeros_like(pg_ref)
        gd_ref[...] = jnp.zeros_like(gd_ref)

    line = lax.broadcasted_iota(jnp.int32, (width, width), 0)
    across = lax.broadcasted_iota(jnp.int32, (width, width), 1)
    flip = (line + across == width - 1).astype(BF)

    for j in range(group):
        face = step * group + j
        pad[DEPTH : DEPTH + height, base : base + width, :] = feat[j].astype(F32)
        pad[:DEPTH, base : base + width, :] = up[j].astype(F32)
        pad[DEPTH + height :, base : base + width, :] = down_rows[j].astype(F32)

        def link(side, what):
            return edge[face * 12 + side * 3 + what]

        for side, column in ((3, lambda k: base - 1 - k), (1, lambda k: base + width + k)):
            g, t, rev = link(side, 0), link(side, 1), link(side, 2)
            for k in range(DEPTH):
                for i in range(tall):
                    pick = jnp.where(rev == 1, tall - 1 - i, i)
                    pad[i, column(k) : column(k) + 1, :] = near[rev, t, g, k, pl.ds(pick, 1), :]

        def frame(side, corners, line_of, mine):
            g, t, rev = link(side, 0), link(side, 1), link(side, 2)
            for k in range(DEPTH):
                picked = jnp.where(
                    t == mine, own[g, k].astype(F32),
                    jnp.where(t == 2 - mine, far[g, k].astype(F32), sides[face, k].astype(F32)),
                ).astype(BF)
                turned = dot(flip, picked)
                pad[line_of(k), base : base + width, :] = jnp.where(
                    rev == 1, turned, picked.astype(F32)
                )
            for e, column in corners:
                cg = corner[face * 12 + e * 3]
                ce = corner[face * 12 + e * 3 + 1]
                cw = corner[face * 12 + e * 3 + 2]
                upper = ce < 2
                t = jnp.where((ce == 0) | (ce == 3), 3, 1)
                away = jnp.where(upper == (mine == 0), 0, 1)
                for a in range(DEPTH):
                    for b in range(DEPTH):
                        u = jnp.where(cw == 1, b, a)
                        v = jnp.where(cw == 1, a, b)
                        i = jnp.where(upper, DEPTH + u, tall - 1 - DEPTH - u)
                        value = near[away, t, jnp.maximum(cg, 0), v, pl.ds(i, 1), :]
                        pad[line_of(a), column(b) : column(b) + 1, :] = jnp.where(
                            cg >= 0, value, jnp.zeros_like(value)
                        )

        @pl.when(row == 0)
        def _():
            frame(
                0,
                ((0, lambda b: base - 1 - b), (1, lambda b: base + width + b)),
                lambda k: DEPTH - 1 - k,
                0,
            )

        @pl.when(row == last_row)
        def _():
            frame(
                2,
                ((3, lambda b: base - 1 - b), (2, lambda b: base + width + b)),
                lambda k: DEPTH + height + k,
                2,
            )

        for tap in range(3):
            at = base - DEPTH + tap * DEPTH
            shifted[tap, j] = pad[:, at : at + width, :].astype(BF)

    pixels = group * height * width
    wide = jnp.concatenate(
        [
            shifted[tap % 3, :, (tap // 3) * DEPTH : (tap // 3) * DEPTH + height].reshape(pixels, 128)
            for tap in range(9)
        ],
        axis=1,
    )
    pre = dot(wide, wc[...])
    half = 0.5 * (1.0 + lax.erf(pre * 0.7071067811865476))
    hidden = (pre * half).astype(BF)
    slope = half + pre * jnp.exp(-0.5 * pre * pre) * 0.3989422804014327

    part = dot(hidden, pj[...])
    part = part + jnp.where(col == 0, feat[...].reshape(pixels, 128).astype(F32), 0.0)
    quarter = pixels // 4
    blocks = (group * height // 2, width // 2, 128)
    resid_scr[...] = part.reshape(resid_scr.shape)
    grouped = jnp.concatenate(
        [
            resid_scr[:, ro, pl.ds(co, width // 2, stride=2), :].reshape(quarter, 128)
            for ro in range(2)
            for co in range(2)
        ],
        axis=1,
    )
    high = grouped.astype(BF)
    low = (grouped - high.astype(F32)).astype(BF)
    out = dot(high, dw[...]) + dot(low, dw[...])
    out_ref[...] = out.reshape(out_ref.shape)
    upstream = cot[...].reshape(quarter, 128)
    gd_ref[...] += dot(high, upstream, ((0,), (0,)))
    back = dot(upstream, dw[...], ((1,), (1,))).astype(BF).astype(F32)
    for ro in range(2):
        for co in range(2):
            at = (2 * ro + co) * 128
            resid_scr[:, ro, pl.ds(co, width // 2, stride=2), :] = back[:, at : at + 128].reshape(blocks)
    gresid = resid_scr[...].reshape(pixels, 128).astype(BF)
    pg_ref[...] += dot(hidden, gresid, ((0,), (0,)))
    gpre = (dot(gresid, pj[...], ((1,), (1,))) * slope).astype(BF)
    gc_ref[...] += dot(wide, gpre, ((0,), (0,)))


def run_block(edge, corner, place, feat, up, down_rows, near, own, far, sides, cot, wc, pj, dw, last_row):
    faces, height, width, channels = feat.shape
    hid = wc.shape[1]
    group = 3 if width <= 64 else 1
    tall = height + 2 * DEPTH
    smem = pl.BlockSpec(memory_space=pltpu.SMEM)

    def per_face(shape):
        return pl.BlockSpec((group,) + shape[1:], lambda s: (s, 0, 0, 0))

    def whole(shape):
        return pl.BlockSpec(shape, lambda s: (0,) * len(shape))

    out_shapes = (
        (faces, height // 2, width // 2, channels),
        (wc.shape[0], hid),
        (hid, channels),
        (4 * channels, channels),
    )
    flops = 2 * faces * height * width * (2 * 9 * channels * hid + 3 * hid * channels)
    return pl.pallas_call(
        functools.partial(block_kernel, group, last_row),
        grid=(faces // group,),
        in_specs=[
            smem, smem, smem,
            per_face(feat.shape), per_face(up.shape), per_face(down_rows.shape),
            whole(near.shape), whole(own.shape), whole(far.shape), whole(sides.shape),
            per_face(cot.shape), whole(wc.shape), whole(pj.shape), whole(dw.shape),
        ],
        out_specs=(
            per_face(out_shapes[0]),
            whole(out_shapes[1]), whole(out_shapes[2]), whole(out_shapes[3]),
        ),
        out_shape=tuple(jax.ShapeDtypeStruct(s, F32) for s in out_shapes),
        scratch_shapes=[
            pltpu.VMEM((tall, width + 16, channels), F32),
            pltpu.VMEM((3, group, tall, width, channels), BF),
            pltpu.VMEM((group * height // 2, 2, width, channels), F32),
        ],
        compiler_params=pltpu.CompilerParams(
            dimension_semantics=("arbitrary",), vmem_limit_bytes=56 << 20
        ),
        cost_estimate=pl.CostEstimate(
            flops=flops, transcendentals=2 * faces * height * width * hid, bytes_accessed=12 << 20
        ),
    )(edge, corner, place, feat, up, down_rows, near, own, far, sides, cot, wc, pj, dw)


def on_device(features, cotangent, conv_weight, projection_weight, down_weight, edge_links, corner_links):
    faces, height, breadth, channels = features.shape
    rows = lax.axis_size("row")
    cols = lax.axis_size("col")
    row = lax.axis_index("row")
    col = lax.axis_index("col")
    last = rows - 1
    tall = height + 2 * DEPTH
    width = cols * breadth
    hid = conv_weight.shape[1]
    part_rows = projection_weight.shape[0]

    feat = gather_pair(features, "col", 2)
    cot = gather_pair(cotangent, "col", 2)
    small = gather_pair(jnp.concatenate([projection_weight, down_weight], axis=0), "col", 1)
    packed = jnp.concatenate([pack_cols(conv_weight), small], axis=0)

    right = jnp.stack([feat[:, :, width - 1 - k] for k in range(DEPTH)], axis=1)
    left = jnp.stack([feat[:, :, k] for k in range(DEPTH)], axis=1)
    edges = jnp.stack([right, left])
    mirror = [(i, last - i) for i in range(rows)]
    mirrored = lax.ppermute(edges, "row", mirror)

    forward = [(i, i + 1) for i in range(last)]
    backward = [(i + 1, i) for i in range(last)]

    def rows_of(value):
        return value.reshape(-1, channels)

    going_down = jnp.concatenate(
        [rows_of(feat[:, height - DEPTH :]), rows_of(mirrored[:, :, :, :DEPTH])]
    )
    going_up = jnp.concatenate(
        [rows_of(feat[:, :DEPTH]), rows_of(mirrored[:, :, :, height - DEPTH :])]
    )
    from_above = lax.ppermute(going_down, "row", forward)
    from_below = lax.ppermute(going_up, "row", backward)
    cut = faces * DEPTH * width
    up = from_above[:cut].reshape(faces, DEPTH, width, channels)
    below = from_below[:cut].reshape(faces, DEPTH, width, channels)
    small_shape = (2, faces, DEPTH, DEPTH, channels)
    mirrored_tall = jnp.concatenate(
        [from_below[cut:].reshape(small_shape), mirrored, from_above[cut:].reshape(small_shape)],
        axis=3,
    )

    def side_columns(lines):
        return jnp.stack(
            [
                jnp.stack([lines[:, :, lines.shape[2] - 1 - k] for k in range(DEPTH)], axis=1),
                jnp.stack([lines[:, :, k] for k in range(DEPTH)], axis=1),
            ]
        )

    edges_tall = jnp.concatenate([side_columns(up), edges, side_columns(below)], axis=3)

    own = jnp.where(row == 0, feat[:, :DEPTH], feat[:, ::-1][:, :DEPTH])
    far = lax.ppermute(own, "row", [(0, last), (last, 0)])

    long = jnp.pad(own, ((0, 0), (0, 0), (DEPTH, DEPTH), (0, 0)))
    pieces = jnp.stack([rows_of(long[:, :, height * d : height * d + tall]) for d in range(rows)])
    pieces = jnp.where(col % 2 == 1, pieces[::-1], pieces)

    sides_of = edge_links[:, 0::2, :].transpose(1, 0, 2).reshape(2 * faces, 3)
    wanted = jnp.where(sides_of[:, 1] % 2 == 1, sides_of[:, 1] // 2 * faces + sides_of[:, 0], -1)
    choose = (wanted[:, None] == jnp.arange(2 * faces)[None, :]).astype(BF)

    def give(columns):
        flat = columns.reshape(2 * faces, DEPTH * height * channels)
        return dot(choose, flat).astype(BF).reshape(2, faces * DEPTH * height, channels)

    given = give(edges)
    given_mirrored = give(mirrored)
    fill = jnp.zeros((2, pieces.shape[1] - given.shape[1], channels), BF)
    given_long = jnp.concatenate([given, fill], axis=1)
    middle = jnp.zeros((rows - 2,) + given_long.shape[1:], BF)
    columns_out = jnp.concatenate([given_long[:1], middle, given_long[1:]])
    bands_out = jnp.where((row == 0) | (row == last), pieces, columns_out)

    half_rows = packed.shape[0] // 2
    weights_out = jnp.tile(packed.reshape(2, half_rows, channels), (rows // 2, 1, 1))
    sent = jnp.concatenate([weights_out, bands_out], axis=1)
    got = lax.all_to_all(sent, "row", 0, 0)

    got_half = got[:, :half_rows]
    other_half = swap(got_half, "row", 1)
    even = row % 2 == 0
    full = jnp.concatenate(
        [jnp.where(even, got_half, other_half), jnp.where(even, other_half, got_half)], axis=1
    )
    conv_rows = packed.shape[0] - 2 * part_rows
    wc = unpack_cols(full[:, :conv_rows], hid).reshape(rows * conv_weight.shape[0], hid)
    pj_all = full[:, conv_rows : conv_rows + part_rows].reshape(rows * part_rows, channels)
    pj = lax.dynamic_slice_in_dim(pj_all, col * hid, hid, 0)
    dw = full[:, conv_rows + part_rows :].reshape(rows * part_rows, channels)

    ends = jnp.stack([got[0, half_rows:], got[last, half_rows:]])
    ends_other = swap(ends, "col", 1)
    even_col = col % 2 == 0
    ends_shape = (2, faces, DEPTH, tall, channels)
    ends_direct = jnp.where(even_col, ends, ends_other).reshape(ends_shape)
    ends_mirror = jnp.where(even_col, ends_other, ends).reshape(ends_shape)

    def strips(ends_part, columns):
        return jnp.stack([ends_part[0], columns[0], ends_part[1], columns[1]])

    near = jnp.stack(
        [strips(ends_direct, edges_tall), strips(ends_mirror, mirrored_tall)]
    ).astype(F32)

    span = given.shape[1]
    mine = jnp.where(row == 0, given[0], given[1])
    theirs = jnp.where(row == 0, given_mirrored[0], given_mirrored[1])
    first = jnp.where(row == 0, mine, theirs)
    final = jnp.where(row == 0, theirs, mine)
    sides = jnp.concatenate(
        [first[None], got[1:last, half_rows : half_rows + span], final[None]]
    )
    sides = sides.reshape(rows, faces, DEPTH, height, channels).transpose(1, 2, 0, 3, 4)
    sides = sides.reshape(faces, DEPTH, rows * height, channels)

    place = jnp.stack([row, col]).astype(jnp.int32)
    out_part, gc, pg, gd = run_block(
        edge_links.reshape(-1), corner_links.reshape(-1), place,
        feat, up, below, near, own, far, sides, cot, wc, pj, dw, last,
    )

    block_out = scatter_sum_pair(out_part, "col", 2).astype(BF)
    gc_out = pack_cols(gc.astype(BF).reshape(rows, conv_weight.shape[0], hid))
    pg_wide = jnp.zeros((rows, part_rows, channels), BF)
    pg_wide = lax.dynamic_update_slice_in_dim(
        pg_wide, pg.astype(BF).reshape(-1, part_rows, channels), col * (rows // cols), 0
    )
    gd_out = gd.astype(BF).reshape(rows, part_rows, channels)
    shares = lax.all_to_all(jnp.concatenate([gc_out, pg_wide, gd_out], axis=1), "row", 0, 0)
    total = jnp.sum(shares.astype(F32), axis=0)
    grad_conv = unpack_cols(total[:conv_rows], hid)
    smaller = scatter_sum_pair(total[conv_rows:], "col", 1)
    return block_out, grad_conv, smaller[:part_rows], smaller[part_rows:]


def solution(mesh):
    return jax.shard_map(
        on_device,
        mesh=mesh,
        in_specs=(
            P(None, "row", "col", None),
            P(None, "row", "col", None),
            P("row", "col"),
            P("row", "col"),
            P("row", "col"),
            P(),
            P(),
        ),
        out_specs=(P(None, "row", "col", None), P("row", "col"), P("row", "col"), P("row", "col")),
        check_vma=False,
    )
```

time: 637 us -> 133 us (0.21)
  waiting for transfers between devices: 208 us -> 40.6 us
  matrix products: 138 us -> 0.39 us
  blocking collectives: 129 us -> 0 us
  local copies, waits for them, and re-layouts: 93.2 us -> 18 us
  starting transfers between devices: 9.09 us -> 39.3 us
  other arithmetic: 34.3 us -> 14.1 us
  Pallas kernels: 0 us -> 17.9 us
  between operations: 14.2 us -> 1.26 us
  loops' own time: 6.47 us -> 0 us
    reduce_scatter x4 -> x0, waiting for transfers between devices: 185 us -> none  [the longest x1 64.4 us: on_device(): lax.psum_scatter(totals[0], 'row', scatter_dimension=0, tiled=True)]
    dot_general x288 -> x2, matrix products: 138 us -> 0.39 us  [dot(): return lax.dot_general(a, b, (dims, ((), ())), preferred_element_type=F32)]
    all_gather x9 -> x0, blocking collectives: 129 us -> none  [the longest x1 23.4 us: on_device(): lax.all_gather(conv_weight, 'row', axis=0, tiled=True)]
    all_to_all x0 -> x2, waiting for transfers between devices: none -> 27.4 us  [the longest x1 15.7 us: on_device(): got = lax.all_to_all(sent, 'row', 0, 0)]
    unnamed x11 -> x0, waiting for transfers between devices: 22.7 us -> none
    pallas_call x0 -> x1, Pallas kernels: none -> 17.9 us  [run_block(): pl.pallas_call(functools.partial(block_kernel, group, last_row), grid=(fa...]
    rev x8 -> x0, local copies, waits for them, and re-layouts: 17.4 us -> none  [the longest x1 4.97 us: border_bands(): left_band = jnp.swapaxes(picked[:, 3, ::-1], 1, 2)]
    all_to_all x0 -> x2, starting transfers between devices: none -> 17 us  [the longest x1 12.2 us: on_device(): lax.all_to_all(jnp.concatenate([gc_out, pg_wide, gd_out], axis=1), 'row',...]
  transfers between devices with their start and end apart: 13 -> 13, of which waited for: 6 -> 8; matrix products, arithmetic and copies ran while one was open for 11% -> 22% of each run, Pallas kernels for 0% -> 0%
where the time goes in v1:
time: 133 us; the launch traced here: 131 us
  waiting for transfers between devices  40.6 us (31%)
  starting transfers between devices  39.3 us (30%)
  local copies, waits for them, and re-layouts  18 us (14%)
  Pallas kernels  17.9 us (13%)
  other arithmetic  14.1 us (11%)
    pallas_call x1, Pallas kernels, run_block(): pl.pallas_call(functools.partial(block_kernel, group, last_row), grid=(fa...  17.9 us
    all_to_all x1, waiting for transfers between devices, on_device(): got = lax.all_to_all(sent, 'row', 0, 0)  15.7 us
    ppermute x7, waiting for transfers between devices, swap(): return lax.ppermute(value, axis, [(i, i ^ bit) for i in range(count)])  12.7 us
    all_to_all x1, starting transfers between devices, on_device(): lax.all_to_all(jnp.concatenate([gc_out, pg_wide, gd_out], axis=1), 'row',...  12.2 us
    all_to_all x1, waiting for transfers between devices, on_device(): lax.all_to_all(jnp.concatenate([gc_out, pg_wide, gd_out], axis=1), 'row',...  11.7 us
    ppermute x7, starting transfers between devices, swap(): return lax.ppermute(value, axis, [(i, i ^ bit) for i in range(count)])  10.8 us
    unnamed x44, local copies, waits for them, and re-layouts  8.94 us
    all_to_all x1, starting transfers between devices, on_device(): got = lax.all_to_all(sent, 'row', 0, 0)  4.77 us
  transfers between devices with their start and end apart: 13, of which 8 were waited for; matrix products, arithmetic and copies ran while one was open for 22% of the time, Pallas kernels for 0%

profile of v1, /device:TPU:0, one launch (start us, length us, event | category | flops | bytes accessed | tf_op | source)
XLA Modules:
  0.0 131.4 jit_solution(8239060978625824826)
XLA Ops:
  0.6 3.0 %collective-permute-start = (bf16[12,4,32,128]{3,2,1,0:T(8,128)(2,1)}, bf16[12,4,32,128]{3,2,1,0:T(8,128)(2,1)S(1)}, u32[]{:S(2)}, u32[]{:S(2)}) collective-permute-start(bf16[12,4,32,128]{3,2,1,0:T(8,128)(2,1)} %param.7), channel_id=1, source_target_pairs={{0,1},{1,0},{2,3},{3,2},{4,5},{5,4},{6,7},{7,6},{8,9},{9,8},{10,11... | collective-permute-start | bytes 1179656 | tf_op jit(solution)/shard_map/ppermute | solution.py:17
  3.7 0.7 constant_dynamic-update-slice_fusion.1
  4.4 0.7 constant_dynamic-update-slice_fusion
  5.1 2.0 %collective-permute-start.7 = (bf16[12,2,16,128]{3,2,1,0:T(8,128)(2,1)}, bf16[12,2,16,128]{3,2,1,0:T(8,128)(2,1)S(1)}, u32[]{:S(2)}, u32[]{:S(2)}) collective-permute-start(bf16[12,2,16,128]{3,2,1,0:T(8,128)(2,1)} %param.8), channel_id=1, source_target_pairs={{0,1},{1,0},{2,3},{3,2},{4,5},{5,4},{6,7},{7,6},{8,9},{9,8},{10,11... | collective-permute-start | bytes 294920 | tf_op jit(solution)/shard_map/ppermute | solution.py:17
  7.1 0.7 slice.282
  7.9 0.7 fusion.21
  9.3 0.8 copy.101
  10.8 0.8 copy.102
  12.3 1.9 %collective-permute-done.4 = bf16[64,64]{1,0:T(8,128)(2,1)S(1)} collective-permute-done((bf16[64,64]{1,0:T(8,128)(2,1)S(1)}, bf16[64,64]{1,0:T(8,128)(2,1)S(1)}, u32[]{:S(2)}, u32[]{:S(2)}) %collective-permute-start.4) | collective-permute-done | bytes 8224 | tf_op jit(solution)/shard_map/ppermute | solution.py:17
  14.3 1.2 collective-permute-done.7
  15.5 0.9 broadcast_select_fusion.7
  16.4 0.7 pad_maximum_fusion.7.cot
  17.5 3.5 %collective-permute-start.1 = (bf16[2,12,2,4,128]{4,3,2,1,0:T(4,128)(2,1)S(1)}, bf16[2,12,2,4,128]{4,3,2,1,0:T(4,128)(2,1)S(1)}, u32[]{:S(2)}, u32[]{:S(2)}) collective-permute-start(bf16[2,12,2,4,128]{4,3,2,1,0:T(4,128)(2,1)S(1)} %pad_maximum_fusion.11), channel_id=1, source_target_pairs={{0,30},{2,28},{4,26},{6,24},{8,22},{10,20},{12,18},{14,16},{16,14}... | collective-permute-start | bytes 147464 | tf_op jit(solution)/shard_map/ppermute | solution.py:263
  21.2 0.9 pad_slice_fusion.4
  22.1 2.9 %collective-permute-start.6 = (bf16[12,2,64,128]{3,2,1,0:T(8,128)(2,1)S(1)}, bf16[12,2,64,128]{3,2,1,0:T(8,128)(2,1)}, u32[]{:S(2)}, u32[]{:S(2)}) collective-permute-start(bf16[12,2,64,128]{3,2,1,0:T(8,128)(2,1)S(1)} %get-tuple-element.12.own), channel_id=1, source_target_pairs={{0,30},{30,0},{1,31},{31,1}} | collective-permute-start | bytes 1179656 | tf_op jit(solution)/shard_map/ppermute | solution.py:299
  25.3 0.8 constant_dynamic-update-slice_fusion.16
  26.1 0.8 constant_dynamic-update-slice_fusion.15
  26.9 0.8 constant_dynamic-update-slice_fusion.14
  27.7 0.8 constant_dynamic-update-slice_fusion.13
  28.5 0.8 constant_dynamic-update-slice_fusion.12
  29.4 0.8 constant_dynamic-update-slice_fusion.11
  30.2 0.8 constant_dynamic-update-slice_fusion.10
  31.0 0.8 constant_dynamic-update-slice_fusion.9
  32.2 1.1 pad_maximum_fusion
  33.4 1.0 pad_maximum_fusion.1.feat
  34.4 4.8 %all-to-all-start = ((bf16[16,296,128]{2,1,0:T(8,128)(2,1)}), bf16[16,296,128]{2,1,0:T(8,128)(2,1)S(1)}, u32[]{:S(2)}, u32[]{:S(2)}) async-start(bf16[16,296,128]{2,1,0:T(8,128)(2,1)} %pad_maximum_fusion), calls=%async_computation | async-start | bytes 2424832 | tf_op jit(solution)/shard_map/all_to_all | solution.py:324
  39.2 0.8 pad_maximum_fusion.5
  40.0 1.3 collective-permute-start.3
  41.3 0.8 pad_maximum_fusion.4
  42.1 3.8 %collective-permute-start.2 = (bf16[1632,128]{1,0:T(8,128)(2,1)}, bf16[1632,128]{1,0:T(8,128)(2,1)}, u32[]{:S(2)}, u32[]{:S(2)}) collective-permute-start(bf16[1632,128]{1,0:T(8,128)(2,1)} %pad_maximum_fusion.4), channel_id=1, source_target_pairs={{0,2},{2,4},{4,6},{6,8},{8,10},{10,12},{12,14},{14,16},{16,18},{18... | collective-permute-start | bytes 1253384 | tf_op jit(solution)/shard_map/ppermute | solution.py:277
  46.8 1.0 slice.334
  48.0 0.8 slice.369
  49.1 15.7 %all-to-all-done = bf16[16,296,128]{2,1,0:T(8,128)(2,1)S(1)} async-done(((bf16[16,296,128]{2,1,0:T(8,128)(2,1)}), bf16[16,296,128]{2,1,0:T(8,128)(2,1)S(1)}, u32[]{:S(2)}, u32[]{:S(2)}) %all-to-all-start) | async-done | bytes 1212448 | tf_op jit(solution)/shard_map/all_to_all | solution.py:324
  64.8 1.0 collective-permute-start.8
  65.8 1.6 %collective-permute-start.5 = (bf16[2,192,128]{2,1,0:T(8,128)(2,1)S(1)}, bf16[2,192,128]{2,1,0:T(8,128)(2,1)S(1)}, u32[]{:S(2)}, u32[]{:S(2)}) collective-permute-start(bf16[2,192,128]{2,1,0:T(8,128)(2,1)S(1)} %pad_maximum_fusion.8), channel_id=1, source_target_pairs={{0,1},{1,0},{2,3},{3,2},{4,5},{5,4},{6,7},{7,6},{8,9},{9,8},{10,11... | collective-permute-start | bytes 294920 | tf_op jit(solution)/shard_map/ppermute | solution.py:17
  67.4 1.0 pad_maximum_fusion.6
  68.4 2.2 %collective-permute-done.5 = bf16[2,192,128]{2,1,0:T(8,128)(2,1)S(1)} collective-permute-done((bf16[2,192,128]{2,1,0:T(8,128)(2,1)S(1)}, bf16[2,192,128]{2,1,0:T(8,128)(2,1)S(1)}, u32[]{:S(2)}, u32[]{:S(2)}) %collective-permute-start.5) | collective-permute-done | bytes 98336 | tf_op jit(solution)/shard_map/ppermute | solution.py:17
  70.7 1.0 maximum_convert_fusion.near
  73.1 0.9 fusion.1
  74.0 17.9 %shard_map.102 = (f32[12,2,32,128]{3,2,1,0:T(8,128)}, f32[1152,256]{1,0:T(8,128)}, f32[256,128]{1,0:T(8,128)}, f32[512,128]{1,0:T(8,128)}) custom-call(s32[144]{0:T(256)} %reshape.166.edge, s32[144]{0:T(256)} %reshape.167.corner, s32[2]{0:T(128)} %pad_add_fusion.where_ref, bf16[12,4,64,128]{3,2,1,0:T(8,128)(2,1)} %pad_maximum_fusion.1.feat, ...), custom_call_target="tpu_custom_call" | custom-call | flops 4227858432 | bytes 12582912 | tf_op jit(solution)/shard_map/pallas_call | solution.py:214
  91.9 1.4 %convert_element_type.31 = bf16[1152,256]{1,0:T(8,128)(2,1)S(1)} convert(f32[1152,256]{1,0:T(8,128)} %get-tuple-element.9) | non-fusion elementwise | flops 294912 | bytes 1769472 | tf_op jit(solution)/shard_map/convert_element_type | solution.py:370
  93.5 1.0 pad_maximum_fusion.2
  94.5 12.2 %all-to-all-start.1 = ((bf16[16,208,128]{2,1,0:T(8,128)(2,1)}), bf16[16,208,128]{2,1,0:T(8,128)(2,1)S(1)}, u32[]{:S(2)}, u32[]{:S(2)}) async-start(bf16[16,208,128]{2,1,0:T(8,128)(2,1)} %pad_maximum_fusion.2), calls=%async_computation.1 | async-start | bytes 1703936 | tf_op jit(solution)/shard_map/all_to_all | solution.py:376
  106.8 1.6 %collective-permute-start.9 = (f32[12,2,16,128]{3,2,1,0:T(8,128)S(1)}, f32[12,2,16,128]{3,2,1,0:T(8,128)S(1)}, u32[]{:S(2)}, u32[]{:S(2)}) collective-permute-start(f32[12,2,16,128]{3,2,1,0:T(8,128)S(1)} %slice_select_fusion), channel_id=1, source_target_pairs={{0,1},{1,0},{2,3},{3,2},{4,5},{5,4},{6,7},{7,6},{8,9},{9,8},{10,11... | collective-permute-start | bytes 589832 | tf_op jit(solution)/shard_map/ppermute | solution.py:17
  108.4 5.7 %collective-permute-done.9 = f32[12,2,16,128]{3,2,1,0:T(8,128)S(1)} collective-permute-done((f32[12,2,16,128]{3,2,1,0:T(8,128)S(1)}, f32[12,2,16,128]{3,2,1,0:T(8,128)S(1)}, u32[]{:S(2)}, u32[]{:S(2)}) %collective-permute-start.9) | collective-permute-done | bytes 196640 | tf_op jit(solution)/shard_map/ppermute | solution.py:17
  114.8 11.7 %all-to-all-done.1 = bf16[16,208,128]{2,1,0:T(8,128)(2,1)S(1)} async-done(((bf16[16,208,128]{2,1,0:T(8,128)(2,1)}), bf16[16,208,128]{2,1,0:T(8,128)(2,1)S(1)}, u32[]{:S(2)}, u32[]{:S(2)}) %all-to-all-start.1) | async-done | bytes 852000 | tf_op jit(solution)/shard_map/all_to_all | solution.py:376
  126.7 1.6 %collective-permute-start.10 = (f32[64,64]{1,0:T(8,128)S(1)}, f32[64,64]{1,0:T(8,128)S(1)}, u32[]{:S(2)}, u32[]{:S(2)}) collective-permute-start(f32[64,64]{1,0:T(8,128)S(1)} %slice_select_fusion.3), channel_id=1, source_target_pairs={{0,1},{1,0},{2,3},{3,2},{4,5},{5,4},{6,7},{7,6},{8,9},{9,8},{10,11... | collective-permute-start | bytes 49160 | tf_op jit(solution)/shard_map/ppermute | solution.py:17
  128.9 1.8 %collective-permute-done.10 = f32[64,64]{1,0:T(8,128)S(1)} collective-permute-done((f32[64,64]{1,0:T(8,128)S(1)}, f32[64,64]{1,0:T(8,128)S(1)}, u32[]{:S(2)}, u32[]{:S(2)}) %collective-permute-start.10) | collective-permute-done | bytes 16416 | tf_op jit(solution)/shard_map/ppermute | solution.py:17
  (107 shorter events, 8.8 us)
Async XLA Ops:
  0.6 16.4 %copy-start.4 = (bf16[12,4,32,128]{3,2,1,0:T(8,128)(2,1)S(1)}, bf16[12,4,32,128]{3,2,1,0:T(8,128)(2,1)}, u32[]{:S(2)}) copy-start(bf16[12,4,32,128]{3,2,1,0:T(8,128)(2,1)} %param.7) | copy-start | bytes 1179652
  0.6 16.4 %collective-permute-start = (bf16[12,4,32,128]{3,2,1,0:T(8,128)(2,1)}, bf16[12,4,32,128]{3,2,1,0:T(8,128)(2,1)S(1)}, u32[]{:S(2)}, u32[]{:S(2)}) collective-permute-start(bf16[12,4,32,128]{3,2,1,0:T(8,128)(2,1)} %param.7), channel_id=1, source_target_pairs={{0,1},{1,0},{2,3},{3,2},{4,5},{5,4},{6,7},{7,6},{8,9},{9,8},{10,11... | collective-permute-start | bytes 1179656 | tf_op jit(solution)/shard_map/ppermute | solution.py:17
  5.1 9.1 %collective-permute-start.4 = (bf16[64,64]{1,0:T(8,128)(2,1)S(1)}, bf16[64,64]{1,0:T(8,128)(2,1)S(1)}, u32[]{:S(2)}, u32[]{:S(2)}) collective-permute-start(bf16[64,64]{1,0:T(8,128)(2,1)S(1)} %constant_dynamic-update-slice_fusion), channel_id=1, source_target_pairs={{0,1},{1,0},{2,3},{3,2},{4,5},{5,4},{6,7},{7,6},{8,9},{9,8},{10,11... | collective-permute-start | bytes 24584 | tf_op jit(solution)/shard_map/ppermute | solution.py:17
  5.1 10.3 %collective-permute-start.7 = (bf16[12,2,16,128]{3,2,1,0:T(8,128)(2,1)}, bf16[12,2,16,128]{3,2,1,0:T(8,128)(2,1)S(1)}, u32[]{:S(2)}, u32[]{:S(2)}) collective-permute-start(bf16[12,2,16,128]{3,2,1,0:T(8,128)(2,1)} %param.8), channel_id=1, source_target_pairs={{0,1},{1,0},{2,3},{3,2},{4,5},{5,4},{6,7},{7,6},{8,9},{9,8},{10,11... | collective-permute-start | bytes 294920 | tf_op jit(solution)/shard_map/ppermute | solution.py:17
  17.5 21.6 %collective-permute-start.1 = (bf16[2,12,2,4,128]{4,3,2,1,0:T(4,128)(2,1)S(1)}, bf16[2,12,2,4,128]{4,3,2,1,0:T(4,128)(2,1)S(1)}, u32[]{:S(2)}, u32[]{:S(2)}) collective-permute-start(bf16[2,12,2,4,128]{4,3,2,1,0:T(4,128)(2,1)S(1)} %pad_maximum_fusion.11), channel_id=1, source_target_pairs={{0,30},{2,28},{4,26},{6,24},{8,22},{10,20},{12,18},{14,16},{16,14}... | collective-permute-start | bytes 147464 | tf_op jit(solution)/shard_map/ppermute | solution.py:263
  21.2 5.8 %copy-start = (bf16[12,2,64,128]{3,2,1,0:T(8,128)(2,1)}, bf16[12,2,64,128]{3,2,1,0:T(8,128)(2,1)S(1)}, u32[]{:S(2)}) copy-start(bf16[12,2,64,128]{3,2,1,0:T(8,128)(2,1)S(1)} %get-tuple-element.12.own) | copy-start | bytes 1179652
  22.1 51.9 %collective-permute-start.6 = (bf16[12,2,64,128]{3,2,1,0:T(8,128)(2,1)S(1)}, bf16[12,2,64,128]{3,2,1,0:T(8,128)(2,1)}, u32[]{:S(2)}, u32[]{:S(2)}) collective-permute-start(bf16[12,2,64,128]{3,2,1,0:T(8,128)(2,1)S(1)} %get-tuple-element.12.own), channel_id=1, source_target_pairs={{0,30},{30,0},{1,31},{31,1}} | collective-permute-start | bytes 1179656 | tf_op jit(solution)/shard_map/ppermute | solution.py:299
  34.4 30.3 %all-to-all-start = ((bf16[16,296,128]{2,1,0:T(8,128)(2,1)}), bf16[16,296,128]{2,1,0:T(8,128)(2,1)S(1)}, u32[]{:S(2)}, u32[]{:S(2)}) async-start(bf16[16,296,128]{2,1,0:T(8,128)(2,1)} %pad_maximum_fusion), calls=%async_computation | async-start | bytes 2424832 | tf_op jit(solution)/shard_map/all_to_all | solution.py:324
  40.0 6.2 %collective-permute-start.3 = (bf16[1632,128]{1,0:T(8,128)(2,1)}, bf16[1632,128]{1,0:T(8,128)(2,1)S(1)}, u32[]{:S(2)}, u32[]{:S(2)}) collective-permute-start(bf16[1632,128]{1,0:T(8,128)(2,1)} %pad_maximum_fusion.5), channel_id=1, source_target_pairs={{2,0},{4,2},{6,4},{8,6},{10,8},{12,10},{14,12},{16,14},{18,16},{20... | collective-permute-start | bytes 1253384 | tf_op jit(solution)/shard_map/ppermute | solution.py:278
  42.1 4.7 %collective-permute-start.2 = (bf16[1632,128]{1,0:T(8,128)(2,1)}, bf16[1632,128]{1,0:T(8,128)(2,1)}, u32[]{:S(2)}, u32[]{:S(2)}) collective-permute-start(bf16[1632,128]{1,0:T(8,128)(2,1)} %pad_maximum_fusion.4), channel_id=1, source_target_pairs={{0,2},{2,4},{4,6},{6,8},{8,10},{10,12},{12,14},{14,16},{16,18},{18... | collective-permute-start | bytes 1253384 | tf_op jit(solution)/shard_map/ppermute | solution.py:277
  46.2 18.5 %copy-start.2 = (bf16[1536,128]{1,0:T(8,128)(2,1)}, bf16[1536,128]{1,0:T(8,128)(2,1)S(1)}, u32[]{:S(2)}) copy-start(bf16[1536,128]{1,0:T(8,128)(2,1)S(1)} %slice.338) | copy-start | bytes 1179652
  47.8 18.0 %copy-start.3 = (bf16[1536,128]{1,0:T(8,128)(2,1)}, bf16[1536,128]{1,0:T(8,128)(2,1)S(1)}, u32[]{:S(2)}) copy-start(bf16[1536,128]{1,0:T(8,128)(2,1)S(1)} %slice.334) | copy-start | bytes 1179652
  64.8 7.0 %collective-permute-start.8 = (bf16[16,104,128]{2,1,0:T(8,128)(2,1)S(1)}, bf16[16,104,128]{2,1,0:T(8,128)(2,1)S(1)}, u32[]{:S(2)}, u32[]{:S(2)}) collective-permute-start(bf16[16,104,128]{2,1,0:T(8,128)(2,1)S(1)} %slice.378), channel_id=1, source_target_pairs={{0,2},{2,0},{4,6},{6,4},{8,10},{10,8},{12,14},{14,12},{16,18},{18,... | collective-permute-start | bytes 1277960 | tf_op jit(solution)/shard_map/ppermute | solution.py:17
  65.8 4.8 %collective-permute-start.5 = (bf16[2,192,128]{2,1,0:T(8,128)(2,1)S(1)}, bf16[2,192,128]{2,1,0:T(8,128)(2,1)S(1)}, u32[]{:S(2)}, u32[]{:S(2)}) collective-permute-start(bf16[2,192,128]{2,1,0:T(8,128)(2,1)S(1)} %pad_maximum_fusion.8), channel_id=1, source_target_pairs={{0,1},{1,0},{2,3},{3,2},{4,5},{5,4},{6,7},{7,6},{8,9},{9,8},{10,11... | collective-permute-start | bytes 294920 | tf_op jit(solution)/shard_map/ppermute | solution.py:17
  91.9 1.5 %copy-start.6 = (f32[256,128]{1,0:T(8,128)S(1)}, f32[256,128]{1,0:T(8,128)}, u32[]{:S(2)}) copy-start(f32[256,128]{1,0:T(8,128)} %get-tuple-element.10) | copy-start | bytes 393220
  91.9 1.5 %copy-start.5 = (f32[512,128]{1,0:T(8,128)S(1)}, f32[512,128]{1,0:T(8,128)}, u32[]{:S(2)}) copy-start(f32[512,128]{1,0:T(8,128)} %get-tuple-element.11) | copy-start | bytes 786436
  94.5 12.3 %copy-start.1 = (f32[12,2,32,128]{3,2,1,0:T(8,128)S(1)}, f32[12,2,32,128]{3,2,1,0:T(8,128)}, u32[]{:S(2)}) copy-start(f32[12,2,32,128]{3,2,1,0:T(8,128)} %get-tuple-element.8) | copy-start | bytes 1179652
  94.5 32.0 %all-to-all-start.1 = ((bf16[16,208,128]{2,1,0:T(8,128)(2,1)}), bf16[16,208,128]{2,1,0:T(8,128)(2,1)S(1)}, u32[]{:S(2)}, u32[]{:S(2)}) async-start(bf16[16,208,128]{2,1,0:T(8,128)(2,1)} %pad_maximum_fusion.2), calls=%async_computation.1 | async-start | bytes 1703936 | tf_op jit(solution)/shard_map/all_to_all | solution.py:376
  106.8 7.3 %collective-permute-start.9 = (f32[12,2,16,128]{3,2,1,0:T(8,128)S(1)}, f32[12,2,16,128]{3,2,1,0:T(8,128)S(1)}, u32[]{:S(2)}, u32[]{:S(2)}) collective-permute-start(f32[12,2,16,128]{3,2,1,0:T(8,128)S(1)} %slice_select_fusion), channel_id=1, source_target_pairs={{0,1},{1,0},{2,3},{3,2},{4,5},{5,4},{6,7},{7,6},{8,9},{9,8},{10,11... | collective-permute-start | bytes 589832 | tf_op jit(solution)/shard_map/ppermute | solution.py:17
  126.7 4.0 %collective-permute-start.10 = (f32[64,64]{1,0:T(8,128)S(1)}, f32[64,64]{1,0:T(8,128)S(1)}, u32[]{:S(2)}, u32[]{:S(2)}) collective-permute-start(f32[64,64]{1,0:T(8,128)S(1)} %slice_select_fusion.3), channel_id=1, source_target_pairs={{0,1},{1,0},{2,3},{3,2},{4,5},{5,4},{6,7},{7,6},{8,9},{9,8},{10,11... | collective-permute-start | bytes 49160 | tf_op jit(solution)/shard_map/ppermute | solution.py:17

commit v2 on v1

--- a/solution.py
+++ b/solution.py
@@ -250,97 +250,169 @@
     width = cols * breadth
     hid = conv_weight.shape[1]
     part_rows = projection_weight.shape[0]
-
-    feat = gather_pair(features, "col", 2)
-    cot = gather_pair(cotangent, "col", 2)
-    small = gather_pair(jnp.concatenate([projection_weight, down_weight], axis=0), "col", 1)
-    packed = jnp.concatenate([pack_cols(conv_weight), small], axis=0)
-
-    right = jnp.stack([feat[:, :, width - 1 - k] for k in range(DEPTH)], axis=1)
-    left = jnp.stack([feat[:, :, k] for k in range(DEPTH)], axis=1)
-    edges = jnp.stack([right, left])
-    mirror = [(i, last - i) for i in range(rows)]
-    mirrored = lax.ppermute(edges, "row", mirror)
-
-    forward = [(i, i + 1) for i in range(last)]
-    backward = [(i + 1, i) for i in range(last)]
+    pairs = rows // 2
+    pair = row // 2
+    core = row % 2
+    even = core == 0
+    pair_height = 2 * height
+    pair_tall = pair_height + 2 * DEPTH
+    same_core = [list(range(c, rows, 2)) for c in range(2)]
+    is_end = (row == 0) | (row == last)
 
     def rows_of(value):
         return value.reshape(-1, channels)
 
-    going_down = jnp.concatenate(
-        [rows_of(feat[:, height - DEPTH :]), rows_of(mirrored[:, :, :, :DEPTH])]
-    )
-    going_up = jnp.concatenate(
-        [rows_of(feat[:, :DEPTH]), rows_of(mirrored[:, :, :, height - DEPTH :])]
-    )
-    from_above = lax.ppermute(going_down, "row", forward)
-    from_below = lax.ppermute(going_up, "row", backward)
-    cut = faces * DEPTH * width
-    up = from_above[:cut].reshape(faces, DEPTH, width, channels)
-    below = from_below[:cut].reshape(faces, DEPTH, width, channels)
-    small_shape = (2, faces, DEPTH, DEPTH, channels)
+    def join_core(mine, other, dim):
+        return jnp.concatenate(
+            [jnp.where(even, mine, other), jnp.where(even, other, mine)], axis=dim
+        )
+
+    strip = jnp.where(row == 0, features[:, :DEPTH], features[:, ::-1][:, :DEPTH])
+    if cols == 2:
+        lefts = jnp.stack([features[:, :, k] for k in range(DEPTH)], axis=1)
+        rights = jnp.stack([features[:, :, breadth - 1 - k] for k in range(DEPTH)], axis=1)
+        mine = jnp.where(col == 0, lefts, rights)
+        seam = jnp.where(col == 0, strip[:, :, breadth - DEPTH :], strip[:, :, :DEPTH])
+        cut = faces * DEPTH * height
+        got = swap(jnp.concatenate([rows_of(mine), rows_of(seam)]), "col", 1)
+        other = got[:cut].reshape(mine.shape)
+        edges = jnp.stack([jnp.where(col == 0, other, mine), jnp.where(col == 0, mine, other)])
+        seam_got = got[cut:].reshape(seam.shape)
+        none = jnp.zeros_like(seam_got)
+        long = jnp.concatenate(
+            [jnp.where(col == 0, none, seam_got), strip, jnp.where(col == 0, seam_got, none)], axis=2
+        )
+        windows = jnp.stack(
+            [rows_of(long[:, :, pair_height * d : pair_height * d + pair_tall]) for d in range(pairs // 2)]
+        )
+        ahead = jnp.concatenate([windows, windows[::-1]])
+        behind = jnp.concatenate([windows[::-1], windows])
+        pieces = jnp.where(col == 0, ahead, behind)
+        direct_here = col == pair // (pairs // 2)
+    else:
+        ends = lax.all_gather(
+            jnp.concatenate([features[:, :, :DEPTH], features[:, :, breadth - DEPTH :]], axis=2), "col"
+        )
+        edges = jnp.stack(
+            [
+                jnp.stack([ends[cols - 1, :, :, 2 * DEPTH - 1 - k] for k in range(DEPTH)], axis=1),
+                jnp.stack([ends[0, :, :, k] for k in range(DEPTH)], axis=1),
+            ]
+        )
+        whole = lax.all_gather(strip, "col", axis=2, tiled=True)
+        long = jnp.pad(whole, ((0, 0), (0, 0), (DEPTH, DEPTH), (0, 0)))
+        windows = jnp.stack(
+            [rows_of(long[:, :, pair_height * d : pair_height * d + pair_tall]) for d in range(pairs)]
+        )
+        pieces = jnp.where(col % 2 == 0, windows, windows[::-1])
+        direct_here = col % 2 == 0
+
+    pair_edges = join_core(edges, swap(edges, "row", 1), 3)
+    sides_of = jnp.where(even, edge_links[:, 0], edge_links[:, 2])
+    wanted = jnp.where(sides_of[:, 1] % 2 == 1, sides_of[:, 1] // 2 * faces + sides_of[:, 0], -1)
+    choose = (wanted[:, None] == jnp.arange(2 * faces)[None, :]).astype(BF)
+    given = dot(choose, pair_edges.reshape(2 * faces, DEPTH * pair_height * channels)).astype(BF)
+    given = given.reshape(faces * DEPTH * pair_height, channels)
+    fill = jnp.zeros((pieces.shape[1] - given.shape[0], channels), BF)
+    given_all = jnp.broadcast_to(jnp.concatenate([given, fill]), pieces.shape)
+    bands_out = jnp.where(is_end, pieces, given_all)
+
+    small = jnp.concatenate([projection_weight, down_weight], axis=1)
+    small = pack_cols(small) if small.shape[1] != channels else small
+    packed = jnp.concatenate([pack_cols(conv_weight), small], axis=0)
+    weight_rows = packed.shape[0]
+    weights_out = jnp.broadcast_to(packed, (pairs,) + packed.shape)
+    sent = jnp.concatenate([weights_out, bands_out], axis=1)
+    got = lax.all_to_all(sent, "row", 0, 0, axis_index_groups=same_core)
+
+    across_pairs = [(i, i + 1) for i in range(1, last, 2)] + [(i + 1, i) for i in range(1, last, 2)]
+    rim = jnp.where(even, features[:, :DEPTH], features[:, height - DEPTH :])
+    rim_got = lax.ppermute(rim, "row", across_pairs)
+    both = gather_pair(jnp.concatenate([features, rim_got], axis=1), "col", 2)
+    feat = both[:, :height]
+    outer = both[:, height:]
+    inner = swap(jnp.where(even, feat[:, height - DEPTH :], feat[:, :DEPTH]), "row", 1)
+    up = jnp.where(even, outer, inner)
+    below = jnp.where(even, inner, outer)
+    cot = gather_pair(cotangent, "col", 2)
+    own = jnp.where(row == 0, feat[:, :DEPTH], feat[:, ::-1][:, :DEPTH])
+    far = lax.ppermute(own, "row", [(0, last), (last, 0)])
+
+    mirrored = lax.ppermute(edges, "row", [(i, last - i) for i in range(rows)])
+    head = mirrored[:, :, :, :DEPTH]
+    foot = mirrored[:, :, :, height - DEPTH :]
+    mirror_inner = swap(jnp.where(even, head, foot), "row", 1)
+    mirror_outer = lax.ppermute(jnp.where(even, foot, head), "row", across_pairs)
     mirrored_tall = jnp.concatenate(
-        [from_below[cut:].reshape(small_shape), mirrored, from_above[cut:].reshape(small_shape)],
+        [
+            jnp.where(even, mirror_inner, mirror_outer),
+            mirrored,
+            jnp.where(even, mirror_outer, mirror_inner),
+        ],
         axis=3,
     )
 
     def side_columns(lines):
         return jnp.stack(
             [
-                jnp.stack([lines[:, :, lines.shape[2] - 1 - k] for k in range(DEPTH)], axis=1),
+                jnp.stack([lines[:, :, width - 1 - k] for k in range(DEPTH)], axis=1),
                 jnp.stack([lines[:, :, k] for k in range(DEPTH)], axis=1),
             ]
         )
 
     edges_tall = jnp.concatenate([side_columns(up), edges, side_columns(below)], axis=3)
 
-    own = jnp.where(row == 0, feat[:, :DEPTH], feat[:, ::-1][:, :DEPTH])
-    far = lax.ppermute(own, "row", [(0, last), (last, 0)])
-
-    long = jnp.pad(own, ((0, 0), (0, 0), (DEPTH, DEPTH), (0, 0)))
-    pieces = jnp.stack([rows_of(long[:, :, height * d : height * d + tall]) for d in range(rows)])
-    pieces = jnp.where(col % 2 == 1, pieces[::-1], pieces)
-
-    sides_of = edge_links[:, 0::2, :].transpose(1, 0, 2).reshape(2 * faces, 3)
-    wanted = jnp.where(sides_of[:, 1] % 2 == 1, sides_of[:, 1] // 2 * faces + sides_of[:, 0], -1)
-    choose = (wanted[:, None] == jnp.arange(2 * faces)[None, :]).astype(BF)
-
-    def give(columns):
-        flat = columns.reshape(2 * faces, DEPTH * height * channels)
-        return dot(choose, flat).astype(BF).reshape(2, faces * DEPTH * height, channels)
-
-    given = give(edges)
-    given_mirrored = give(mirrored)
-    fill = jnp.zeros((2, pieces.shape[1] - given.shape[1], channels), BF)
-    given_long = jnp.concatenate([given, fill], axis=1)
-    middle = jnp.zeros((rows - 2,) + given_long.shape[1:], BF)
-    columns_out = jnp.concatenate([given_long[:1], middle, given_long[1:]])
-    bands_out = jnp.where((row == 0) | (row == last), pieces, columns_out)
-
-    half_rows = packed.shape[0] // 2
-    weights_out = jnp.tile(packed.reshape(2, half_rows, channels), (rows // 2, 1, 1))
-    sent = jnp.concatenate([weights_out, bands_out], axis=1)
-    got = lax.all_to_all(sent, "row", 0, 0)
-
-    got_half = got[:, :half_rows]
-    other_half = swap(got_half, "row", 1)
-    even = row % 2 == 0
-    full = jnp.concatenate(
-        [jnp.where(even, got_half, other_half), jnp.where(even, other_half, got_half)], axis=1
-    )
-    conv_rows = packed.shape[0] - 2 * part_rows
-    wc = unpack_cols(full[:, :conv_rows], hid).reshape(rows * conv_weight.shape[0], hid)
-    pj_all = full[:, conv_rows : conv_rows + part_rows].reshape(rows * part_rows, channels)
-    pj = lax.dynamic_slice_in_dim(pj_all, col * hid, hid, 0)
-    dw = full[:, conv_rows + part_rows :].reshape(rows * part_rows, channels)
-
-    ends = jnp.stack([got[0, half_rows:], got[last, half_rows:]])
-    ends_other = swap(ends, "col", 1)
-    even_col = col % 2 == 0
-    ends_shape = (2, faces, DEPTH, tall, channels)
-    ends_direct = jnp.where(even_col, ends, ends_other).reshape(ends_shape)
-    ends_mirror = jnp.where(even_col, ends_other, ends).reshape(ends_shape)
+    conv_got = got[:, : weight_rows - small.shape[0]]
+    conv_all = join_core(conv_got[:, None], swap(conv_got, "row", 1)[:, None], 1)
+    wc = unpack_cols(conv_all, hid).reshape(rows * conv_weight.shape[0], hid)
+
+    small_got = got[:, weight_rows - small.shape[0] : weight_rows]
+    end = jnp.where(even, got[0, weight_rows:], got[pairs - 1, weight_rows:])
+    if cols == 2:
+        crossed = swap(jnp.concatenate([rows_of(small_got), end]), "col", 1)
+        small_other = crossed[: pairs * part_rows].reshape(small_got.shape)
+        end_other = crossed[pairs * part_rows :]
+        low = jnp.where(col == 0, small_got, small_other)
+        high = jnp.where(col == 0, small_other, small_got)
+        cut = channels // 2
+        pj_half = jnp.concatenate([low[..., :cut], high[..., :cut]], axis=-1)
+        dw_half = jnp.concatenate([low[..., cut:], high[..., cut:]], axis=-1)
+    else:
+        end_other = swap(end, "col", 1)
+        part = small_got.reshape(pairs, part_rows, 2 * projection_weight.shape[1])
+        part = lax.all_gather(part, "col")
+        part = part.transpose(1, 2, 0, 3)
+        cut = projection_weight.shape[1]
+        pj_half = part[..., :cut].reshape(pairs, part_rows, channels)
+        dw_half = part[..., cut:].reshape(pairs, part_rows, channels)
+    end_direct = jnp.where(direct_here, end, end_other)
+    end_mirror = jnp.where(direct_here, end_other, end)
+    bundle = jnp.concatenate([rows_of(pj_half), rows_of(dw_half), end_direct, end_mirror])
+    bundle_other = swap(bundle, "row", 1)
+    edge_of = pairs * part_rows
+
+    def both_cores(start):
+        return join_core(
+            bundle[start : start + edge_of].reshape(pairs, 1, part_rows, channels),
+            bundle_other[start : start + edge_of].reshape(pairs, 1, part_rows, channels),
+            1,
+        ).reshape(rows * part_rows, channels)
+
+    pj = lax.dynamic_slice_in_dim(both_cores(0), col * hid, hid, 0)
+    dw = both_cores(edge_of)
+    span = end.shape[0]
+
+    def ends_of(start, offset):
+        both_ends = join_core(
+            bundle[start : start + span][None], bundle_other[start : start + span][None], 0
+        ).reshape(2, faces, DEPTH, pair_tall, channels)
+        return jnp.where(
+            even, both_ends[:, :, :, offset : offset + tall],
+            both_ends[:, :, :, height - offset : height - offset + tall],
+        )
+
+    ends_direct = ends_of(2 * edge_of, 0)
+    ends_mirror = ends_of(2 * edge_of + span, height)
 
     def strips(ends_part, columns):
         return jnp.stack([ends_part[0], columns[0], ends_part[1], columns[1]])
@@ -349,15 +421,10 @@
         [strips(ends_direct, edges_tall), strips(ends_mirror, mirrored_tall)]
     ).astype(F32)
 
-    span = given.shape[1]
-    mine = jnp.where(row == 0, given[0], given[1])
-    theirs = jnp.where(row == 0, given_mirrored[0], given_mirrored[1])
-    first = jnp.where(row == 0, mine, theirs)
-    final = jnp.where(row == 0, theirs, mine)
-    sides = jnp.concatenate(
-        [first[None], got[1:last, half_rows : half_rows + span], final[None]]
-    )
-    sides = sides.reshape(rows, faces, DEPTH, height, channels).transpose(1, 2, 0, 3, 4)
+    sides = got[:, weight_rows : weight_rows + given.shape[0]]
+    here = jnp.arange(pairs)[:, None, None] == pair
+    sides = jnp.where(here, given[None], sides)
+    sides = sides.reshape(pairs, faces, DEPTH, pair_height, channels).transpose(1, 2, 0, 3, 4)
     sides = sides.reshape(faces, DEPTH, rows * height, channels)
 
     place = jnp.stack([row, col]).astype(jnp.int32)
@@ -366,15 +433,28 @@
         feat, up, below, near, own, far, sides, cot, wc, pj, dw, last,
     )
 
+    gc_parts = gc.reshape(pairs, 2, conv_weight.shape[0], hid)
+    pg_wide = jnp.zeros((rows, part_rows, channels), F32)
+    pg_wide = lax.dynamic_update_slice_in_dim(
+        pg_wide, pg.reshape(-1, part_rows, channels), col * (rows // cols), 0
+    )
+    pg_parts = pg_wide.reshape(pairs, 2, part_rows, channels)
+    gd_parts = gd.reshape(pairs, 2, part_rows, channels)
+
+    def mine_of(value):
+        return jnp.where(even, value[:, 0], value[:, 1])
+
+    def theirs_of(value):
+        return jnp.where(even, value[:, 1], value[:, 0])
+
+    def join_parts(pick):
+        return jnp.concatenate([pack_cols(pick(gc_parts)), pick(pg_parts), pick(gd_parts)], axis=1)
+
+    summed = (join_parts(mine_of) + swap(join_parts(theirs_of), "row", 1)).astype(BF)
+    shares = lax.all_to_all(summed, "row", 0, 0, axis_index_groups=same_core)
     block_out = scatter_sum_pair(out_part, "col", 2).astype(BF)
-    gc_out = pack_cols(gc.astype(BF).reshape(rows, conv_weight.shape[0], hid))
-    pg_wide = jnp.zeros((rows, part_rows, channels), BF)
-    pg_wide = lax.dynamic_update_slice_in_dim(
-        pg_wide, pg.astype(BF).reshape(-1, part_rows, channels), col * (rows // cols), 0
-    )
-    gd_out = gd.astype(BF).reshape(rows, part_rows, channels)
-    shares = lax.all_to_all(jnp.concatenate([gc_out, pg_wide, gd_out], axis=1), "row", 0, 0)
     total = jnp.sum(shares.astype(F32), axis=0)
+    conv_rows = total.shape[0] - 2 * part_rows
     grad_conv = unpack_cols(total[:conv_rows], hid)
     smaller = scatter_sum_pair(total[conv_rows:], "col", 1)
     return block_out, grad_conv, smaller[:part_rows], smaller[part_rows:]

time: 133 us -> 105 us (0.79); the launches traced: 131 us -> 105 us
  waiting for transfers between devices: 40.6 us -> 29.2 us
  starting transfers between devices: 39.3 us -> 32.6 us
  local copies, waits for them, and re-layouts: 18 us -> 11.4 us
  other arithmetic: 14.1 us -> 11.9 us
    all_to_all x2, waiting for transfers between devices: 27.4 us -> 5.23 us  [the longest x1 5.23 us: on_device(): shares = lax.all_to_all(summed, 'row', 0, 0, axis_index_groups=same_core)]
    ppermute x7 -> x12, waiting for transfers between devices: 12.7 us -> 24 us  [swap(): return lax.ppermute(value, axis, [(i, i ^ bit) for i in range(count)])]
    all_to_all x2, starting transfers between devices: 17 us -> 9.03 us  [the longest x1 5.48 us: on_device(): shares = lax.all_to_all(summed, 'row', 0, 0, axis_index_groups=same_core)]
    unnamed x44 -> x56, local copies, waits for them, and re-layouts: 8.94 us -> 3.27 us
    ppermute x3, starting transfers between devices: 8.52 us -> 4.65 us  [the longest x1 3.33 us: on_device(): mirrored = lax.ppermute(edges, 'row', [(i, last - i) for i in range(rows)])]
    select_n x5 -> x26, other arithmetic: 0.57 us -> 4.09 us  [the longest x1 1.36 us: theirs_of(): return jnp.where(even, value[:, 1], value[:, 0])]
    ppermute x1, starting transfers between devices: 2.95 us -> 6.02 us  [on_device(): far = lax.ppermute(own, 'row', [(0, last), (last, 0)])]
    concatenate x5 -> x12, other arithmetic: 3.65 us -> 0.65 us  [the longest x1 0.16 us: on_device(): jnp.concatenate([jnp.where(col == 0, none, seam_got), strip, jnp.where(co...]
  transfers between devices with their start and end apart: 13 -> 18, of which waited for: 8 -> 8; matrix products, arithmetic and copies ran while one was open for 22% -> 13% of each run, Pallas kernels for 0% -> 0%
where the time goes in v2:
time: 105 us
  starting transfers between devices  32.6 us (31%)
  waiting for transfers between devices  29.2 us (28%)
  Pallas kernels  17.9 us (17%)
  other arithmetic  11.9 us (11%)
  local copies, waits for them, and re-layouts  11.4 us (11%)
  between operations  1.77 us (2%)
    ppermute x12, waiting for transfers between devices, swap(): return lax.ppermute(value, axis, [(i, i ^ bit) for i in range(count)])  24 us
    pallas_call x1, Pallas kernels, run_block(): pl.pallas_call(functools.partial(block_kernel, group, last_row), grid=(fa...  17.9 us
    ppermute x12, starting transfers between devices, swap(): return lax.ppermute(value, axis, [(i, i ^ bit) for i in range(count)])  12.9 us
    ppermute x1, starting transfers between devices, on_device(): far = lax.ppermute(own, 'row', [(0, last), (last, 0)])  6.02 us
    all_to_all x1, starting transfers between devices, on_device(): shares = lax.all_to_all(summed, 'row', 0, 0, axis_index_groups=same_core)  5.48 us
    all_to_all x1, waiting for transfers between devices, on_device(): shares = lax.all_to_all(summed, 'row', 0, 0, axis_index_groups=same_core)  5.23 us
    all_to_all x1, starting transfers between devices, on_device(): got = lax.all_to_all(sent, 'row', 0, 0, axis_index_groups=same_core)  3.55 us
    ppermute x1, starting transfers between devices, on_device(): mirrored = lax.ppermute(edges, 'row', [(i, last - i) for i in range(rows)])  3.33 us
  transfers between devices with their start and end apart: 18, of which 8 were waited for; matrix products, arithmetic and copies ran while one was open for 13% of the time, Pallas kernels for 0%

profile of v2, /device:TPU:0, one launch (start us, length us, event | category | flops | bytes accessed | tf_op | source)
XLA Modules:
  0.0 104.9 jit_solution(12633310367124767145)
XLA Ops:
  0.7 1.0 slice.260
  1.7 1.1 %fusion.15 = (bf16[12,4,1,128]{3,2,1,0:T(2,128)(2,1)S(1)}, bf16[12,4,1,128]{3,2,1,0:T(2,128)(2,1)S(1)}, bf16[12,4,1,128]{3,2,1,0:T(2,128)(2,1)S(1)}, bf16[12,4,1,128]{3,2,1,0:T(2,128)(2,1)S(1)}) fusion(bf16[12,4,32,128]{3,2,1,0:T(8,128)(2,1)} %param.7), kind=kLoop, calls=%fused_computation.162 | loop fusion | bytes 98304 | tf_op jit(solution)/shard_map/slice | solution.py:273
  3.0 1.1 %reverse_select_fusion.1 = (bf16[12,2,32,128]{3,2,1,0:T(8,128)(2,1)S(1)}, bf16[12,2,32,128]{3,2,1,0:T(8,128)(2,1)S(1)}) fusion(bf16[12,2,32,128]{3,2,1,0:T(8,128)(2,1)S(1)} %slice.260, pred[]{:T(512)S(6)} %eq.66, bf16[12,4,32,128]{3,2,1,0:T(8,128)(2,1)} %param.7, pred[]{:T(512)S(6)} %eq.64), kind=kLoop, calls=%fused_computation.44 | loop fusion | flops 196608 | bytes 983042 | tf_op jit(solution)/shard_map/jit(_where)/select_n | solution.py:270
  4.2 3.0 %collective-permute-start.3 = (bf16[144,128]{1,0:T(8,128)(2,1)S(1)}, bf16[144,128]{1,0:T(8,128)(2,1)S(1)}, u32[]{:S(2)}, u32[]{:S(2)}) collective-permute-start(bf16[144,128]{1,0:T(8,128)(2,1)S(1)} %pad_maximum_fusion.20), channel_id=1, source_target_pairs={{0,1},{1,0},{2,3},{3,2},{4,5},{5,4},{6,7},{7,6},{8,9},{9,8},{10,11... | collective-permute-start | bytes 110600 | tf_op jit(solution)/shard_map/ppermute | solution.py:17
  7.3 0.7 collective-permute-start
  8.3 0.6 pad_add_fusion.where_ref
  8.9 0.1 copy.107
  9.0 0.7 reshape.384.edge
  9.8 0.7 reshape.385.corner
  10.6 3.2 %collective-permute-start.4 = (bf16[2,12,2,4,128]{4,3,2,1,0:T(4,128)(2,1)S(1)}, bf16[2,12,2,4,128]{4,3,2,1,0:T(4,128)(2,1)S(1)}, u32[]{:S(2)}, u32[]{:S(2)}) collective-permute-start(bf16[2,12,2,4,128]{4,3,2,1,0:T(4,128)(2,1)S(1)} %pad_maximum_fusion.19), channel_id=1, source_target_pairs={{0,2},{2,0},{4,6},{6,4},{8,10},{10,8},{12,14},{14,12},{16,18},{18,... | collective-permute-start | bytes 147464 | tf_op jit(solution)/shard_map/ppermute | solution.py:17
  13.8 3.3 %collective-permute-start.7 = (bf16[2,12,2,4,128]{4,3,2,1,0:T(4,128)(2,1)S(1)}, bf16[2,12,2,4,128]{4,3,2,1,0:T(4,128)(2,1)S(1)}, u32[]{:S(2)}, u32[]{:S(2)}) collective-permute-start(bf16[2,12,2,4,128]{4,3,2,1,0:T(4,128)(2,1)S(1)} %pad_maximum_fusion.19), channel_id=1, source_target_pairs={{0,30},{2,28},{4,26},{6,24},{8,22},{10,20},{12,18},{14,16},{16,14}... | collective-permute-start | bytes 147464 | tf_op jit(solution)/shard_map/ppermute | solution.py:341
  17.1 0.2 pad_maximum_fusion.10
  17.9 0.2 convolution_convert_fusion
  18.3 1.1 %pad_maximum_fusion = bf16[8,464,128]{2,1,0:T(8,128)(2,1)} fusion(bf16[8,288,128]{2,1,0:T(8,128)(2,1)S(1)} %select_select_fusion, bf16[8,176,128]{2,1,0:T(8,128)(2,1)S(1)} %broadcast_in_dim.20), kind=kLoop, calls=%fused_computation.7 | loop fusion | flops 1900544 | bytes 1900544 | tf_op jit(solution)/shard_map/concatenate | solution.py:325
  19.4 3.6 %all-to-all-start = ((bf16[8,464,128]{2,1,0:T(8,128)(2,1)}), bf16[8,464,128]{2,1,0:T(8,128)(2,1)S(1)}, u32[]{:S(2)}, u32[]{:S(2)}) async-start(bf16[8,464,128]{2,1,0:T(8,128)(2,1)} %pad_maximum_fusion), calls=%async_computation | async-start | bytes 1900544 | tf_op jit(solution)/shard_map/all_to_all | solution.py:326
  23.0 1.6 %collective-permute-start.1 = (bf16[12,6,32,128]{3,2,1,0:T(8,128)(2,1)S(1)}, bf16[12,6,32,128]{3,2,1,0:T(8,128)(2,1)S(1)}, u32[]{:S(2)}, u32[]{:S(2)}) collective-permute-start(bf16[12,6,32,128]{3,2,1,0:T(8,128)(2,1)S(1)} %constant_dynamic-update-slice_fusion), channel_id=1, source_target_pairs={{0,1},{1,0},{2,3},{3,2},{4,5},{5,4},{6,7},{7,6},{8,9},{9,8},{10,11... | collective-permute-start | bytes 1769480 | tf_op jit(solution)/shard_map/ppermute | solution.py:17
  24.7 0.7 collective-permute-start.9
  25.4 0.7 pad_maximum_fusion.6.cot
  26.1 12.2 %collective-permute-done.1 = bf16[12,6,32,128]{3,2,1,0:T(8,128)(2,1)S(1)} collective-permute-done((bf16[12,6,32,128]{3,2,1,0:T(8,128)(2,1)S(1)}, bf16[12,6,32,128]{3,2,1,0:T(8,128)(2,1)S(1)}, u32[]{:S(2)}, u32[]{:S(2)}) %collective-permute-start.1) | collective-permute-done | bytes 589856 | tf_op jit(solution)/shard_map/ppermute | solution.py:17
  38.4 0.2 broadcast_select_fusion.4
  38.8 1.0 fusion.1.feat
  39.8 0.6 collective-permute-done.2
  40.4 0.3 broadcast_select_fusion.2
  41.0 6.0 %collective-permute-start.10 = (bf16[12,2,64,128]{3,2,1,0:T(8,128)(2,1)S(1)}, bf16[12,2,64,128]{3,2,1,0:T(8,128)(2,1)S(1)}, u32[]{:S(2)}, u32[]{:S(2)}) collective-permute-start(bf16[12,2,64,128]{3,2,1,0:T(8,128)(2,1)S(1)} %get-tuple-element.18.own), channel_id=1, source_target_pairs={{0,30},{30,0},{1,31},{31,1}} | collective-permute-start | bytes 1179656 | tf_op jit(solution)/shard_map/ppermute | solution.py:339
  47.4 1.6 %collective-permute-start.5 = (bf16[544,128]{1,0:T(8,128)(2,1)S(1)}, bf16[544,128]{1,0:T(8,128)(2,1)S(1)}, u32[]{:S(2)}, u32[]{:S(2)}) collective-permute-start(bf16[544,128]{1,0:T(8,128)(2,1)S(1)} %pad_maximum_fusion.7), channel_id=1, source_target_pairs={{0,1},{1,0},{2,3},{3,2},{4,5},{5,4},{6,7},{7,6},{8,9},{9,8},{10,11... | collective-permute-start | bytes 417800 | tf_op jit(solution)/shard_map/ppermute | solution.py:17
  49.1 0.9 copy.177
  50.0 2.5 %collective-permute-done.5 = bf16[544,128]{1,0:T(8,128)(2,1)S(1)} collective-permute-done((bf16[544,128]{1,0:T(8,128)(2,1)S(1)}, bf16[544,128]{1,0:T(8,128)(2,1)S(1)}, u32[]{:S(2)}, u32[]{:S(2)}) %collective-permute-start.5) | collective-permute-done | bytes 139296 | tf_op jit(solution)/shard_map/ppermute | solution.py:17
  53.2 0.9 copy.125
  54.1 0.5 collective-permute-done.6
  55.2 0.6 constant_dynamic-slice_fusion.pj
  55.9 0.7 copy.127
  56.6 1.0 maximum_convert_fusion.near
  57.6 0.7 copy-done.14
  58.3 17.9 %shard_map.102 = (f32[12,2,32,128]{3,2,1,0:T(8,128)}, f32[1152,256]{1,0:T(8,128)}, f32[256,128]{1,0:T(8,128)}, f32[512,128]{1,0:T(8,128)}) custom-call(s32[144]{0:T(256)} %reshape.384.edge, s32[144]{0:T(256)} %reshape.385.corner, s32[2]{0:T(128)} %pad_add_fusion.where_ref, bf16[12,4,64,128]{3,2,1,0:T(8,128)(2,1)} %fusion.1.feat, ...), custom_call_target="tpu_custom_call" | custom-call | flops 4227858432 | bytes 12582912 | tf_op jit(solution)/shard_map/pallas_call | solution.py:214
  76.2 1.4 %select_bitcast_fusion = f32[8,72,256]{2,1,0:T(8,128)S(1)} fusion(f32[8,2,72,256]{3,2,1,0:T(8,128)} %bitcast.170, pred[]{:T(512)S(6)} %eq.64), kind=kLoop, calls=%fused_computation.19 | loop fusion | flops 147456 | bytes 1769473 | tf_op jit(solution)/shard_map/jit(_where)/select_n | solution.py:448
  77.7 0.8 copy-done.6
  78.7 1.1 %copy-done = f32[1152,256]{1,0:T(8,128)S(1)} copy-done((f32[1152,256]{1,0:T(8,128)S(1)}, f32[1152,256]{1,0:T(8,128)}, u32[]{:S(2)}) %copy-start) | copy-done | bytes 1179672
  79.9 1.2 %collective-permute-done.14 = f32[8,208,128]{2,1,0:T(8,128)S(1)} collective-permute-done((f32[8,208,128]{2,1,0:T(8,128)S(1)}, f32[8,208,128]{2,1,0:T(8,128)S(1)}, u32[]{:S(2)}, u32[]{:S(2)}) %collective-permute-start.14) | collective-permute-done | bytes 852000 | tf_op jit(solution)/shard_map/ppermute | solution.py:17
  81.1 0.9 fusion
  81.9 5.5 %all-to-all-start.1 = ((bf16[8,208,128]{2,1,0:T(8,128)(2,1)}), bf16[8,208,128]{2,1,0:T(8,128)(2,1)S(1)}, u32[]{:S(2)}, u32[]{:S(2)}) async-start(bf16[8,208,128]{2,1,0:T(8,128)(2,1)} %fusion), calls=%async_computation.1 | async-start | bytes 851968 | tf_op jit(solution)/shard_map/all_to_all | solution.py:454
  87.4 1.6 %collective-permute-start.13 = (f32[12,2,16,128]{3,2,1,0:T(8,128)S(1)}, f32[12,2,16,128]{3,2,1,0:T(8,128)S(1)}, u32[]{:S(2)}, u32[]{:S(2)}) collective-permute-start(f32[12,2,16,128]{3,2,1,0:T(8,128)S(1)} %slice_select_fusion.1), channel_id=1, source_target_pairs={{0,1},{1,0},{2,3},{3,2},{4,5},{5,4},{6,7},{7,6},{8,9},{9,8},{10,11... | collective-permute-start | bytes 589832 | tf_op jit(solution)/shard_map/ppermute | solution.py:17
  89.0 5.2 %collective-permute-done.13 = f32[12,2,16,128]{3,2,1,0:T(8,128)S(1)} collective-permute-done((f32[12,2,16,128]{3,2,1,0:T(8,128)S(1)}, f32[12,2,16,128]{3,2,1,0:T(8,128)S(1)}, u32[]{:S(2)}, u32[]{:S(2)}) %collective-permute-start.13) | collective-permute-done | bytes 196640 | tf_op jit(solution)/shard_map/ppermute | solution.py:17
  94.2 0.7 add_convert_fusion
  94.8 5.2 %all-to-all-done.1 = bf16[8,208,128]{2,1,0:T(8,128)(2,1)S(1)} async-done(((bf16[8,208,128]{2,1,0:T(8,128)(2,1)}), bf16[8,208,128]{2,1,0:T(8,128)(2,1)S(1)}, u32[]{:S(2)}, u32[]{:S(2)}) %all-to-all-start.1) | async-done | bytes 426016 | tf_op jit(solution)/shard_map/all_to_all | solution.py:454
  100.2 1.6 %collective-permute-start.15 = (f32[64,64]{1,0:T(8,128)S(1)}, f32[64,64]{1,0:T(8,128)S(1)}, u32[]{:S(2)}, u32[]{:S(2)}) collective-permute-start(f32[64,64]{1,0:T(8,128)S(1)} %slice_select_fusion.5), channel_id=1, source_target_pairs={{0,1},{1,0},{2,3},{3,2},{4,5},{5,4},{6,7},{7,6},{8,9},{9,8},{10,11... | collective-permute-start | bytes 49160 | tf_op jit(solution)/shard_map/ppermute | solution.py:17
  101.8 0.6 pad_maximum_fusion.14
  102.4 1.8 %collective-permute-done.15 = f32[64,64]{1,0:T(8,128)S(1)} collective-permute-done((f32[64,64]{1,0:T(8,128)S(1)}, f32[64,64]{1,0:T(8,128)S(1)}, u32[]{:S(2)}, u32[]{:S(2)}) %collective-permute-start.15) | collective-permute-done | bytes 16416 | tf_op jit(solution)/shard_map/ppermute | solution.py:17
  104.3 0.6 fusion.23
  (156 shorter events, 4.2 us)
Async XLA Ops:
  0.6 7.4 %copy-start.1 = (bf16[12,4,32,128]{3,2,1,0:T(8,128)(2,1)S(1)}, bf16[12,4,32,128]{3,2,1,0:T(8,128)(2,1)}, u32[]{:S(2)}) copy-start(bf16[12,4,32,128]{3,2,1,0:T(8,128)(2,1)} %param.7) | copy-start | bytes 1179652
  0.6 7.3 %copy-start.8 = (bf16[12,2,16,128]{3,2,1,0:T(8,128)(2,1)S(1)}, bf16[12,2,16,128]{3,2,1,0:T(8,128)(2,1)}, u32[]{:S(2)}) copy-start(bf16[12,2,16,128]{3,2,1,0:T(8,128)(2,1)} %param.8) | copy-start | bytes 294916
  1.7 6.4 %copy-start.10 = (s32[12,4,3]{0,1,2:T(4,128)S(1)}, s32[12,4,3]{0,1,2:T(4,128)}, u32[]{:S(2)}) copy-start(s32[12,4,3]{0,1,2:T(4,128)} %param.12) | copy-start | bytes 1732
  1.7 6.4 %copy-start.9 = (bf16[72,256]{1,0:T(8,128)(2,1)S(1)}, bf16[72,256]{1,0:T(8,128)(2,1)}, u32[]{:S(2)}) copy-start(bf16[72,256]{1,0:T(8,128)(2,1)} %param.9) | copy-start | bytes 110596
  2.9 5.3 %copy-start.11 = (bf16[32,64]{1,0:T(8,128)(2,1)S(1)}, bf16[32,64]{1,0:T(8,128)(2,1)}, u32[]{:S(2)}) copy-start(bf16[32,64]{1,0:T(8,128)(2,1)} %param.11) | copy-start | bytes 12292
  2.9 5.3 %copy-start.12 = (bf16[32,64]{1,0:T(8,128)(2,1)S(1)}, bf16[32,64]{1,0:T(8,128)(2,1)}, u32[]{:S(2)}) copy-start(bf16[32,64]{1,0:T(8,128)(2,1)} %param.10) | copy-start | bytes 12292
  2.9 6.7 %copy-start.13 = (s32[12,4,3]{0,1,2:T(4,128)S(1)}, s32[12,4,3]{0,1,2:T(4,128)}, u32[]{:S(2)}) copy-start(s32[12,4,3]{0,1,2:T(4,128)} %param.13) | copy-start | bytes 1732
  4.2 6.3 %collective-permute-start.3 = (bf16[144,128]{1,0:T(8,128)(2,1)S(1)}, bf16[144,128]{1,0:T(8,128)(2,1)S(1)}, u32[]{:S(2)}, u32[]{:S(2)}) collective-permute-start(bf16[144,128]{1,0:T(8,128)(2,1)S(1)} %pad_maximum_fusion.20), channel_id=1, source_target_pairs={{0,1},{1,0},{2,3},{3,2},{4,5},{5,4},{6,7},{7,6},{8,9},{9,8},{10,11... | collective-permute-start | bytes 110600 | tf_op jit(solution)/shard_map/ppermute | solution.py:17
  7.3 15.7 %collective-permute-start = (bf16[12,2,32,128]{3,2,1,0:T(8,128)(2,1)S(1)}, bf16[12,2,32,128]{3,2,1,0:T(8,128)(2,1)S(1)}, u32[]{:S(2)}, u32[]{:S(2)}) collective-permute-start(bf16[12,2,32,128]{3,2,1,0:T(8,128)(2,1)S(1)} %get-tuple-element.40), channel_id=1, source_target_pairs={{2,4},{6,8},{10,12},{14,16},{18,20},{22,24},{26,28},{4,2},{8,6},{1... | collective-permute-start | bytes 589832 | tf_op jit(solution)/shard_map/ppermute | solution.py:330
  7.9 17.4 %collective-permute-start.11 = (bf16[12,2,16,128]{3,2,1,0:T(8,128)(2,1)S(1)}, bf16[12,2,16,128]{3,2,1,0:T(8,128)(2,1)S(1)}, u32[]{:S(2)}, u32[]{:S(2)}) collective-permute-start(bf16[12,2,16,128]{3,2,1,0:T(8,128)(2,1)S(1)} %copy-done.8), channel_id=1, source_target_pairs={{0,1},{1,0},{2,3},{3,2},{4,5},{5,4},{6,7},{7,6},{8,9},{9,8},{10,11... | collective-permute-start | bytes 294920 | tf_op jit(solution)/shard_map/ppermute | solution.py:17
  10.6 7.1 %collective-permute-start.4 = (bf16[2,12,2,4,128]{4,3,2,1,0:T(4,128)(2,1)S(1)}, bf16[2,12,2,4,128]{4,3,2,1,0:T(4,128)(2,1)S(1)}, u32[]{:S(2)}, u32[]{:S(2)}) collective-permute-start(bf16[2,12,2,4,128]{4,3,2,1,0:T(4,128)(2,1)S(1)} %pad_maximum_fusion.19), channel_id=1, source_target_pairs={{0,2},{2,0},{4,6},{6,4},{8,10},{10,8},{12,14},{14,12},{16,18},{18,... | collective-permute-start | bytes 147464 | tf_op jit(solution)/shard_map/ppermute | solution.py:17
  13.8 10.8 %collective-permute-start.7 = (bf16[2,12,2,4,128]{4,3,2,1,0:T(4,128)(2,1)S(1)}, bf16[2,12,2,4,128]{4,3,2,1,0:T(4,128)(2,1)S(1)}, u32[]{:S(2)}, u32[]{:S(2)}) collective-permute-start(bf16[2,12,2,4,128]{4,3,2,1,0:T(4,128)(2,1)S(1)} %pad_maximum_fusion.19), channel_id=1, source_target_pairs={{0,30},{2,28},{4,26},{6,24},{8,22},{10,20},{12,18},{14,16},{16,14}... | collective-permute-start | bytes 147464 | tf_op jit(solution)/shard_map/ppermute | solution.py:341
  19.4 27.9 %all-to-all-start = ((bf16[8,464,128]{2,1,0:T(8,128)(2,1)}), bf16[8,464,128]{2,1,0:T(8,128)(2,1)S(1)}, u32[]{:S(2)}, u32[]{:S(2)}) async-start(bf16[8,464,128]{2,1,0:T(8,128)(2,1)} %pad_maximum_fusion), calls=%async_computation | async-start | bytes 1900544 | tf_op jit(solution)/shard_map/all_to_all | solution.py:326
  23.0 15.4 %collective-permute-start.1 = (bf16[12,6,32,128]{3,2,1,0:T(8,128)(2,1)S(1)}, bf16[12,6,32,128]{3,2,1,0:T(8,128)(2,1)S(1)}, u32[]{:S(2)}, u32[]{:S(2)}) collective-permute-start(bf16[12,6,32,128]{3,2,1,0:T(8,128)(2,1)S(1)} %constant_dynamic-update-slice_fusion), channel_id=1, source_target_pairs={{0,1},{1,0},{2,3},{3,2},{4,5},{5,4},{6,7},{7,6},{8,9},{9,8},{10,11... | collective-permute-start | bytes 1769480 | tf_op jit(solution)/shard_map/ppermute | solution.py:17
  24.6 1.5 %collective-permute-start.8 = (bf16[2,12,2,2,128]{4,3,2,1,0:T(2,128)(2,1)S(1)}, bf16[2,12,2,2,128]{4,3,2,1,0:T(2,128)(2,1)S(1)}, u32[]{:S(2)}, u32[]{:S(2)}) collective-permute-start(bf16[2,12,2,2,128]{4,3,2,1,0:T(2,128)(2,1)S(1)} %get-tuple-element.91), channel_id=1, source_target_pairs={{0,2},{2,0},{4,6},{6,4},{8,10},{10,8},{12,14},{14,12},{16,18},{18,... | collective-permute-start | bytes 73736 | tf_op jit(solution)/shard_map/ppermute | solution.py:17
  24.7 1.4 %collective-permute-start.9 = (bf16[2,12,2,2,128]{4,3,2,1,0:T(2,128)(2,1)S(1)}, bf16[2,12,2,2,128]{4,3,2,1,0:T(2,128)(2,1)S(1)}, u32[]{:S(2)}, u32[]{:S(2)}) collective-permute-start(bf16[2,12,2,2,128]{4,3,2,1,0:T(2,128)(2,1)S(1)} %get-tuple-element.92), channel_id=1, source_target_pairs={{2,4},{6,8},{10,12},{14,16},{18,20},{22,24},{26,28},{4,2},{8,6},{1... | collective-permute-start | bytes 73736 | tf_op jit(solution)/shard_map/ppermute | solution.py:345
  38.6 1.8 %collective-permute-start.2 = (bf16[12,2,64,128]{3,2,1,0:T(8,128)(2,1)S(1)}, bf16[12,2,64,128]{3,2,1,0:T(8,128)(2,1)S(1)}, u32[]{:S(2)}, u32[]{:S(2)}) collective-permute-start(bf16[12,2,64,128]{3,2,1,0:T(8,128)(2,1)S(1)} %get-tuple-element.12), channel_id=1, source_target_pairs={{0,2},{2,0},{4,6},{6,4},{8,10},{10,8},{12,14},{14,12},{16,18},{18,... | collective-permute-start | bytes 1179656 | tf_op jit(solution)/shard_map/ppermute | solution.py:17
  40.8 8.3 %copy-start.3 = (bf16[12,2,64,128]{3,2,1,0:T(8,128)(2,1)}, bf16[12,2,64,128]{3,2,1,0:T(8,128)(2,1)S(1)}, u32[]{:S(2)}) copy-start(bf16[12,2,64,128]{3,2,1,0:T(8,128)(2,1)S(1)} %get-tuple-element.14.down_rows) | copy-start | bytes 1179652
  40.8 8.3 %copy-start.4 = (bf16[12,2,64,128]{3,2,1,0:T(8,128)(2,1)}, bf16[12,2,64,128]{3,2,1,0:T(8,128)(2,1)S(1)}, u32[]{:S(2)}) copy-start(bf16[12,2,64,128]{3,2,1,0:T(8,128)(2,1)S(1)} %get-tuple-element.15.up) | copy-start | bytes 1179652
  40.8 8.3 %copy-start.5 = (bf16[12,2,64,128]{3,2,1,0:T(8,128)(2,1)}, bf16[12,2,64,128]{3,2,1,0:T(8,128)(2,1)S(1)}, u32[]{:S(2)}) copy-start(bf16[12,2,64,128]{3,2,1,0:T(8,128)(2,1)S(1)} %get-tuple-element.18.own) | copy-start | bytes 1179652
  41.0 16.5 %collective-permute-start.10 = (bf16[12,2,64,128]{3,2,1,0:T(8,128)(2,1)S(1)}, bf16[12,2,64,128]{3,2,1,0:T(8,128)(2,1)S(1)}, u32[]{:S(2)}, u32[]{:S(2)}) collective-permute-start(bf16[12,2,64,128]{3,2,1,0:T(8,128)(2,1)S(1)} %get-tuple-element.18.own), channel_id=1, source_target_pairs={{0,30},{30,0},{1,31},{31,1}} | collective-permute-start | bytes 1179656 | tf_op jit(solution)/shard_map/ppermute | solution.py:339
  47.4 5.1 %collective-permute-start.5 = (bf16[544,128]{1,0:T(8,128)(2,1)S(1)}, bf16[544,128]{1,0:T(8,128)(2,1)S(1)}, u32[]{:S(2)}, u32[]{:S(2)}) collective-permute-start(bf16[544,128]{1,0:T(8,128)(2,1)S(1)} %pad_maximum_fusion.7), channel_id=1, source_target_pairs={{0,1},{1,0},{2,3},{3,2},{4,5},{5,4},{6,7},{7,6},{8,9},{9,8},{10,11... | collective-permute-start | bytes 417800 | tf_op jit(solution)/shard_map/ppermute | solution.py:17
  48.9 4.1 %collective-permute-start.12 = (bf16[8,144,128]{2,1,0:T(8,128)(2,1)S(1)}, bf16[8,144,128]{2,1,0:T(8,128)(2,1)S(1)}, u32[]{:S(2)}, u32[]{:S(2)}) collective-permute-start(bf16[8,144,128]{2,1,0:T(8,128)(2,1)S(1)} %slice.384), channel_id=1, source_target_pairs={{0,2},{2,0},{4,6},{6,4},{8,10},{10,8},{12,14},{14,12},{16,18},{18,... | collective-permute-start | bytes 884744 | tf_op jit(solution)/shard_map/ppermute | solution.py:17
  52.9 1.6 %collective-permute-start.6 = (bf16[1088,128]{1,0:T(8,128)(2,1)S(1)}, bf16[1088,128]{1,0:T(8,128)(2,1)S(1)}, u32[]{:S(2)}, u32[]{:S(2)}) collective-permute-start(bf16[1088,128]{1,0:T(8,128)(2,1)S(1)} %pad_maximum_fusion.5), channel_id=1, source_target_pairs={{0,2},{2,0},{4,6},{6,4},{8,10},{10,8},{12,14},{14,12},{16,18},{18,... | collective-permute-start | bytes 835592 | tf_op jit(solution)/shard_map/ppermute | solution.py:17
  57.6 0.7 copy-start.14
  76.2 1.5 %copy-start.7 = (f32[256,128]{1,0:T(8,128)S(1)}, f32[256,128]{1,0:T(8,128)}, u32[]{:S(2)}) copy-start(f32[256,128]{1,0:T(8,128)} %get-tuple-element.10) | copy-start | bytes 393220
  77.5 1.0 copy-start.6
  78.5 1.3 %copy-start = (f32[1152,256]{1,0:T(8,128)S(1)}, f32[1152,256]{1,0:T(8,128)}, u32[]{:S(2)}) copy-start(f32[1152,256]{1,0:T(8,128)} %get-tuple-element.9) | copy-start | bytes 3538948
  78.6 2.4 %collective-permute-start.14 = (f32[8,208,128]{2,1,0:T(8,128)S(1)}, f32[8,208,128]{2,1,0:T(8,128)S(1)}, u32[]{:S(2)}, u32[]{:S(2)}) collective-permute-start(f32[8,208,128]{2,1,0:T(8,128)S(1)} %pad_maximum_fusion.1), channel_id=1, source_target_pairs={{0,2},{2,0},{4,6},{6,4},{8,10},{10,8},{12,14},{14,12},{16,18},{18,... | collective-permute-start | bytes 2555912 | tf_op jit(solution)/shard_map/ppermute | solution.py:17
  81.0 6.3 %copy-start.2 = (f32[12,2,32,128]{3,2,1,0:T(8,128)S(1)}, f32[12,2,32,128]{3,2,1,0:T(8,128)}, u32[]{:S(2)}) copy-start(f32[12,2,32,128]{3,2,1,0:T(8,128)} %get-tuple-element.8) | copy-start | bytes 1179652
  81.9 18.2 %all-to-all-start.1 = ((bf16[8,208,128]{2,1,0:T(8,128)(2,1)}), bf16[8,208,128]{2,1,0:T(8,128)(2,1)S(1)}, u32[]{:S(2)}, u32[]{:S(2)}) async-start(bf16[8,208,128]{2,1,0:T(8,128)(2,1)} %fusion), calls=%async_computation.1 | async-start | bytes 851968 | tf_op jit(solution)/shard_map/all_to_all | solution.py:454
  87.4 6.7 %collective-permute-start.13 = (f32[12,2,16,128]{3,2,1,0:T(8,128)S(1)}, f32[12,2,16,128]{3,2,1,0:T(8,128)S(1)}, u32[]{:S(2)}, u32[]{:S(2)}) collective-permute-start(f32[12,2,16,128]{3,2,1,0:T(8,128)S(1)} %slice_select_fusion.1), channel_id=1, source_target_pairs={{0,1},{1,0},{2,3},{3,2},{4,5},{5,4},{6,7},{7,6},{8,9},{9,8},{10,11... | collective-permute-start | bytes 589832 | tf_op jit(solution)/shard_map/ppermute | solution.py:17
  100.2 4.0 %collective-permute-start.15 = (f32[64,64]{1,0:T(8,128)S(1)}, f32[64,64]{1,0:T(8,128)S(1)}, u32[]{:S(2)}, u32[]{:S(2)}) collective-permute-start(f32[64,64]{1,0:T(8,128)S(1)} %slice_select_fusion.5), channel_id=1, source_target_pairs={{0,1},{1,0},{2,3},{3,2},{4,5},{5,4},{6,7},{7,6},{8,9},{9,8},{10,11... | collective-permute-start | bytes 49160 | tf_op jit(solution)/shard_map/ppermute | solution.py:17

commit v3 on v2

--- a/solution.py
+++ b/solution.py
@@ -61,16 +61,16 @@
 
 def block_kernel(
     group, last_row, edge, corner, where_ref,
-    feat, up, down_rows, near, own, far, sides, cot, wc, pj, dw,
+    feat, up, down_rows, near, own, far, sides, cot, wc, pj_all, dw,
     out_ref, gc_ref, pg_ref, gd_ref,
-    pad, shifted, resid_scr,
+    shifted, resid_scr,
 ):
     step = pl.program_id(0)
     row = where_ref[0]
     col = where_ref[1]
     height, width = feat.shape[1], feat.shape[2]
     tall = height + 2 * DEPTH
-    base = 8
+    hid = wc.shape[1]
 
     @pl.when(step == 0)
     def _():
@@ -78,76 +78,84 @@
         pg_ref[...] = jnp.zeros_like(pg_ref)
         gd_ref[...] = jnp.zeros_like(gd_ref)
 
-    line = lax.broadcasted_iota(jnp.int32, (width, width), 0)
-    across = lax.broadcasted_iota(jnp.int32, (width, width), 1)
-    flip = (line + across == width - 1).astype(BF)
+    def link(face, side, what):
+        return edge[face * 12 + side * 3 + what]
 
     for j in range(group):
         face = step * group + j
-        pad[DEPTH : DEPTH + height, base : base + width, :] = feat[j].astype(F32)
-        pad[:DEPTH, base : base + width, :] = up[j].astype(F32)
-        pad[DEPTH + height :, base : base + width, :] = down_rows[j].astype(F32)
-
-        def link(side, what):
-            return edge[face * 12 + side * 3 + what]
-
-        for side, column in ((3, lambda k: base - 1 - k), (1, lambda k: base + width + k)):
-            g, t, rev = link(side, 0), link(side, 1), link(side, 2)
+
+        def column(side, k, i):
+            g, t, rev = link(face, side, 0), link(face, side, 1), link(face, side, 2)
+            return near[rev, t, g, k, pl.ds(jnp.where(rev == 1, tall - 1 - i, i), 1), :]
+
+        for i in range(tall):
+            if i < DEPTH:
+                line = up[j, i]
+            elif i < DEPTH + height:
+                line = feat[j, i - DEPTH]
+            else:
+                line = down_rows[j, i - DEPTH - height]
+            left = jnp.concatenate([column(3, k, i) for k in reversed(range(DEPTH))], axis=0)
+            right = jnp.concatenate([column(1, k, i) for k in range(DEPTH)], axis=0)
+            shifted[0, j, i] = jnp.concatenate([left.astype(BF), line[: width - DEPTH]], axis=0)
+            shifted[1, j, i] = line
+            shifted[2, j, i] = jnp.concatenate([line[DEPTH:], right.astype(BF)], axis=0)
+
+    out_line = lax.broadcasted_iota(jnp.int32, (3 * width, width), 0)
+    source = lax.broadcasted_iota(jnp.int32, (3 * width, width), 1)
+    place = out_line % width + DEPTH * (out_line // width - 1)
+
+    def frame(side, ends, line_of, mine):
+        for j in range(group):
+            face = step * group + j
+            g, t, rev = link(face, side, 0), link(face, side, 1), link(face, side, 2)
+            picked = jnp.concatenate(
+                [
+                    jnp.where(
+                        t == mine, own[g, k].astype(F32),
+                        jnp.where(t == 2 - mine, far[g, k].astype(F32), sides[face, k].astype(F32)),
+                    ).astype(BF)
+                    for k in range(DEPTH)
+                ],
+                axis=1,
+            )
+            move = (jnp.where(rev == 1, width - 1 - place, place) == source).astype(F32).astype(BF)
+            turned = dot(move, picked).astype(BF)
             for k in range(DEPTH):
-                for i in range(tall):
-                    pick = jnp.where(rev == 1, tall - 1 - i, i)
-                    pad[i, column(k) : column(k) + 1, :] = near[rev, t, g, k, pl.ds(pick, 1), :]
-
-        def frame(side, corners, line_of, mine):
-            g, t, rev = link(side, 0), link(side, 1), link(side, 2)
-            for k in range(DEPTH):
-                picked = jnp.where(
-                    t == mine, own[g, k].astype(F32),
-                    jnp.where(t == 2 - mine, far[g, k].astype(F32), sides[face, k].astype(F32)),
-                ).astype(BF)
-                turned = dot(flip, picked)
-                pad[line_of(k), base : base + width, :] = jnp.where(
-                    rev == 1, turned, picked.astype(F32)
-                )
-            for e, column in corners:
+                for tap in range(3):
+                    shifted[tap, j, line_of(k)] = turned[
+                        tap * width : (tap + 1) * width, 128 * k : 128 * (k + 1)
+                    ]
+            for e, tap in zip(ends, (0, 2)):
                 cg = corner[face * 12 + e * 3]
                 ce = corner[face * 12 + e * 3 + 1]
                 cw = corner[face * 12 + e * 3 + 2]
                 upper = ce < 2
-                t = jnp.where((ce == 0) | (ce == 3), 3, 1)
+                side_of = jnp.where((ce == 0) | (ce == 3), 3, 1)
                 away = jnp.where(upper == (mine == 0), 0, 1)
+
+                def beyond(a, b):
+                    u = jnp.where(cw == 1, b, a)
+                    v = jnp.where(cw == 1, a, b)
+                    i = jnp.where(upper, DEPTH + u, tall - 1 - DEPTH - u)
+                    value = near[away, side_of, jnp.maximum(cg, 0), v, pl.ds(i, 1), :]
+                    return jnp.where(cg >= 0, value, jnp.zeros_like(value))
+
+                at = 0 if tap == 0 else width - DEPTH
                 for a in range(DEPTH):
-                    for b in range(DEPTH):
-                        u = jnp.where(cw == 1, b, a)
-                        v = jnp.where(cw == 1, a, b)
-                        i = jnp.where(upper, DEPTH + u, tall - 1 - DEPTH - u)
-                        value = near[away, t, jnp.maximum(cg, 0), v, pl.ds(i, 1), :]
-                        pad[line_of(a), column(b) : column(b) + 1, :] = jnp.where(
-                            cg >= 0, value, jnp.zeros_like(value)
-                        )
-
-        @pl.when(row == 0)
-        def _():
-            frame(
-                0,
-                ((0, lambda b: base - 1 - b), (1, lambda b: base + width + b)),
-                lambda k: DEPTH - 1 - k,
-                0,
-            )
-
-        @pl.when(row == last_row)
-        def _():
-            frame(
-                2,
-                ((3, lambda b: base - 1 - b), (2, lambda b: base + width + b)),
-                lambda k: DEPTH + height + k,
-                2,
-            )
-
-        for tap in range(3):
-            at = base - DEPTH + tap * DEPTH
-            shifted[tap, j] = pad[:, at : at + width, :].astype(BF)
-
+                    order = reversed(range(DEPTH)) if tap == 0 else range(DEPTH)
+                    pixels_beyond = jnp.concatenate([beyond(a, b) for b in order], axis=0)
+                    shifted[tap, j, line_of(a), at : at + DEPTH, :] = pixels_beyond.astype(BF)
+
+    @pl.when(row == 0)
+    def _():
+        frame(0, (0, 1), lambda k: DEPTH - 1 - k, 0)
+
+    @pl.when(row == last_row)
+    def _():
+        frame(2, (3, 2), lambda k: DEPTH + height + k, 2)
+
+    pj = pj_all[pl.ds(pl.multiple_of(col * hid, hid), hid), :]
     pixels = group * height * width
     wide = jnp.concatenate(
         [
@@ -161,7 +169,7 @@
     hidden = (pre * half).astype(BF)
     slope = half + pre * jnp.exp(-0.5 * pre * pre) * 0.3989422804014327
 
-    part = dot(hidden, pj[...])
+    part = dot(hidden, pj)
     part = part + jnp.where(col == 0, feat[...].reshape(pixels, 128).astype(F32), 0.0)
     quarter = pixels // 4
     blocks = (group * height // 2, width // 2, 128)
@@ -187,14 +195,14 @@
             resid_scr[:, ro, pl.ds(co, width // 2, stride=2), :] = back[:, at : at + 128].reshape(blocks)
     gresid = resid_scr[...].reshape(pixels, 128).astype(BF)
     pg_ref[...] += dot(hidden, gresid, ((0,), (0,)))
-    gpre = (dot(gresid, pj[...], ((1,), (1,))) * slope).astype(BF)
+    gpre = (dot(gresid, pj, ((1,), (1,))) * slope).astype(BF)
     gc_ref[...] += dot(wide, gpre, ((0,), (0,)))
 
 
 def run_block(edge, corner, place, feat, up, down_rows, near, own, far, sides, cot, wc, pj, dw, last_row):
     faces, height, width, channels = feat.shape
     hid = wc.shape[1]
-    group = 3 if width <= 64 else 1
+    group = 6 if width <= 64 else 1
     tall = height + 2 * DEPTH
     smem = pl.BlockSpec(memory_space=pltpu.SMEM)
 
@@ -226,7 +234,6 @@
         ),
         out_shape=tuple(jax.ShapeDtypeStruct(s, F32) for s in out_shapes),
         scratch_shapes=[
-            pltpu.VMEM((tall, width + 16, channels), F32),
             pltpu.VMEM((3, group, tall, width, channels), BF),
             pltpu.VMEM((group * height // 2, 2, width, channels), F32),
         ],
@@ -323,6 +330,9 @@
     weight_rows = packed.shape[0]
     weights_out = jnp.broadcast_to(packed, (pairs,) + packed.shape)
     sent = jnp.concatenate([weights_out, bands_out], axis=1)
+    sent, edge_table, corner_table, row_late = lax.optimization_barrier(
+        (sent, edge_links, corner_links, row)
+    )
     got = lax.all_to_all(sent, "row", 0, 0, axis_index_groups=same_core)
 
     across_pairs = [(i, i + 1) for i in range(1, last, 2)] + [(i + 1, i) for i in range(1, last, 2)]
@@ -398,7 +408,7 @@
             1,
         ).reshape(rows * part_rows, channels)
 
-    pj = lax.dynamic_slice_in_dim(both_cores(0), col * hid, hid, 0)
+    pj = both_cores(0)
     dw = both_cores(edge_of)
     span = end.shape[0]
 
@@ -427,9 +437,9 @@
     sides = sides.reshape(pairs, faces, DEPTH, pair_height, channels).transpose(1, 2, 0, 3, 4)
     sides = sides.reshape(faces, DEPTH, rows * height, channels)
 
-    place = jnp.stack([row, col]).astype(jnp.int32)
+    place = jnp.stack([row_late, col]).astype(jnp.int32)
     out_part, gc, pg, gd = run_block(
-        edge_links.reshape(-1), corner_links.reshape(-1), place,
+        edge_table.reshape(-1), corner_table.reshape(-1), place,
         feat, up, below, near, own, far, sides, cot, wc, pj, dw, last,
     )
 

time: 105 us -> 101 us (0.962)
  Pallas kernels: 17.9 us -> 14.8 us
  waiting for transfers between devices: 29.2 us -> 26.8 us
  starting transfers between devices: 32.6 us -> 34.1 us
    pallas_call x1, Pallas kernels: 17.9 us -> 14.8 us  [run_block(): pl.pallas_call(functools.partial(block_kernel, group, last_row), grid=(fa...]
    ppermute x12, waiting for transfers between devices: 24 us -> 21.5 us  [swap(): return lax.ppermute(value, axis, [(i, i ^ bit) for i in range(count)])]
    ppermute x12, starting transfers between devices: 12.9 us -> 14.7 us  [swap(): return lax.ppermute(value, axis, [(i, i ^ bit) for i in range(count)])]
    unnamed x56 -> x54, local copies, waits for them, and re-layouts: 3.27 us -> 3.04 us
  transfers between devices with their start and end apart: 18 -> 18, of which waited for: 8 -> 9; matrix products, arithmetic and copies ran while one was open for 13% -> 14% of each run, Pallas kernels for 0% -> 0%
where the time goes in v3:
time: 101 us
  starting transfers between devices  34.1 us (34%)
  waiting for transfers between devices  26.8 us (27%)
  Pallas kernels  14.8 us (15%)
  other arithmetic  11.9 us (12%)
  local copies, waits for them, and re-layouts  11.4 us (11%)
  between operations  1.71 us (2%)
    ppermute x12, waiting for transfers between devices, swap(): return lax.ppermute(value, axis, [(i, i ^ bit) for i in range(count)])  21.5 us
    pallas_call x1, Pallas kernels, run_block(): pl.pallas_call(functools.partial(block_kernel, group, last_row), grid=(fa...  14.8 us
    ppermute x12, starting transfers between devices, swap(): return lax.ppermute(value, axis, [(i, i ^ bit) for i in range(count)])  14.7 us
    ppermute x1, starting transfers between devices, on_device(): far = lax.ppermute(own, 'row', [(0, last), (last, 0)])  6.2 us
    all_to_all x1, waiting for transfers between devices, on_device(): shares = lax.all_to_all(summed, 'row', 0, 0, axis_index_groups=same_core)  5.23 us
    all_to_all x1, starting transfers between devices, on_device(): shares = lax.all_to_all(summed, 'row', 0, 0, axis_index_groups=same_core)  4.93 us
    all_to_all x1, starting transfers between devices, on_device(): got = lax.all_to_all(sent, 'row', 0, 0, axis_index_groups=same_core)  3.68 us
    ppermute x1, starting transfers between devices, on_device(): mirrored = lax.ppermute(edges, 'row', [(i, last - i) for i in range(rows)])  3.33 us
  transfers between devices with their start and end apart: 18, of which 9 were waited for; matrix products, arithmetic and copies ran while one was open for 14% of the time, Pallas kernels for 0%

profile of v3, /device:TPU:0, one launch (start us, length us, event | category | flops | bytes accessed | tf_op | source)
XLA Modules:
  0.0 100.9 jit_solution(10135826465869982866)
XLA Ops:
  0.7 1.0 %slice.266 = bf16[12,2,32,128]{3,2,1,0:T(8,128)(2,1)S(1)} slice(bf16[12,4,32,128]{3,2,1,0:T(8,128)(2,1)} %param.7), slice={[0:12], [2:4], [0:32], [0:128]} | slice | bytes 393216 | tf_op jit(solution)/shard_map/slice | solution.py:277
  1.7 1.1 %fusion.15 = (bf16[12,4,1,128]{3,2,1,0:T(2,128)(2,1)S(1)}, bf16[12,4,1,128]{3,2,1,0:T(2,128)(2,1)S(1)}, bf16[12,4,1,128]{3,2,1,0:T(2,128)(2,1)S(1)}, bf16[12,4,1,128]{3,2,1,0:T(2,128)(2,1)S(1)}) fusion(bf16[12,4,32,128]{3,2,1,0:T(8,128)(2,1)} %param.7), kind=kLoop, calls=%fused_computation.161 | loop fusion | bytes 98304 | tf_op jit(solution)/shard_map/slice | solution.py:280
  3.0 1.1 %broadcast_select_fusion.5 = (bf16[12,2,32,128]{3,2,1,0:T(8,128)(2,1)S(1)}, bf16[12,2,32,128]{3,2,1,0:T(8,128)(2,1)S(1)}) fusion(pred[]{:T(512)S(6)} %eq.66, bf16[12,4,32,128]{3,2,1,0:T(8,128)(2,1)} %param.7, bf16[12,2,32,128]{3,2,1,0:T(8,128)(2,1)S(1)} %slice.266, pred[]{:T(512)S(6)} %eq.64), kind=kLoop, calls=%fused_computation.45 | loop fusion | flops 196608 | bytes 983042 | tf_op jit(solution)/shard_map/jit(_where)/select_n | solution.py:339
  4.2 3.0 %collective-permute-start = (bf16[144,128]{1,0:T(8,128)(2,1)S(1)}, bf16[144,128]{1,0:T(8,128)(2,1)S(1)}, u32[]{:S(2)}, u32[]{:S(2)}) collective-permute-start(bf16[144,128]{1,0:T(8,128)(2,1)S(1)} %pad_maximum_fusion.20), channel_id=1, source_target_pairs={{0,1},{1,0},{2,3},{3,2},{4,5},{5,4},{6,7},{7,6},{8,9},{9,8},{10,11... | collective-permute-start | bytes 110600 | tf_op jit(solution)/shard_map/ppermute | solution.py:17
  7.2 0.7 collective-permute-start.2
  8.3 0.9 collective-permute-done
  9.3 2.3 %collective-permute-start.1 = (bf16[2,12,2,4,128]{4,3,2,1,0:T(4,128)(2,1)S(1)}, bf16[2,12,2,4,128]{4,3,2,1,0:T(4,128)(2,1)S(1)}, u32[]{:S(2)}, u32[]{:S(2)}) collective-permute-start(bf16[2,12,2,4,128]{4,3,2,1,0:T(4,128)(2,1)S(1)} %pad_maximum_fusion.19), channel_id=1, source_target_pairs={{0,2},{2,0},{4,6},{6,4},{8,10},{10,8},{12,14},{14,12},{16,18},{18,... | collective-permute-start | bytes 147464 | tf_op jit(solution)/shard_map/ppermute | solution.py:17
  11.5 3.3 %collective-permute-start.7 = (bf16[2,12,2,4,128]{4,3,2,1,0:T(4,128)(2,1)S(1)}, bf16[2,12,2,4,128]{4,3,2,1,0:T(4,128)(2,1)S(1)}, u32[]{:S(2)}, u32[]{:S(2)}) collective-permute-start(bf16[2,12,2,4,128]{4,3,2,1,0:T(4,128)(2,1)S(1)} %pad_maximum_fusion.19), channel_id=1, source_target_pairs={{0,30},{2,28},{4,26},{6,24},{8,22},{10,20},{12,18},{14,16},{16,14}... | collective-permute-start | bytes 147464 | tf_op jit(solution)/shard_map/ppermute | solution.py:351
  15.7 0.2 convolution_convert_fusion
  16.1 1.1 %pad_maximum_fusion = bf16[8,464,128]{2,1,0:T(8,128)(2,1)} fusion(bf16[8,288,128]{2,1,0:T(8,128)(2,1)S(1)} %select_select_fusion, bf16[8,176,128]{2,1,0:T(8,128)(2,1)S(1)} %broadcast_in_dim.20), kind=kLoop, calls=%fused_computation.7 | loop fusion | flops 1900544 | bytes 1900544 | tf_op jit(solution)/shard_map/concatenate | solution.py:332
  17.1 3.7 %all-to-all-start = ((bf16[8,464,128]{2,1,0:T(8,128)(2,1)}), bf16[8,464,128]{2,1,0:T(8,128)(2,1)S(1)}, u32[]{:S(2)}, u32[]{:S(2)}) async-start(bf16[8,464,128]{2,1,0:T(8,128)(2,1)} %pad_maximum_fusion), calls=%async_computation | async-start | bytes 1900544 | tf_op jit(solution)/shard_map/all_to_all | solution.py:336
  21.1 0.7 collective-permute-start.9
  21.8 1.6 %collective-permute-start.3 = (bf16[12,6,32,128]{3,2,1,0:T(8,128)(2,1)S(1)}, bf16[12,6,32,128]{3,2,1,0:T(8,128)(2,1)S(1)}, u32[]{:S(2)}, u32[]{:S(2)}) collective-permute-start(bf16[12,6,32,128]{3,2,1,0:T(8,128)(2,1)S(1)} %constant_dynamic-update-slice_fusion.8), channel_id=1, source_target_pairs={{0,1},{1,0},{2,3},{3,2},{4,5},{5,4},{6,7},{7,6},{8,9},{9,8},{10,11... | collective-permute-start | bytes 1769480 | tf_op jit(solution)/shard_map/ppermute | solution.py:17
  23.4 0.6 pad_add_fusion.where_ref
  24.1 0.7 reshape.388.edge
  24.9 0.7 reshape.389.corner
  25.6 0.7 pad_maximum_fusion.6.cot
  26.4 9.4 %collective-permute-done.3 = bf16[12,6,32,128]{3,2,1,0:T(8,128)(2,1)S(1)} collective-permute-done((bf16[12,6,32,128]{3,2,1,0:T(8,128)(2,1)S(1)}, bf16[12,6,32,128]{3,2,1,0:T(8,128)(2,1)S(1)}, u32[]{:S(2)}, u32[]{:S(2)}) %collective-permute-start.3) | collective-permute-done | bytes 589856 | tf_op jit(solution)/shard_map/ppermute | solution.py:17
  35.9 0.2 broadcast_select_fusion.4
  36.1 2.4 %collective-permute-start.4 = (bf16[12,2,64,128]{3,2,1,0:T(8,128)(2,1)S(1)}, bf16[12,2,64,128]{3,2,1,0:T(8,128)(2,1)S(1)}, u32[]{:S(2)}, u32[]{:S(2)}) collective-permute-start(bf16[12,2,64,128]{3,2,1,0:T(8,128)(2,1)S(1)} %get-tuple-element.20), channel_id=1, source_target_pairs={{0,2},{2,0},{4,6},{6,4},{8,10},{10,8},{12,14},{14,12},{16,18},{18,... | collective-permute-start | bytes 1179656 | tf_op jit(solution)/shard_map/ppermute | solution.py:17
  38.6 1.0 fusion.1.feat
  39.6 0.3 collective-permute-done.4
  39.8 0.3 broadcast_select_fusion.2
  40.5 6.2 %collective-permute-start.10 = (bf16[12,2,64,128]{3,2,1,0:T(8,128)(2,1)S(1)}, bf16[12,2,64,128]{3,2,1,0:T(8,128)(2,1)S(1)}, u32[]{:S(2)}, u32[]{:S(2)}) collective-permute-start(bf16[12,2,64,128]{3,2,1,0:T(8,128)(2,1)S(1)} %get-tuple-element.26.own), channel_id=1, source_target_pairs={{0,30},{30,0},{1,31},{31,1}} | collective-permute-start | bytes 1179656 | tf_op jit(solution)/shard_map/ppermute | solution.py:349
  47.0 1.6 %collective-permute-start.5 = (bf16[544,128]{1,0:T(8,128)(2,1)S(1)}, bf16[544,128]{1,0:T(8,128)(2,1)S(1)}, u32[]{:S(2)}, u32[]{:S(2)}) collective-permute-start(bf16[544,128]{1,0:T(8,128)(2,1)S(1)} %pad_maximum_fusion.7), channel_id=1, source_target_pairs={{0,1},{1,0},{2,3},{3,2},{4,5},{5,4},{6,7},{7,6},{8,9},{9,8},{10,11... | collective-permute-start | bytes 417800 | tf_op jit(solution)/shard_map/ppermute | solution.py:17
  48.8 0.9 copy.177
  49.7 2.4 %collective-permute-done.5 = bf16[544,128]{1,0:T(8,128)(2,1)S(1)} collective-permute-done((bf16[544,128]{1,0:T(8,128)(2,1)S(1)}, bf16[544,128]{1,0:T(8,128)(2,1)S(1)}, u32[]{:S(2)}, u32[]{:S(2)}) %collective-permute-start.5) | collective-permute-done | bytes 139296 | tf_op jit(solution)/shard_map/ppermute | solution.py:17
  52.8 0.9 copy.125
  53.7 0.5 collective-permute-done.6
  54.8 0.7 copy.127
  55.5 0.7 copy.126
  56.2 1.0 maximum_convert_fusion.near
  57.2 0.7 copy-done.14
  57.9 14.8 %shard_map.102 = (f32[12,2,32,128]{3,2,1,0:T(8,128)}, f32[1152,256]{1,0:T(8,128)}, f32[256,128]{1,0:T(8,128)}, f32[512,128]{1,0:T(8,128)}) custom-call(s32[144]{0:T(256)} %reshape.388.edge, s32[144]{0:T(256)} %reshape.389.corner, s32[2]{0:T(128)} %pad_add_fusion.where_ref, bf16[12,4,64,128]{3,2,1,0:T(8,128)(2,1)} %fusion.1.feat, ...), custom_call_target="tpu_custom_call" | custom-call | flops 4227858432 | bytes 12582912 | tf_op jit(solution)/shard_map/pallas_call | solution.py:222
  72.7 1.4 %select_bitcast_fusion = f32[8,72,256]{2,1,0:T(8,128)S(1)} fusion(f32[8,2,72,256]{3,2,1,0:T(8,128)} %bitcast.170, pred[]{:T(512)S(6)} %eq.66), kind=kLoop, calls=%fused_computation.19 | loop fusion | flops 147456 | bytes 1769473 | tf_op jit(solution)/shard_map/jit(_where)/select_n | solution.py:458
  74.2 0.8 copy-done.6
  75.2 1.1 %copy-done = f32[1152,256]{1,0:T(8,128)S(1)} copy-done((f32[1152,256]{1,0:T(8,128)S(1)}, f32[1152,256]{1,0:T(8,128)}, u32[]{:S(2)}) %copy-start) | copy-done | bytes 1179672
  76.4 1.2 %collective-permute-done.14 = f32[8,208,128]{2,1,0:T(8,128)S(1)} collective-permute-done((f32[8,208,128]{2,1,0:T(8,128)S(1)}, f32[8,208,128]{2,1,0:T(8,128)S(1)}, u32[]{:S(2)}, u32[]{:S(2)}) %collective-permute-start.14) | collective-permute-done | bytes 852000 | tf_op jit(solution)/shard_map/ppermute | solution.py:17
  77.6 0.9 fusion
  78.5 4.9 %all-to-all-start.1 = ((bf16[8,208,128]{2,1,0:T(8,128)(2,1)}), bf16[8,208,128]{2,1,0:T(8,128)(2,1)S(1)}, u32[]{:S(2)}, u32[]{:S(2)}) async-start(bf16[8,208,128]{2,1,0:T(8,128)(2,1)} %fusion), calls=%async_computation.1 | async-start | bytes 851968 | tf_op jit(solution)/shard_map/all_to_all | solution.py:464
  83.4 1.6 %collective-permute-start.13 = (f32[12,2,16,128]{3,2,1,0:T(8,128)S(1)}, f32[12,2,16,128]{3,2,1,0:T(8,128)S(1)}, u32[]{:S(2)}, u32[]{:S(2)}) collective-permute-start(f32[12,2,16,128]{3,2,1,0:T(8,128)S(1)} %slice_select_fusion.1), channel_id=1, source_target_pairs={{0,1},{1,0},{2,3},{3,2},{4,5},{5,4},{6,7},{7,6},{8,9},{9,8},{10,11... | collective-permute-start | bytes 589832 | tf_op jit(solution)/shard_map/ppermute | solution.py:17
  85.0 5.1 %collective-permute-done.13 = f32[12,2,16,128]{3,2,1,0:T(8,128)S(1)} collective-permute-done((f32[12,2,16,128]{3,2,1,0:T(8,128)S(1)}, f32[12,2,16,128]{3,2,1,0:T(8,128)S(1)}, u32[]{:S(2)}, u32[]{:S(2)}) %collective-permute-start.13) | collective-permute-done | bytes 196640 | tf_op jit(solution)/shard_map/ppermute | solution.py:17
  90.2 0.7 add_convert_fusion
  90.8 5.2 %all-to-all-done.1 = bf16[8,208,128]{2,1,0:T(8,128)(2,1)S(1)} async-done(((bf16[8,208,128]{2,1,0:T(8,128)(2,1)}), bf16[8,208,128]{2,1,0:T(8,128)(2,1)S(1)}, u32[]{:S(2)}, u32[]{:S(2)}) %all-to-all-start.1) | async-done | bytes 426016 | tf_op jit(solution)/shard_map/all_to_all | solution.py:464
  96.2 1.6 %collective-permute-start.15 = (f32[64,64]{1,0:T(8,128)S(1)}, f32[64,64]{1,0:T(8,128)S(1)}, u32[]{:S(2)}, u32[]{:S(2)}) collective-permute-start(f32[64,64]{1,0:T(8,128)S(1)} %slice_select_fusion.5), channel_id=1, source_target_pairs={{0,1},{1,0},{2,3},{3,2},{4,5},{5,4},{6,7},{7,6},{8,9},{9,8},{10,11... | collective-permute-start | bytes 49160 | tf_op jit(solution)/shard_map/ppermute | solution.py:17
  97.8 0.6 pad_maximum_fusion.14
  98.5 1.7 %collective-permute-done.15 = f32[64,64]{1,0:T(8,128)S(1)} collective-permute-done((f32[64,64]{1,0:T(8,128)S(1)}, f32[64,64]{1,0:T(8,128)S(1)}, u32[]{:S(2)}, u32[]{:S(2)}) %collective-permute-start.15) | collective-permute-done | bytes 16416 | tf_op jit(solution)/shard_map/ppermute | solution.py:17
  100.3 0.6 fusion.23
  (155 shorter events, 4.4 us)
Async XLA Ops:
  0.6 7.4 %copy-start.1 = (bf16[12,4,32,128]{3,2,1,0:T(8,128)(2,1)S(1)}, bf16[12,4,32,128]{3,2,1,0:T(8,128)(2,1)}, u32[]{:S(2)}) copy-start(bf16[12,4,32,128]{3,2,1,0:T(8,128)(2,1)} %param.7) | copy-start | bytes 1179652
  0.6 7.3 %copy-start.8 = (bf16[12,2,16,128]{3,2,1,0:T(8,128)(2,1)S(1)}, bf16[12,2,16,128]{3,2,1,0:T(8,128)(2,1)}, u32[]{:S(2)}) copy-start(bf16[12,2,16,128]{3,2,1,0:T(8,128)(2,1)} %param.8) | copy-start | bytes 294916
  1.7 6.4 %copy-start.10 = (s32[12,4,3]{0,1,2:T(4,128)S(1)}, s32[12,4,3]{0,1,2:T(4,128)}, u32[]{:S(2)}) copy-start(s32[12,4,3]{0,1,2:T(4,128)} %param.12) | copy-start | bytes 1732
  1.7 6.4 %copy-start.9 = (bf16[72,256]{1,0:T(8,128)(2,1)S(1)}, bf16[72,256]{1,0:T(8,128)(2,1)}, u32[]{:S(2)}) copy-start(bf16[72,256]{1,0:T(8,128)(2,1)} %param.9) | copy-start | bytes 110596
  2.9 5.3 %copy-start.11 = (bf16[32,64]{1,0:T(8,128)(2,1)S(1)}, bf16[32,64]{1,0:T(8,128)(2,1)}, u32[]{:S(2)}) copy-start(bf16[32,64]{1,0:T(8,128)(2,1)} %param.11) | copy-start | bytes 12292
  2.9 5.3 %copy-start.12 = (bf16[32,64]{1,0:T(8,128)(2,1)S(1)}, bf16[32,64]{1,0:T(8,128)(2,1)}, u32[]{:S(2)}) copy-start(bf16[32,64]{1,0:T(8,128)(2,1)} %param.10) | copy-start | bytes 12292
  4.2 5.0 %collective-permute-start = (bf16[144,128]{1,0:T(8,128)(2,1)S(1)}, bf16[144,128]{1,0:T(8,128)(2,1)S(1)}, u32[]{:S(2)}, u32[]{:S(2)}) collective-permute-start(bf16[144,128]{1,0:T(8,128)(2,1)S(1)} %pad_maximum_fusion.20), channel_id=1, source_target_pairs={{0,1},{1,0},{2,3},{3,2},{4,5},{5,4},{6,7},{7,6},{8,9},{9,8},{10,11... | collective-permute-start | bytes 110600 | tf_op jit(solution)/shard_map/ppermute | solution.py:17
  7.2 14.5 %collective-permute-start.2 = (bf16[12,2,32,128]{3,2,1,0:T(8,128)(2,1)S(1)}, bf16[12,2,32,128]{3,2,1,0:T(8,128)(2,1)S(1)}, u32[]{:S(2)}, u32[]{:S(2)}) collective-permute-start(bf16[12,2,32,128]{3,2,1,0:T(8,128)(2,1)S(1)} %get-tuple-element.43), channel_id=1, source_target_pairs={{2,4},{6,8},{10,12},{14,16},{18,20},{22,24},{26,28},{4,2},{8,6},{1... | collective-permute-start | bytes 589832 | tf_op jit(solution)/shard_map/ppermute | solution.py:340
  7.9 17.7 %collective-permute-start.11 = (bf16[12,2,16,128]{3,2,1,0:T(8,128)(2,1)S(1)}, bf16[12,2,16,128]{3,2,1,0:T(8,128)(2,1)S(1)}, u32[]{:S(2)}, u32[]{:S(2)}) collective-permute-start(bf16[12,2,16,128]{3,2,1,0:T(8,128)(2,1)S(1)} %copy-done.8), channel_id=1, source_target_pairs={{0,1},{1,0},{2,3},{3,2},{4,5},{5,4},{6,7},{7,6},{8,9},{9,8},{10,11... | collective-permute-start | bytes 294920 | tf_op jit(solution)/shard_map/ppermute | solution.py:17
  9.3 6.2 %collective-permute-start.1 = (bf16[2,12,2,4,128]{4,3,2,1,0:T(4,128)(2,1)S(1)}, bf16[2,12,2,4,128]{4,3,2,1,0:T(4,128)(2,1)S(1)}, u32[]{:S(2)}, u32[]{:S(2)}) collective-permute-start(bf16[2,12,2,4,128]{4,3,2,1,0:T(4,128)(2,1)S(1)} %pad_maximum_fusion.19), channel_id=1, source_target_pairs={{0,2},{2,0},{4,6},{6,4},{8,10},{10,8},{12,14},{14,12},{16,18},{18,... | collective-permute-start | bytes 147464 | tf_op jit(solution)/shard_map/ppermute | solution.py:17
  11.5 9.3 %collective-permute-start.7 = (bf16[2,12,2,4,128]{4,3,2,1,0:T(4,128)(2,1)S(1)}, bf16[2,12,2,4,128]{4,3,2,1,0:T(4,128)(2,1)S(1)}, u32[]{:S(2)}, u32[]{:S(2)}) collective-permute-start(bf16[2,12,2,4,128]{4,3,2,1,0:T(4,128)(2,1)S(1)} %pad_maximum_fusion.19), channel_id=1, source_target_pairs={{0,30},{2,28},{4,26},{6,24},{8,22},{10,20},{12,18},{14,16},{16,14}... | collective-permute-start | bytes 147464 | tf_op jit(solution)/shard_map/ppermute | solution.py:351
  17.1 7.6 %copy-start.13 = (s32[12,4,3]{0,1,2:T(4,128)S(1)}, s32[12,4,3]{0,1,2:T(4,128)}, u32[]{:S(2)}) copy-start(s32[12,4,3]{0,1,2:T(4,128)} %param.13) | copy-start | bytes 1732
  17.1 29.8 %all-to-all-start = ((bf16[8,464,128]{2,1,0:T(8,128)(2,1)}), bf16[8,464,128]{2,1,0:T(8,128)(2,1)S(1)}, u32[]{:S(2)}, u32[]{:S(2)}) async-start(bf16[8,464,128]{2,1,0:T(8,128)(2,1)} %pad_maximum_fusion), calls=%async_computation | async-start | bytes 1900544 | tf_op jit(solution)/shard_map/all_to_all | solution.py:336
  20.9 5.4 %collective-permute-start.8 = (bf16[2,12,2,2,128]{4,3,2,1,0:T(2,128)(2,1)S(1)}, bf16[2,12,2,2,128]{4,3,2,1,0:T(2,128)(2,1)S(1)}, u32[]{:S(2)}, u32[]{:S(2)}) collective-permute-start(bf16[2,12,2,2,128]{4,3,2,1,0:T(2,128)(2,1)S(1)} %get-tuple-element.99), channel_id=1, source_target_pairs={{0,2},{2,0},{4,6},{6,4},{8,10},{10,8},{12,14},{14,12},{16,18},{18,... | collective-permute-start | bytes 73736 | tf_op jit(solution)/shard_map/ppermute | solution.py:17
  21.1 5.3 %collective-permute-start.9 = (bf16[2,12,2,2,128]{4,3,2,1,0:T(2,128)(2,1)S(1)}, bf16[2,12,2,2,128]{4,3,2,1,0:T(2,128)(2,1)S(1)}, u32[]{:S(2)}, u32[]{:S(2)}) collective-permute-start(bf16[2,12,2,2,128]{4,3,2,1,0:T(2,128)(2,1)S(1)} %get-tuple-element.100), channel_id=1, source_target_pairs={{2,4},{6,8},{10,12},{14,16},{18,20},{22,24},{26,28},{4,2},{8,6},{1... | collective-permute-start | bytes 73736 | tf_op jit(solution)/shard_map/ppermute | solution.py:355
  21.8 14.0 %collective-permute-start.3 = (bf16[12,6,32,128]{3,2,1,0:T(8,128)(2,1)S(1)}, bf16[12,6,32,128]{3,2,1,0:T(8,128)(2,1)S(1)}, u32[]{:S(2)}, u32[]{:S(2)}) collective-permute-start(bf16[12,6,32,128]{3,2,1,0:T(8,128)(2,1)S(1)} %constant_dynamic-update-slice_fusion.8), channel_id=1, source_target_pairs={{0,1},{1,0},{2,3},{3,2},{4,5},{5,4},{6,7},{7,6},{8,9},{9,8},{10,11... | collective-permute-start | bytes 1769480 | tf_op jit(solution)/shard_map/ppermute | solution.py:17
  36.1 3.8 %collective-permute-start.4 = (bf16[12,2,64,128]{3,2,1,0:T(8,128)(2,1)S(1)}, bf16[12,2,64,128]{3,2,1,0:T(8,128)(2,1)S(1)}, u32[]{:S(2)}, u32[]{:S(2)}) collective-permute-start(bf16[12,2,64,128]{3,2,1,0:T(8,128)(2,1)S(1)} %get-tuple-element.20), channel_id=1, source_target_pairs={{0,2},{2,0},{4,6},{6,4},{8,10},{10,8},{12,14},{14,12},{16,18},{18,... | collective-permute-start | bytes 1179656 | tf_op jit(solution)/shard_map/ppermute | solution.py:17
  40.2 8.6 %copy-start.3 = (bf16[12,2,64,128]{3,2,1,0:T(8,128)(2,1)}, bf16[12,2,64,128]{3,2,1,0:T(8,128)(2,1)S(1)}, u32[]{:S(2)}) copy-start(bf16[12,2,64,128]{3,2,1,0:T(8,128)(2,1)S(1)} %get-tuple-element.22.down_rows) | copy-start | bytes 1179652
  40.2 8.6 %copy-start.4 = (bf16[12,2,64,128]{3,2,1,0:T(8,128)(2,1)}, bf16[12,2,64,128]{3,2,1,0:T(8,128)(2,1)S(1)}, u32[]{:S(2)}) copy-start(bf16[12,2,64,128]{3,2,1,0:T(8,128)(2,1)S(1)} %get-tuple-element.23.up) | copy-start | bytes 1179652
  40.2 8.6 %copy-start.5 = (bf16[12,2,64,128]{3,2,1,0:T(8,128)(2,1)}, bf16[12,2,64,128]{3,2,1,0:T(8,128)(2,1)S(1)}, u32[]{:S(2)}) copy-start(bf16[12,2,64,128]{3,2,1,0:T(8,128)(2,1)S(1)} %get-tuple-element.26.own) | copy-start | bytes 1179652
  40.5 16.7 %collective-permute-start.10 = (bf16[12,2,64,128]{3,2,1,0:T(8,128)(2,1)S(1)}, bf16[12,2,64,128]{3,2,1,0:T(8,128)(2,1)S(1)}, u32[]{:S(2)}, u32[]{:S(2)}) collective-permute-start(bf16[12,2,64,128]{3,2,1,0:T(8,128)(2,1)S(1)} %get-tuple-element.26.own), channel_id=1, source_target_pairs={{0,30},{30,0},{1,31},{31,1}} | collective-permute-start | bytes 1179656 | tf_op jit(solution)/shard_map/ppermute | solution.py:349
  47.0 5.1 %collective-permute-start.5 = (bf16[544,128]{1,0:T(8,128)(2,1)S(1)}, bf16[544,128]{1,0:T(8,128)(2,1)S(1)}, u32[]{:S(2)}, u32[]{:S(2)}) collective-permute-start(bf16[544,128]{1,0:T(8,128)(2,1)S(1)} %pad_maximum_fusion.7), channel_id=1, source_target_pairs={{0,1},{1,0},{2,3},{3,2},{4,5},{5,4},{6,7},{7,6},{8,9},{9,8},{10,11... | collective-permute-start | bytes 417800 | tf_op jit(solution)/shard_map/ppermute | solution.py:17
  48.6 4.0 %collective-permute-start.12 = (bf16[8,144,128]{2,1,0:T(8,128)(2,1)S(1)}, bf16[8,144,128]{2,1,0:T(8,128)(2,1)S(1)}, u32[]{:S(2)}, u32[]{:S(2)}) collective-permute-start(bf16[8,144,128]{2,1,0:T(8,128)(2,1)S(1)} %slice.384), channel_id=1, source_target_pairs={{0,2},{2,0},{4,6},{6,4},{8,10},{10,8},{12,14},{14,12},{16,18},{18,... | collective-permute-start | bytes 884744 | tf_op jit(solution)/shard_map/ppermute | solution.py:17
  52.5 1.6 %collective-permute-start.6 = (bf16[1088,128]{1,0:T(8,128)(2,1)S(1)}, bf16[1088,128]{1,0:T(8,128)(2,1)S(1)}, u32[]{:S(2)}, u32[]{:S(2)}) collective-permute-start(bf16[1088,128]{1,0:T(8,128)(2,1)S(1)} %pad_maximum_fusion.5), channel_id=1, source_target_pairs={{0,2},{2,0},{4,6},{6,4},{8,10},{10,8},{12,14},{14,12},{16,18},{18,... | collective-permute-start | bytes 835592 | tf_op jit(solution)/shard_map/ppermute | solution.py:17
  57.2 0.7 copy-start.14
  72.7 1.5 %copy-start.7 = (f32[256,128]{1,0:T(8,128)S(1)}, f32[256,128]{1,0:T(8,128)}, u32[]{:S(2)}) copy-start(f32[256,128]{1,0:T(8,128)} %get-tuple-element.18) | copy-start | bytes 393220
  74.1 1.0 copy-start.6
  75.0 1.3 %copy-start = (f32[1152,256]{1,0:T(8,128)S(1)}, f32[1152,256]{1,0:T(8,128)}, u32[]{:S(2)}) copy-start(f32[1152,256]{1,0:T(8,128)} %get-tuple-element.17) | copy-start | bytes 3538948
  75.1 2.4 %collective-permute-start.14 = (f32[8,208,128]{2,1,0:T(8,128)S(1)}, f32[8,208,128]{2,1,0:T(8,128)S(1)}, u32[]{:S(2)}, u32[]{:S(2)}) collective-permute-start(f32[8,208,128]{2,1,0:T(8,128)S(1)} %pad_maximum_fusion.1), channel_id=1, source_target_pairs={{0,2},{2,0},{4,6},{6,4},{8,10},{10,8},{12,14},{14,12},{16,18},{18,... | collective-permute-start | bytes 2555912 | tf_op jit(solution)/shard_map/ppermute | solution.py:17
  77.6 5.8 %copy-start.2 = (f32[12,2,32,128]{3,2,1,0:T(8,128)S(1)}, f32[12,2,32,128]{3,2,1,0:T(8,128)}, u32[]{:S(2)}) copy-start(f32[12,2,32,128]{3,2,1,0:T(8,128)} %get-tuple-element.16) | copy-start | bytes 1179652
  78.5 17.6 %all-to-all-start.1 = ((bf16[8,208,128]{2,1,0:T(8,128)(2,1)}), bf16[8,208,128]{2,1,0:T(8,128)(2,1)S(1)}, u32[]{:S(2)}, u32[]{:S(2)}) async-start(bf16[8,208,128]{2,1,0:T(8,128)(2,1)} %fusion), calls=%async_computation.1 | async-start | bytes 851968 | tf_op jit(solution)/shard_map/all_to_all | solution.py:464
  83.4 6.7 %collective-permute-start.13 = (f32[12,2,16,128]{3,2,1,0:T(8,128)S(1)}, f32[12,2,16,128]{3,2,1,0:T(8,128)S(1)}, u32[]{:S(2)}, u32[]{:S(2)}) collective-permute-start(f32[12,2,16,128]{3,2,1,0:T(8,128)S(1)} %slice_select_fusion.1), channel_id=1, source_target_pairs={{0,1},{1,0},{2,3},{3,2},{4,5},{5,4},{6,7},{7,6},{8,9},{9,8},{10,11... | collective-permute-start | bytes 589832 | tf_op jit(solution)/shard_map/ppermute | solution.py:17
  96.2 4.0 %collective-permute-start.15 = (f32[64,64]{1,0:T(8,128)S(1)}, f32[64,64]{1,0:T(8,128)S(1)}, u32[]{:S(2)}, u32[]{:S(2)}) collective-permute-start(f32[64,64]{1,0:T(8,128)S(1)} %slice_select_fusion.5), channel_id=1, source_target_pairs={{0,1},{1,0},{2,3},{3,2},{4,5},{5,4},{6,7},{7,6},{8,9},{9,8},{10,11... | collective-permute-start | bytes 49160 | tf_op jit(solution)/shard_map/ppermute | solution.py:17

commit v4 on v3

--- a/solution.py
+++ b/solution.py
@@ -444,12 +444,20 @@
     )
 
     gc_parts = gc.reshape(pairs, 2, conv_weight.shape[0], hid)
-    pg_wide = jnp.zeros((rows, part_rows, channels), F32)
-    pg_wide = lax.dynamic_update_slice_in_dim(
-        pg_wide, pg.reshape(-1, part_rows, channels), col * (rows // cols), 0
-    )
-    pg_parts = pg_wide.reshape(pairs, 2, part_rows, channels)
-    gd_parts = gd.reshape(pairs, 2, part_rows, channels)
+    pg_wide = jnp.zeros((rows * part_rows, channels), F32)
+    pg_wide = lax.dynamic_update_slice_in_dim(pg_wide, pg, col * hid, 0)
+    if cols == 2:
+        cut = channels // 2
+        low = jnp.concatenate([pg_wide[:, :cut], gd[:, :cut]], axis=1)
+        high = jnp.concatenate([pg_wide[:, cut:], gd[:, cut:]], axis=1)
+        joint = jnp.where(col == 0, low, high)
+        joint = joint + swap(jnp.where(col == 0, high, low).astype(BF), "col", 1).astype(F32)
+    else:
+        joint = jnp.concatenate(
+            [scatter_sum_pair(pg_wide, "col", 1), scatter_sum_pair(gd, "col", 1)], axis=1
+        )
+    joint_width = joint.shape[1]
+    joint = joint.reshape(pairs, 2, part_rows, joint_width)
 
     def mine_of(value):
         return jnp.where(even, value[:, 0], value[:, 1])
@@ -457,17 +465,20 @@
     def theirs_of(value):
         return jnp.where(even, value[:, 1], value[:, 0])
 
-    def join_parts(pick):
-        return jnp.concatenate([pack_cols(pick(gc_parts)), pick(pg_parts), pick(gd_parts)], axis=1)
-
-    summed = (join_parts(mine_of) + swap(join_parts(theirs_of), "row", 1)).astype(BF)
+    def narrow(value):
+        return value if joint_width == channels else pack_cols(value)
+
+    conv_sum = pack_cols(mine_of(gc_parts)) + swap(pack_cols(theirs_of(gc_parts)), "row", 1)
+    joint_sum = narrow(mine_of(joint)) + swap(narrow(theirs_of(joint)), "row", 1)
+    summed = jnp.concatenate([conv_sum, joint_sum], axis=1).astype(BF)
     shares = lax.all_to_all(summed, "row", 0, 0, axis_index_groups=same_core)
     block_out = scatter_sum_pair(out_part, "col", 2).astype(BF)
     total = jnp.sum(shares.astype(F32), axis=0)
-    conv_rows = total.shape[0] - 2 * part_rows
+    conv_rows = conv_sum.shape[1]
     grad_conv = unpack_cols(total[:conv_rows], hid)
-    smaller = scatter_sum_pair(total[conv_rows:], "col", 1)
-    return block_out, grad_conv, smaller[:part_rows], smaller[part_rows:]
+    smaller = total[conv_rows:].reshape(part_rows, joint_width)
+    cut = joint_width // 2
+    return block_out, grad_conv, smaller[:, :cut], smaller[:, cut:]
 
 
 def solution(mesh):

time: 101 us -> 102 us (level)
    ppermute x12 -> x13, waiting for transfers between devices: 21.5 us -> 23.5 us  [swap(): return lax.ppermute(value, axis, [(i, i ^ bit) for i in range(count)])]
    all_to_all x1, waiting for transfers between devices: 5.23 us -> 3.83 us  [on_device(): shares = lax.all_to_all(summed, 'row', 0, 0, axis_index_groups=same_core)]
    unnamed x54, local copies, waits for them, and re-layouts: 3.04 us -> 1.82 us
    ppermute x12 -> x13, starting transfers between devices: 14.7 us -> 14.7 us  [swap(): return lax.ppermute(value, axis, [(i, i ^ bit) for i in range(count)])]
  transfers between devices with their start and end apart: 18 -> 19, of which waited for: 9 -> 9; matrix products, arithmetic and copies ran while one was open for 14% -> 14% of each run, Pallas kernels for 0% -> 0%
where the time goes in v4:
time: 102 us; the launch traced here: 101 us
  starting transfers between devices  34.5 us (34%)
  waiting for transfers between devices  27.3 us (27%)
  Pallas kernels  14.8 us (15%)
  other arithmetic  12 us (12%)
  local copies, waits for them, and re-layouts  10.5 us (10%)
  between operations  1.75 us (2%)
    ppermute x13, waiting for transfers between devices, swap(): return lax.ppermute(value, axis, [(i, i ^ bit) for i in range(count)])  23.5 us
    pallas_call x1, Pallas kernels, run_block(): pl.pallas_call(functools.partial(block_kernel, group, last_row), grid=(fa...  14.8 us
    ppermute x13, starting transfers between devices, swap(): return lax.ppermute(value, axis, [(i, i ^ bit) for i in range(count)])  14.7 us
    ppermute x1, starting transfers between devices, on_device(): far = lax.ppermute(own, 'row', [(0, last), (last, 0)])  6.2 us
    all_to_all x1, starting transfers between devices, on_device(): shares = lax.all_to_all(summed, 'row', 0, 0, axis_index_groups=same_core)  5.24 us
    all_to_all x1, waiting for transfers between devices, on_device(): shares = lax.all_to_all(summed, 'row', 0, 0, axis_index_groups=same_core)  3.83 us
    all_to_all x1, starting transfers between devices, on_device(): got = lax.all_to_all(sent, 'row', 0, 0, axis_index_groups=same_core)  3.68 us
    ppermute x1, starting transfers between devices, on_device(): mirrored = lax.ppermute(edges, 'row', [(i, last - i) for i in range(rows)])  3.33 us
  transfers between devices with their start and end apart: 19, of which 9 were waited for; matrix products, arithmetic and copies ran while one was open for 14% of the time, Pallas kernels for 0%

profile of v4, /device:TPU:0, one launch (start us, length us, event | category | flops | bytes accessed | tf_op | source)
XLA Modules:
  0.0 101.1 jit_solution(15160157130294035762)
XLA Ops:
  0.7 1.0 %slice.270 = bf16[12,2,32,128]{3,2,1,0:T(8,128)(2,1)S(1)} slice(bf16[12,4,32,128]{3,2,1,0:T(8,128)(2,1)} %param.7), slice={[0:12], [2:4], [0:32], [0:128]} | slice | bytes 393216 | tf_op jit(solution)/shard_map/slice | solution.py:277
  1.7 1.1 %fusion.16 = (bf16[12,4,1,128]{3,2,1,0:T(2,128)(2,1)S(1)}, bf16[12,4,1,128]{3,2,1,0:T(2,128)(2,1)S(1)}, bf16[12,4,1,128]{3,2,1,0:T(2,128)(2,1)S(1)}, bf16[12,4,1,128]{3,2,1,0:T(2,128)(2,1)S(1)}) fusion(bf16[12,4,32,128]{3,2,1,0:T(8,128)(2,1)} %param.7), kind=kLoop, calls=%fused_computation.161 | loop fusion | bytes 98304 | tf_op jit(solution)/shard_map/slice | solution.py:280
  3.0 1.1 %broadcast_select_fusion.5 = (bf16[12,2,32,128]{3,2,1,0:T(8,128)(2,1)S(1)}, bf16[12,2,32,128]{3,2,1,0:T(8,128)(2,1)S(1)}) fusion(pred[]{:T(512)S(6)} %eq.67, bf16[12,4,32,128]{3,2,1,0:T(8,128)(2,1)} %param.7, bf16[12,2,32,128]{3,2,1,0:T(8,128)(2,1)S(1)} %slice.270, pred[]{:T(512)S(6)} %eq.65), kind=kLoop, calls=%fused_computation.50 | loop fusion | flops 196608 | bytes 983042 | tf_op jit(solution)/shard_map/jit(_where)/select_n | solution.py:339
  4.2 3.0 %collective-permute-start = (bf16[144,128]{1,0:T(8,128)(2,1)S(1)}, bf16[144,128]{1,0:T(8,128)(2,1)S(1)}, u32[]{:S(2)}, u32[]{:S(2)}) collective-permute-start(bf16[144,128]{1,0:T(8,128)(2,1)S(1)} %pad_maximum_fusion.23), channel_id=1, source_target_pairs={{0,1},{1,0},{2,3},{3,2},{4,5},{5,4},{6,7},{7,6},{8,9},{9,8},{10,11... | collective-permute-start | bytes 110600 | tf_op jit(solution)/shard_map/ppermute | solution.py:17
  7.2 0.7 collective-permute-start.2
  8.3 0.9 collective-permute-done
  9.3 2.3 %collective-permute-start.1 = (bf16[2,12,2,4,128]{4,3,2,1,0:T(4,128)(2,1)S(1)}, bf16[2,12,2,4,128]{4,3,2,1,0:T(4,128)(2,1)S(1)}, u32[]{:S(2)}, u32[]{:S(2)}) collective-permute-start(bf16[2,12,2,4,128]{4,3,2,1,0:T(4,128)(2,1)S(1)} %pad_maximum_fusion.22), channel_id=1, source_target_pairs={{0,2},{2,0},{4,6},{6,4},{8,10},{10,8},{12,14},{14,12},{16,18},{18,... | collective-permute-start | bytes 147464 | tf_op jit(solution)/shard_map/ppermute | solution.py:17
  11.5 3.3 %collective-permute-start.7 = (bf16[2,12,2,4,128]{4,3,2,1,0:T(4,128)(2,1)S(1)}, bf16[2,12,2,4,128]{4,3,2,1,0:T(4,128)(2,1)S(1)}, u32[]{:S(2)}, u32[]{:S(2)}) collective-permute-start(bf16[2,12,2,4,128]{4,3,2,1,0:T(4,128)(2,1)S(1)} %pad_maximum_fusion.22), channel_id=1, source_target_pairs={{0,30},{2,28},{4,26},{6,24},{8,22},{10,20},{12,18},{14,16},{16,14}... | collective-permute-start | bytes 147464 | tf_op jit(solution)/shard_map/ppermute | solution.py:351
  15.7 0.2 convolution_convert_fusion
  16.1 1.1 %pad_maximum_fusion = bf16[8,464,128]{2,1,0:T(8,128)(2,1)} fusion(bf16[8,288,128]{2,1,0:T(8,128)(2,1)S(1)} %select_select_fusion, bf16[8,176,128]{2,1,0:T(8,128)(2,1)S(1)} %broadcast_in_dim.20), kind=kLoop, calls=%fused_computation.7 | loop fusion | flops 1900544 | bytes 1900544 | tf_op jit(solution)/shard_map/concatenate | solution.py:332
  17.2 3.7 %all-to-all-start = ((bf16[8,464,128]{2,1,0:T(8,128)(2,1)}), bf16[8,464,128]{2,1,0:T(8,128)(2,1)S(1)}, u32[]{:S(2)}, u32[]{:S(2)}) async-start(bf16[8,464,128]{2,1,0:T(8,128)(2,1)} %pad_maximum_fusion), calls=%async_computation | async-start | bytes 1900544 | tf_op jit(solution)/shard_map/all_to_all | solution.py:336
  21.1 0.7 collective-permute-start.9
  21.8 1.6 %collective-permute-start.3 = (bf16[12,6,32,128]{3,2,1,0:T(8,128)(2,1)S(1)}, bf16[12,6,32,128]{3,2,1,0:T(8,128)(2,1)S(1)}, u32[]{:S(2)}, u32[]{:S(2)}) collective-permute-start(bf16[12,6,32,128]{3,2,1,0:T(8,128)(2,1)S(1)} %constant_dynamic-update-slice_fusion.8), channel_id=1, source_target_pairs={{0,1},{1,0},{2,3},{3,2},{4,5},{5,4},{6,7},{7,6},{8,9},{9,8},{10,11... | collective-permute-start | bytes 1769480 | tf_op jit(solution)/shard_map/ppermute | solution.py:17
  23.4 0.6 pad_add_fusion.where_ref
  24.1 0.7 reshape.378.edge
  24.9 0.7 reshape.379.corner
  25.6 0.7 pad_maximum_fusion.9.cot
  26.4 9.4 %collective-permute-done.3 = bf16[12,6,32,128]{3,2,1,0:T(8,128)(2,1)S(1)} collective-permute-done((bf16[12,6,32,128]{3,2,1,0:T(8,128)(2,1)S(1)}, bf16[12,6,32,128]{3,2,1,0:T(8,128)(2,1)S(1)}, u32[]{:S(2)}, u32[]{:S(2)}) %collective-permute-start.3) | collective-permute-done | bytes 589856 | tf_op jit(solution)/shard_map/ppermute | solution.py:17
  35.9 0.2 broadcast_select_fusion.4
  36.1 2.4 %collective-permute-start.4 = (bf16[12,2,64,128]{3,2,1,0:T(8,128)(2,1)S(1)}, bf16[12,2,64,128]{3,2,1,0:T(8,128)(2,1)S(1)}, u32[]{:S(2)}, u32[]{:S(2)}) collective-permute-start(bf16[12,2,64,128]{3,2,1,0:T(8,128)(2,1)S(1)} %get-tuple-element.20), channel_id=1, source_target_pairs={{0,2},{2,0},{4,6},{6,4},{8,10},{10,8},{12,14},{14,12},{16,18},{18,... | collective-permute-start | bytes 1179656 | tf_op jit(solution)/shard_map/ppermute | solution.py:17
  38.6 1.0 fusion.feat
  39.6 0.3 collective-permute-done.4
  39.9 0.3 broadcast_select_fusion.2
  40.4 6.2 %collective-permute-start.10 = (bf16[12,2,64,128]{3,2,1,0:T(8,128)(2,1)S(1)}, bf16[12,2,64,128]{3,2,1,0:T(8,128)(2,1)S(1)}, u32[]{:S(2)}, u32[]{:S(2)}) collective-permute-start(bf16[12,2,64,128]{3,2,1,0:T(8,128)(2,1)S(1)} %get-tuple-element.26.own), channel_id=1, source_target_pairs={{0,30},{30,0},{1,31},{31,1}} | collective-permute-start | bytes 1179656 | tf_op jit(solution)/shard_map/ppermute | solution.py:349
  47.0 1.6 %collective-permute-start.5 = (bf16[544,128]{1,0:T(8,128)(2,1)S(1)}, bf16[544,128]{1,0:T(8,128)(2,1)S(1)}, u32[]{:S(2)}, u32[]{:S(2)}) collective-permute-start(bf16[544,128]{1,0:T(8,128)(2,1)S(1)} %pad_maximum_fusion.10), channel_id=1, source_target_pairs={{0,1},{1,0},{2,3},{3,2},{4,5},{5,4},{6,7},{7,6},{8,9},{9,8},{10,11... | collective-permute-start | bytes 417800 | tf_op jit(solution)/shard_map/ppermute | solution.py:17
  48.8 0.8 copy.174
  49.7 2.4 %collective-permute-done.5 = bf16[544,128]{1,0:T(8,128)(2,1)S(1)} collective-permute-done((bf16[544,128]{1,0:T(8,128)(2,1)S(1)}, bf16[544,128]{1,0:T(8,128)(2,1)S(1)}, u32[]{:S(2)}, u32[]{:S(2)}) %collective-permute-start.5) | collective-permute-done | bytes 139296 | tf_op jit(solution)/shard_map/ppermute | solution.py:17
  52.8 0.9 copy.126
  53.7 0.5 collective-permute-done.6
  54.7 0.7 copy.128
  55.4 0.7 copy.127
  56.1 1.0 maximum_convert_fusion.near
  57.1 0.7 copy-done.14
  57.8 14.8 %shard_map.102 = (f32[12,2,32,128]{3,2,1,0:T(8,128)}, f32[1152,256]{1,0:T(8,128)}, f32[256,128]{1,0:T(8,128)}, f32[512,128]{1,0:T(8,128)}) custom-call(s32[144]{0:T(256)} %reshape.378.edge, s32[144]{0:T(256)} %reshape.379.corner, s32[2]{0:T(128)} %pad_add_fusion.where_ref, bf16[12,4,64,128]{3,2,1,0:T(8,128)(2,1)} %fusion.feat, ...), custom_call_target="tpu_custom_call" | custom-call | flops 4227858432 | bytes 12582912 | tf_op jit(solution)/shard_map/pallas_call | solution.py:222
  72.6 1.3 %select_bitcast_fusion = f32[8,72,256]{2,1,0:T(8,128)S(1)} fusion(f32[8,2,72,256]{3,2,1,0:T(8,128)} %bitcast.154, pred[]{:T(512)S(6)} %eq.67), kind=kLoop, calls=%fused_computation.19 | loop fusion | flops 147456 | bytes 1769473 | tf_op jit(solution)/shard_map/jit(_where)/select_n | solution.py:466
  74.2 0.7 copy-done.7
  75.3 1.6 %collective-permute-start.15 = (bf16[512,128]{1,0:T(8,128)(2,1)S(1)}, bf16[512,128]{1,0:T(8,128)(2,1)S(1)}, u32[]{:S(2)}, u32[]{:S(2)}) collective-permute-start(bf16[512,128]{1,0:T(8,128)(2,1)S(1)} %select_convert_fusion), channel_id=1, source_target_pairs={{0,1},{1,0},{2,3},{3,2},{4,5},{5,4},{6,7},{7,6},{8,9},{9,8},{10,11... | collective-permute-start | bytes 393224 | tf_op jit(solution)/shard_map/ppermute | solution.py:17
  77.0 3.6 %collective-permute-done.15 = bf16[512,128]{1,0:T(8,128)(2,1)S(1)} collective-permute-done((bf16[512,128]{1,0:T(8,128)(2,1)S(1)}, bf16[512,128]{1,0:T(8,128)(2,1)S(1)}, u32[]{:S(2)}, u32[]{:S(2)}) %collective-permute-start.15) | collective-permute-done | bytes 131104 | tf_op jit(solution)/shard_map/ppermute | solution.py:17
  80.6 0.2 convert_add_fusion
  81.0 1.3 %collective-permute-done.16 = f32[8,32,128]{2,1,0:T(8,128)S(1)} collective-permute-done((f32[8,32,128]{2,1,0:T(8,128)S(1)}, f32[8,32,128]{2,1,0:T(8,128)S(1)}, u32[]{:S(2)}, u32[]{:S(2)}) %collective-permute-start.16) | collective-permute-done | bytes 131104 | tf_op jit(solution)/shard_map/ppermute | solution.py:17
  82.4 0.8 pad_maximum_fusion.4
  83.2 5.2 %all-to-all-start.1 = ((bf16[8,176,128]{2,1,0:T(8,128)(2,1)}), bf16[8,176,128]{2,1,0:T(8,128)(2,1)S(1)}, u32[]{:S(2)}, u32[]{:S(2)}) async-start(bf16[8,176,128]{2,1,0:T(8,128)(2,1)} %pad_maximum_fusion.4), calls=%async_computation.1 | async-start | bytes 720896 | tf_op jit(solution)/shard_map/all_to_all | solution.py:474
  88.4 1.6 %collective-permute-start.13 = (f32[12,2,16,128]{3,2,1,0:T(8,128)S(1)}, f32[12,2,16,128]{3,2,1,0:T(8,128)S(1)}, u32[]{:S(2)}, u32[]{:S(2)}) collective-permute-start(f32[12,2,16,128]{3,2,1,0:T(8,128)S(1)} %slice_select_fusion.1), channel_id=1, source_target_pairs={{0,1},{1,0},{2,3},{3,2},{4,5},{5,4},{6,7},{7,6},{8,9},{9,8},{10,11... | collective-permute-start | bytes 589832 | tf_op jit(solution)/shard_map/ppermute | solution.py:17
  90.1 5.1 %collective-permute-done.13 = f32[12,2,16,128]{3,2,1,0:T(8,128)S(1)} collective-permute-done((f32[12,2,16,128]{3,2,1,0:T(8,128)S(1)}, f32[12,2,16,128]{3,2,1,0:T(8,128)S(1)}, u32[]{:S(2)}, u32[]{:S(2)}) %collective-permute-start.13) | collective-permute-done | bytes 196640 | tf_op jit(solution)/shard_map/ppermute | solution.py:17
  95.2 0.7 add_convert_fusion
  95.9 3.8 %all-to-all-done.1 = bf16[8,176,128]{2,1,0:T(8,128)(2,1)S(1)} async-done(((bf16[8,176,128]{2,1,0:T(8,128)(2,1)}), bf16[8,176,128]{2,1,0:T(8,128)(2,1)S(1)}, u32[]{:S(2)}, u32[]{:S(2)}) %all-to-all-start.1) | async-done | bytes 360480 | tf_op jit(solution)/shard_map/all_to_all | solution.py:474
  99.8 0.7 fusion.24
  100.4 0.6 pad_maximum_fusion.17
  (158 shorter events, 4.7 us)
Async XLA Ops:
  0.6 7.4 %copy-start.1 = (bf16[12,4,32,128]{3,2,1,0:T(8,128)(2,1)S(1)}, bf16[12,4,32,128]{3,2,1,0:T(8,128)(2,1)}, u32[]{:S(2)}) copy-start(bf16[12,4,32,128]{3,2,1,0:T(8,128)(2,1)} %param.7) | copy-start | bytes 1179652
  0.6 7.3 %copy-start.8 = (bf16[12,2,16,128]{3,2,1,0:T(8,128)(2,1)S(1)}, bf16[12,2,16,128]{3,2,1,0:T(8,128)(2,1)}, u32[]{:S(2)}) copy-start(bf16[12,2,16,128]{3,2,1,0:T(8,128)(2,1)} %param.8) | copy-start | bytes 294916
  1.7 6.4 %copy-start.10 = (s32[12,4,3]{0,1,2:T(4,128)S(1)}, s32[12,4,3]{0,1,2:T(4,128)}, u32[]{:S(2)}) copy-start(s32[12,4,3]{0,1,2:T(4,128)} %param.12) | copy-start | bytes 1732
  1.7 6.4 %copy-start.9 = (bf16[72,256]{1,0:T(8,128)(2,1)S(1)}, bf16[72,256]{1,0:T(8,128)(2,1)}, u32[]{:S(2)}) copy-start(bf16[72,256]{1,0:T(8,128)(2,1)} %param.9) | copy-start | bytes 110596
  2.9 5.3 %copy-start.11 = (bf16[32,64]{1,0:T(8,128)(2,1)S(1)}, bf16[32,64]{1,0:T(8,128)(2,1)}, u32[]{:S(2)}) copy-start(bf16[32,64]{1,0:T(8,128)(2,1)} %param.11) | copy-start | bytes 12292
  2.9 5.3 %copy-start.12 = (bf16[32,64]{1,0:T(8,128)(2,1)S(1)}, bf16[32,64]{1,0:T(8,128)(2,1)}, u32[]{:S(2)}) copy-start(bf16[32,64]{1,0:T(8,128)(2,1)} %param.10) | copy-start | bytes 12292
  4.2 5.0 %collective-permute-start = (bf16[144,128]{1,0:T(8,128)(2,1)S(1)}, bf16[144,128]{1,0:T(8,128)(2,1)S(1)}, u32[]{:S(2)}, u32[]{:S(2)}) collective-permute-start(bf16[144,128]{1,0:T(8,128)(2,1)S(1)} %pad_maximum_fusion.23), channel_id=1, source_target_pairs={{0,1},{1,0},{2,3},{3,2},{4,5},{5,4},{6,7},{7,6},{8,9},{9,8},{10,11... | collective-permute-start | bytes 110600 | tf_op jit(solution)/shard_map/ppermute | solution.py:17
  7.2 14.5 %collective-permute-start.2 = (bf16[12,2,32,128]{3,2,1,0:T(8,128)(2,1)S(1)}, bf16[12,2,32,128]{3,2,1,0:T(8,128)(2,1)S(1)}, u32[]{:S(2)}, u32[]{:S(2)}) collective-permute-start(bf16[12,2,32,128]{3,2,1,0:T(8,128)(2,1)S(1)} %get-tuple-element.43), channel_id=1, source_target_pairs={{2,4},{6,8},{10,12},{14,16},{18,20},{22,24},{26,28},{4,2},{8,6},{1... | collective-permute-start | bytes 589832 | tf_op jit(solution)/shard_map/ppermute | solution.py:340
  7.9 17.7 %collective-permute-start.11 = (bf16[12,2,16,128]{3,2,1,0:T(8,128)(2,1)S(1)}, bf16[12,2,16,128]{3,2,1,0:T(8,128)(2,1)S(1)}, u32[]{:S(2)}, u32[]{:S(2)}) collective-permute-start(bf16[12,2,16,128]{3,2,1,0:T(8,128)(2,1)S(1)} %copy-done.8), channel_id=1, source_target_pairs={{0,1},{1,0},{2,3},{3,2},{4,5},{5,4},{6,7},{7,6},{8,9},{9,8},{10,11... | collective-permute-start | bytes 294920 | tf_op jit(solution)/shard_map/ppermute | solution.py:17
  9.3 6.2 %collective-permute-start.1 = (bf16[2,12,2,4,128]{4,3,2,1,0:T(4,128)(2,1)S(1)}, bf16[2,12,2,4,128]{4,3,2,1,0:T(4,128)(2,1)S(1)}, u32[]{:S(2)}, u32[]{:S(2)}) collective-permute-start(bf16[2,12,2,4,128]{4,3,2,1,0:T(4,128)(2,1)S(1)} %pad_maximum_fusion.22), channel_id=1, source_target_pairs={{0,2},{2,0},{4,6},{6,4},{8,10},{10,8},{12,14},{14,12},{16,18},{18,... | collective-permute-start | bytes 147464 | tf_op jit(solution)/shard_map/ppermute | solution.py:17
  11.5 9.3 %collective-permute-start.7 = (bf16[2,12,2,4,128]{4,3,2,1,0:T(4,128)(2,1)S(1)}, bf16[2,12,2,4,128]{4,3,2,1,0:T(4,128)(2,1)S(1)}, u32[]{:S(2)}, u32[]{:S(2)}) collective-permute-start(bf16[2,12,2,4,128]{4,3,2,1,0:T(4,128)(2,1)S(1)} %pad_maximum_fusion.22), channel_id=1, source_target_pairs={{0,30},{2,28},{4,26},{6,24},{8,22},{10,20},{12,18},{14,16},{16,14}... | collective-permute-start | bytes 147464 | tf_op jit(solution)/shard_map/ppermute | solution.py:351
  17.2 7.6 %copy-start.13 = (s32[12,4,3]{0,1,2:T(4,128)S(1)}, s32[12,4,3]{0,1,2:T(4,128)}, u32[]{:S(2)}) copy-start(s32[12,4,3]{0,1,2:T(4,128)} %param.13) | copy-start | bytes 1732
  17.2 29.7 %all-to-all-start = ((bf16[8,464,128]{2,1,0:T(8,128)(2,1)}), bf16[8,464,128]{2,1,0:T(8,128)(2,1)S(1)}, u32[]{:S(2)}, u32[]{:S(2)}) async-start(bf16[8,464,128]{2,1,0:T(8,128)(2,1)} %pad_maximum_fusion), calls=%async_computation | async-start | bytes 1900544 | tf_op jit(solution)/shard_map/all_to_all | solution.py:336
  20.9 5.4 %collective-permute-start.8 = (bf16[2,12,2,2,128]{4,3,2,1,0:T(2,128)(2,1)S(1)}, bf16[2,12,2,2,128]{4,3,2,1,0:T(2,128)(2,1)S(1)}, u32[]{:S(2)}, u32[]{:S(2)}) collective-permute-start(bf16[2,12,2,2,128]{4,3,2,1,0:T(2,128)(2,1)S(1)} %get-tuple-element.101), channel_id=1, source_target_pairs={{0,2},{2,0},{4,6},{6,4},{8,10},{10,8},{12,14},{14,12},{16,18},{18,... | collective-permute-start | bytes 73736 | tf_op jit(solution)/shard_map/ppermute | solution.py:17
  21.1 5.3 %collective-permute-start.9 = (bf16[2,12,2,2,128]{4,3,2,1,0:T(2,128)(2,1)S(1)}, bf16[2,12,2,2,128]{4,3,2,1,0:T(2,128)(2,1)S(1)}, u32[]{:S(2)}, u32[]{:S(2)}) collective-permute-start(bf16[2,12,2,2,128]{4,3,2,1,0:T(2,128)(2,1)S(1)} %get-tuple-element.102), channel_id=1, source_target_pairs={{2,4},{6,8},{10,12},{14,16},{18,20},{22,24},{26,28},{4,2},{8,6},{1... | collective-permute-start | bytes 73736 | tf_op jit(solution)/shard_map/ppermute | solution.py:355
  21.8 14.0 %collective-permute-start.3 = (bf16[12,6,32,128]{3,2,1,0:T(8,128)(2,1)S(1)}, bf16[12,6,32,128]{3,2,1,0:T(8,128)(2,1)S(1)}, u32[]{:S(2)}, u32[]{:S(2)}) collective-permute-start(bf16[12,6,32,128]{3,2,1,0:T(8,128)(2,1)S(1)} %constant_dynamic-update-slice_fusion.8), channel_id=1, source_target_pairs={{0,1},{1,0},{2,3},{3,2},{4,5},{5,4},{6,7},{7,6},{8,9},{9,8},{10,11... | collective-permute-start | bytes 1769480 | tf_op jit(solution)/shard_map/ppermute | solution.py:17
  36.1 3.8 %collective-permute-start.4 = (bf16[12,2,64,128]{3,2,1,0:T(8,128)(2,1)S(1)}, bf16[12,2,64,128]{3,2,1,0:T(8,128)(2,1)S(1)}, u32[]{:S(2)}, u32[]{:S(2)}) collective-permute-start(bf16[12,2,64,128]{3,2,1,0:T(8,128)(2,1)S(1)} %get-tuple-element.20), channel_id=1, source_target_pairs={{0,2},{2,0},{4,6},{6,4},{8,10},{10,8},{12,14},{14,12},{16,18},{18,... | collective-permute-start | bytes 1179656 | tf_op jit(solution)/shard_map/ppermute | solution.py:17
  40.2 8.6 %copy-start.4 = (bf16[12,2,64,128]{3,2,1,0:T(8,128)(2,1)}, bf16[12,2,64,128]{3,2,1,0:T(8,128)(2,1)S(1)}, u32[]{:S(2)}) copy-start(bf16[12,2,64,128]{3,2,1,0:T(8,128)(2,1)S(1)} %get-tuple-element.22.down_rows) | copy-start | bytes 1179652
  40.2 8.6 %copy-start.5 = (bf16[12,2,64,128]{3,2,1,0:T(8,128)(2,1)}, bf16[12,2,64,128]{3,2,1,0:T(8,128)(2,1)S(1)}, u32[]{:S(2)}) copy-start(bf16[12,2,64,128]{3,2,1,0:T(8,128)(2,1)S(1)} %get-tuple-element.23.up) | copy-start | bytes 1179652
  40.2 8.6 %copy-start.6 = (bf16[12,2,64,128]{3,2,1,0:T(8,128)(2,1)}, bf16[12,2,64,128]{3,2,1,0:T(8,128)(2,1)S(1)}, u32[]{:S(2)}) copy-start(bf16[12,2,64,128]{3,2,1,0:T(8,128)(2,1)S(1)} %get-tuple-element.26.own) | copy-start | bytes 1179652
  40.4 16.6 %collective-permute-start.10 = (bf16[12,2,64,128]{3,2,1,0:T(8,128)(2,1)S(1)}, bf16[12,2,64,128]{3,2,1,0:T(8,128)(2,1)S(1)}, u32[]{:S(2)}, u32[]{:S(2)}) collective-permute-start(bf16[12,2,64,128]{3,2,1,0:T(8,128)(2,1)S(1)} %get-tuple-element.26.own), channel_id=1, source_target_pairs={{0,30},{30,0},{1,31},{31,1}} | collective-permute-start | bytes 1179656 | tf_op jit(solution)/shard_map/ppermute | solution.py:349
  47.0 5.1 %collective-permute-start.5 = (bf16[544,128]{1,0:T(8,128)(2,1)S(1)}, bf16[544,128]{1,0:T(8,128)(2,1)S(1)}, u32[]{:S(2)}, u32[]{:S(2)}) collective-permute-start(bf16[544,128]{1,0:T(8,128)(2,1)S(1)} %pad_maximum_fusion.10), channel_id=1, source_target_pairs={{0,1},{1,0},{2,3},{3,2},{4,5},{5,4},{6,7},{7,6},{8,9},{9,8},{10,11... | collective-permute-start | bytes 417800 | tf_op jit(solution)/shard_map/ppermute | solution.py:17
  48.6 4.0 %collective-permute-start.12 = (bf16[8,144,128]{2,1,0:T(8,128)(2,1)S(1)}, bf16[8,144,128]{2,1,0:T(8,128)(2,1)S(1)}, u32[]{:S(2)}, u32[]{:S(2)}) collective-permute-start(bf16[8,144,128]{2,1,0:T(8,128)(2,1)S(1)} %slice.390), channel_id=1, source_target_pairs={{0,2},{2,0},{4,6},{6,4},{8,10},{10,8},{12,14},{14,12},{16,18},{18,... | collective-permute-start | bytes 884744 | tf_op jit(solution)/shard_map/ppermute | solution.py:17
  52.5 1.6 %collective-permute-start.6 = (bf16[1088,128]{1,0:T(8,128)(2,1)S(1)}, bf16[1088,128]{1,0:T(8,128)(2,1)S(1)}, u32[]{:S(2)}, u32[]{:S(2)}) collective-permute-start(bf16[1088,128]{1,0:T(8,128)(2,1)S(1)} %pad_maximum_fusion.6), channel_id=1, source_target_pairs={{0,2},{2,0},{4,6},{6,4},{8,10},{10,8},{12,14},{14,12},{16,18},{18,... | collective-permute-start | bytes 835592 | tf_op jit(solution)/shard_map/ppermute | solution.py:17
  57.1 0.7 copy-start.14
  74.0 0.9 copy-start.7
  74.0 1.0 %copy-start.3 = (f32[512,128]{1,0:T(8,128)S(1)}, f32[512,128]{1,0:T(8,128)}, u32[]{:S(2)}) copy-start(f32[512,128]{1,0:T(8,128)} %get-tuple-element.19) | copy-start | bytes 786436
  74.1 8.2 %collective-permute-start.14 = (f32[8,144,128]{2,1,0:T(8,128)S(1)}, f32[8,144,128]{2,1,0:T(8,128)S(1)}, u32[]{:S(2)}, u32[]{:S(2)}) collective-permute-start(f32[8,144,128]{2,1,0:T(8,128)S(1)} %pad_maximum_fusion.2), channel_id=1, source_target_pairs={{0,2},{2,0},{4,6},{6,4},{8,10},{10,8},{12,14},{14,12},{16,18},{18,... | collective-permute-start | bytes 1769480 | tf_op jit(solution)/shard_map/ppermute | solution.py:17
  75.0 1.9 %copy-start = (f32[1152,256]{1,0:T(8,128)S(1)}, f32[1152,256]{1,0:T(8,128)}, u32[]{:S(2)}) copy-start(f32[1152,256]{1,0:T(8,128)} %get-tuple-element.17) | copy-start | bytes 3538948
  75.3 5.3 %collective-permute-start.15 = (bf16[512,128]{1,0:T(8,128)(2,1)S(1)}, bf16[512,128]{1,0:T(8,128)(2,1)S(1)}, u32[]{:S(2)}, u32[]{:S(2)}) collective-permute-start(bf16[512,128]{1,0:T(8,128)(2,1)S(1)} %select_convert_fusion), channel_id=1, source_target_pairs={{0,1},{1,0},{2,3},{3,2},{4,5},{5,4},{6,7},{7,6},{8,9},{9,8},{10,11... | collective-permute-start | bytes 393224 | tf_op jit(solution)/shard_map/ppermute | solution.py:17
  80.9 1.4 %collective-permute-start.16 = (f32[8,32,128]{2,1,0:T(8,128)S(1)}, f32[8,32,128]{2,1,0:T(8,128)S(1)}, u32[]{:S(2)}, u32[]{:S(2)}) collective-permute-start(f32[8,32,128]{2,1,0:T(8,128)S(1)} %select_bitcast_fusion.3), channel_id=1, source_target_pairs={{0,2},{2,0},{4,6},{6,4},{8,10},{10,8},{12,14},{14,12},{16,18},{18,... | collective-permute-start | bytes 393224 | tf_op jit(solution)/shard_map/ppermute | solution.py:17
  82.3 6.1 %copy-start.2 = (f32[12,2,32,128]{3,2,1,0:T(8,128)S(1)}, f32[12,2,32,128]{3,2,1,0:T(8,128)}, u32[]{:S(2)}) copy-start(f32[12,2,32,128]{3,2,1,0:T(8,128)} %get-tuple-element.16) | copy-start | bytes 1179652
  83.2 16.5 %all-to-all-start.1 = ((bf16[8,176,128]{2,1,0:T(8,128)(2,1)}), bf16[8,176,128]{2,1,0:T(8,128)(2,1)S(1)}, u32[]{:S(2)}, u32[]{:S(2)}) async-start(bf16[8,176,128]{2,1,0:T(8,128)(2,1)} %pad_maximum_fusion.4), calls=%async_computation.1 | async-start | bytes 720896 | tf_op jit(solution)/shard_map/all_to_all | solution.py:474
  88.4 6.7 %collective-permute-start.13 = (f32[12,2,16,128]{3,2,1,0:T(8,128)S(1)}, f32[12,2,16,128]{3,2,1,0:T(8,128)S(1)}, u32[]{:S(2)}, u32[]{:S(2)}) collective-permute-start(f32[12,2,16,128]{3,2,1,0:T(8,128)S(1)} %slice_select_fusion.1), channel_id=1, source_target_pairs={{0,1},{1,0},{2,3},{3,2},{4,5},{5,4},{6,7},{7,6},{8,9},{9,8},{10,11... | collective-permute-start | bytes 589832 | tf_op jit(solution)/shard_map/ppermute | solution.py:17
